TPU v7x, 32 devices: a whole 2x2x4 slice. The times are simulated.
32 devices in a mesh: dp: 8 (over z, x), tok: 4 (over y, core).
Axes of the slice: x: 2, y: 2, z: 4, core: 2. Of those that a mesh axis runs over, the one named last changes fastest.
Arguments:
- inputs: bfloat16 [32, 1024, 768], P('dp', 'tok'), may hold values from -6 to 6
- history: bfloat16 [24, 32, 1024, 768], P(None, 'dp', 'tok'), may hold values from -6 to 6
- document_lengths: int32 [32, 8], P('dp'), may hold values from 1 to 512, 1024 in all within a row
- cotangent: bfloat16 [32, 1024, 768], P('dp', 'tok')
- attention_params: float32 [2363904], P(('dp', 'tok'))
- attention_first: float32 [2363904], P(('dp', 'tok')), may hold values from -0.078125 to 0.078125
- attention_second: float32 [2363904], P(('dp', 'tok')), may hold values from 3.0517579e-06 to 0.00030517578
- feedforward_params: float32 [4723968], P(('dp', 'tok'))
- feedforward_first: float32 [4723968], P(('dp', 'tok')), may hold values from -0.078125 to 0.078125
- feedforward_second: float32 [4723968], P(('dp', 'tok')), may hold values from 3.0517579e-06 to 0.00030517578
- mixing_offsets: float32 [25], replicated, may hold values from -0.5 to 0.5
- mixing_first: float32 [25], replicated, may hold values from -2.5 to 2.5
- mixing_second: float32 [25], replicated, may hold values from 0.0030517578 to 0.30517578
- step_count: int32 [1], replicated, may hold values from 1 to 5
Outputs:
- mixed: bfloat16 [32, 1024, 768], P('dp', 'tok')
- grad_inputs: float32 [32, 1024, 768], P('dp', 'tok')
- grad_history: float32 [24, 32, 1024, 768], P(None, 'dp', 'tok')
- attention_new: float32 [2363904], P(('dp', 'tok'))
- attention_first_new: float32 [2363904], P(('dp', 'tok'))
- attention_second_new: float32 [2363904], P(('dp', 'tok'))
- feedforward_new: float32 [4723968], P(('dp', 'tok'))
- feedforward_first_new: float32 [4723968], P(('dp', 'tok'))
- feedforward_second_new: float32 [4723968], P(('dp', 'tok'))
- mixing_new: float32 [25], replicated
- mixing_first_new: float32 [25], replicated
- mixing_second_new: float32 [25], replicated
Inputs may be any that keep to these rules, and one draw needn't show every extreme that they name: `document_lengths`: in each row the first 7 entries are document lengths in order and the last is the padding at the row's end; a row's entries sum to 1024, and its largest is exactly 512.
All inputs are finite; a program needn't handle non-finite values.
Results may differ from a plain program's by a relative error of at most 0.008.
The roundings to bfloat16 on the way count: a program that leaves them out, or rounds other values in their place, can miss the bound.
Values may be sent and summed in bfloat16 or wider, within the bound.
A program may use at most 384 MiB of HBM per device.

v0:
```python
from functools import partial
import math

import jax
import jax.numpy as jnp
from jax import lax
from jax.sharding import PartitionSpec as P

D = 768
HEADS = 12
HEAD_DIM = 64
FF = 3072
DOCS = 7


beta_first = 0.9
beta_second = 0.95
learning_rate = 0.05
decay_rate = 0.1
adam_epsilon = 1e-08
norm_epsilon = 1e-05
masked_score = -1e30


def layer_norm(values, gain, shift):
    centered = values - jnp.mean(values, axis=-1, keepdims=True)
    variance = jnp.mean(centered * centered, axis=-1, keepdims=True)
    return centered * lax.rsqrt(variance + norm_epsilon) * gain + shift


def rotate(values, position):
    half_dim = values.shape[-1] // 2
    frequency = jnp.exp(
        jnp.arange(half_dim, dtype=jnp.float32) * (-2.0 * math.log(10000.0) / values.shape[-1])
    )
    angle = position.astype(jnp.float32)[..., None] * frequency
    cosine = jnp.cos(angle)[..., None, :]
    sine = jnp.sin(angle)[..., None, :]
    first_half = values[..., :half_dim]
    second_half = values[..., half_dim:]
    return jnp.concatenate(
        [first_half * cosine - second_half * sine, second_half * cosine + first_half * sine],
        axis=-1,
    )


def turn_back(gradient_part, position):
    return jax.vjp(partial(rotate, position=position), gradient_part)[1](gradient_part)[0]


def layout(lengths_rows, places):
    ends = jnp.cumsum(lengths_rows, axis=1)
    starts = ends - lengths_rows
    doc_count = lengths_rows.shape[1] - 1
    inside = places[None, :, None] >= ends[:, None, :doc_count]
    segment = jnp.sum(inside.astype(jnp.int32), axis=2)
    labels = jnp.arange(doc_count + 1, dtype=jnp.int32)
    chosen = segment[:, :, None] == labels[None, None, :]
    begin = jnp.sum(jnp.where(chosen, starts[:, None, :], 0), axis=2)
    return (segment, places[None, :] - begin)


def allowed_mask(segment_row, first_row, query_count):
    query_place = first_row + jnp.arange(query_count, dtype=jnp.int32)
    key_place = jnp.arange(segment_row.shape[0], dtype=jnp.int32)
    query_segment = lax.dynamic_slice_in_dim(segment_row, first_row, query_count, 0)
    earlier = key_place[None, :] <= query_place[:, None]
    same_doc = segment_row[None, :] == query_segment[:, None]
    real_key = (segment_row[None, :] < DOCS) | (key_place[None, :] == query_place[:, None])
    return earlier & same_doc & real_key


def block_scores(queries, keys_all, segment_row, first_row):
    scores = jnp.einsum(
        "qhd,khd->hqk", queries, keys_all, preferred_element_type=jnp.float32
    ) * HEAD_DIM ** (-0.5)
    allowed = allowed_mask(segment_row, first_row, queries.shape[0])
    return jnp.where(allowed[None], scores, masked_score)


def attention_shapes():
    return [(D,), (D,), (D, 3 * D), (3 * D,), (D, D), (D,)]


def feedforward_shapes():
    return [(D,), (D,), (D, FF), (FF,), (FF, D), (D,)]


def unpack(flat_vector, shape_list):
    pieces = []
    offset_at = 0
    for piece_shape in shape_list:
        piece_size = math.prod(piece_shape)
        pieces.append(flat_vector[offset_at : offset_at + piece_size].reshape(piece_shape))
        offset_at = offset_at + piece_size
    return pieces


def decay_mask(places, shape_list):
    mask_values = jnp.zeros(places.shape, jnp.float32)
    offset_at = 0
    for piece_shape in shape_list:
        piece_size = math.prod(piece_shape)
        if len(piece_shape) == 2:
            inside = (places >= offset_at) & (places < offset_at + piece_size)
            mask_values = mask_values + inside.astype(jnp.float32)
        offset_at = offset_at + piece_size
    return mask_values * decay_rate


def adam_update(values, gradient, moment_one, moment_two, step_number, decay_values):
    first_new = beta_first * moment_one + (1.0 - beta_first) * gradient
    second_new = beta_second * moment_two + (1.0 - beta_second) * gradient * gradient
    power_now = step_number.astype(jnp.float32)
    fix_one = 1.0 - jnp.power(beta_first, power_now)
    fix_two = 1.0 - jnp.power(beta_second, power_now)
    step_size = first_new / fix_one / (jnp.sqrt(second_new / fix_two) + adam_epsilon)
    return (values - learning_rate * (step_size + decay_values * values), first_new, second_new)


def to_groups(values, subsets):
    full_shape = values.shape
    row_total = full_shape[0]
    half_width = full_shape[-1] // 2
    split_view = values.reshape(
        (subsets, row_total // subsets) + full_shape[1:-1] + (2, half_width)
    )
    moved = jnp.moveaxis(split_view, -2, 0)
    return moved.reshape((2 * subsets, row_total // subsets) + full_shape[1:-1] + (half_width,))


def from_groups(values, subsets):
    full_shape = values.shape
    split_view = values.reshape((2, subsets) + full_shape[1:])
    moved = jnp.moveaxis(split_view, 0, -2)
    return moved.reshape((subsets * full_shape[1],) + full_shape[2:-1] + (2 * full_shape[-1],))


def attend_rows(head_qkv, head_segment):
    item_count = head_qkv.shape[1]
    length_all = head_qkv.shape[2]
    group_width = head_qkv.shape[4]
    head_count = group_width // HEAD_DIM
    block_rows = min(512, length_all)
    block_count = length_all // block_rows
    rows_qkv = head_qkv.reshape(item_count, length_all, 3, head_count, HEAD_DIM)
    rows_segment = head_segment.reshape(item_count, length_all)

    def attend_one_block(block_index):
        row_index = block_index // block_count
        first_row = block_index % block_count * block_rows
        current = rows_qkv[row_index]
        queries = lax.dynamic_slice_in_dim(current[:, 0], first_row, block_rows, 0)
        masked = block_scores(queries, current[:, 1], rows_segment[row_index], first_row)
        top_score = jnp.max(masked, axis=2, keepdims=True)
        exponent = jnp.exp(masked - top_score)
        total_weight = jnp.sum(exponent, axis=2, keepdims=True)
        soft_weights = (exponent / total_weight).astype(jnp.bfloat16)
        attended = jnp.einsum(
            "hqk,khd->qhd", soft_weights, current[:, 2], preferred_element_type=jnp.float32
        )
        log_total = (top_score + jnp.log(total_weight))[:, :, 0]
        return (attended.reshape(block_rows, group_width).astype(jnp.bfloat16), log_total)

    outputs, log_totals = lax.map(
        attend_one_block, jnp.arange(item_count * block_count, dtype=jnp.int32)
    )
    return (
        outputs.reshape(1, item_count, length_all, group_width),
        log_totals.reshape(1, item_count, block_count, head_count, block_rows),
    )


def attend_back(head_qkv, head_segment, log_totals, head_grads):
    item_count = head_qkv.shape[1]
    length_all = head_qkv.shape[2]
    group_width = head_qkv.shape[4]
    head_count = group_width // HEAD_DIM
    block_rows = min(512, length_all)
    block_count = length_all // block_rows
    scale_value = HEAD_DIM ** (-0.5)

    def one_row(pieces):
        current, segment_row, log_row, grad_row = pieces
        keys_all = current[:, 1]
        values_all = current[:, 2]

        def one_one_block(carried, block_index):
            first_row = block_index * block_rows
            queries = lax.dynamic_slice_in_dim(current[:, 0], first_row, block_rows, 0)
            grad_block = lax.dynamic_slice_in_dim(grad_row, first_row, block_rows, 0)
            masked = block_scores(queries, keys_all, segment_row, first_row)
            soft_weights = jnp.exp(masked - log_row[block_index][:, :, None])
            grad_weights = jnp.einsum(
                "qhd,khd->hqk", grad_block, values_all, preferred_element_type=jnp.float32
            )
            inner_sum = jnp.sum(soft_weights * grad_weights, axis=2, keepdims=True)
            grad_scores = (soft_weights * (grad_weights - inner_sum)).astype(jnp.bfloat16)
            grad_query = (
                jnp.einsum(
                    "hqk,khd->qhd", grad_scores, keys_all, preferred_element_type=jnp.float32
                )
                * scale_value
            )
            grad_key = (
                carried[0]
                + jnp.einsum(
                    "hqk,qhd->khd", grad_scores, queries, preferred_element_type=jnp.float32
                )
                * scale_value
            )
            grad_value = carried[1] + jnp.einsum(
                "hqk,qhd->khd",
                soft_weights.astype(jnp.bfloat16),
                grad_block,
                preferred_element_type=jnp.float32,
            )
            return ((grad_key, grad_value), grad_query)

        empty_grad = jnp.zeros((length_all, head_count, HEAD_DIM), jnp.float32)
        (grad_key, grad_value), grad_query = lax.scan(
            one_one_block, (empty_grad, empty_grad), jnp.arange(block_count, dtype=jnp.int32)
        )
        grad_query = grad_query.reshape(length_all, head_count, HEAD_DIM)
        return jnp.stack([grad_query, grad_key, grad_value], axis=1).astype(jnp.bfloat16)

    row_grads = lax.map(
        one_row,
        (
            head_qkv.reshape(item_count, length_all, 3, head_count, HEAD_DIM),
            head_segment.reshape(item_count, length_all),
            log_totals.reshape(item_count, block_count, head_count, block_rows),
            head_grads.reshape(item_count, length_all, head_count, HEAD_DIM),
        ),
    )
    return row_grads.reshape(1, item_count, length_all, 3, group_width)


def shards(
    inputs,
    history,
    document_lengths,
    cotangent,
    attention_params,
    attention_first,
    attention_second,
    feedforward_params,
    feedforward_first,
    feedforward_second,
    mixing_offsets,
    mixing_first,
    mixing_second,
    step_count,
):
    row_count, token_span, model_width = inputs.shape
    subsets = lax.axis_size("tok") // 2
    per_device = row_count // subsets
    tokens_all = row_count * token_span * lax.axis_size("dp") * lax.axis_size("tok")
    attention_flat, feedforward_flat = (
        lax.all_gather(attention_params.astype(jnp.bfloat16), ("dp", "tok"), axis=0, tiled=True),
        lax.all_gather(feedforward_params.astype(jnp.bfloat16), ("dp", "tok"), axis=0, tiled=True),
    )
    gain_one, shift_one, w_qkv, b_qkv, w_out, b_out = unpack(attention_flat, attention_shapes())
    gain_two, shift_two, w_up, b_up, w_down, b_down = unpack(feedforward_flat, feedforward_shapes())
    gain_one = gain_one.astype(jnp.float32)
    shift_one = shift_one.astype(jnp.float32)
    gain_two = gain_two.astype(jnp.float32)
    shift_two = shift_two.astype(jnp.float32)
    places = lax.axis_index("tok") * token_span + jnp.arange(token_span, dtype=jnp.int32)
    segment, position = layout(document_lengths, places)
    current = inputs.astype(jnp.float32)
    normed_one = layer_norm(current, gain_one, shift_one).astype(jnp.bfloat16)
    project = jnp.dot(normed_one, w_qkv, preferred_element_type=jnp.float32) + b_qkv.astype(
        jnp.float32
    )
    project = project.reshape(row_count, token_span, 3, HEADS, HEAD_DIM)
    queries = rotate(project[:, :, 0], position)
    keys_all = rotate(project[:, :, 1], position)
    packed = jnp.stack([queries, keys_all, project[:, :, 2]], axis=2).astype(jnp.bfloat16)
    send_qkv = to_groups(packed.reshape(row_count, token_span, 3, model_width), subsets)
    send_segment = jnp.broadcast_to(
        segment.reshape(1, subsets, per_device, token_span), (2, subsets, per_device, token_span)
    ).reshape(2 * subsets, per_device, token_span)
    head_qkv = lax.all_to_all(send_qkv, "tok", split_axis=0, concat_axis=2, tiled=True)
    head_segment = lax.all_to_all(send_segment, "tok", split_axis=0, concat_axis=2, tiled=True)
    outputs, log_totals = attend_rows(head_qkv, head_segment)
    returned = lax.all_to_all(outputs, "tok", split_axis=2, concat_axis=0, tiled=True)
    returned, head_qkv, head_segment, log_totals = (returned, head_qkv, head_segment, log_totals)
    attended = from_groups(returned, subsets)
    hidden = (
        current
        + jnp.dot(attended, w_out, preferred_element_type=jnp.float32)
        + b_out.astype(jnp.float32)
    )
    normed_two = layer_norm(hidden, gain_two, shift_two).astype(jnp.bfloat16)
    up_value = jnp.dot(normed_two, w_up, preferred_element_type=jnp.float32) + b_up.astype(
        jnp.float32
    )
    active = jax.nn.gelu(up_value).astype(jnp.bfloat16)
    block_out = (
        hidden
        + jnp.dot(active, w_down, preferred_element_type=jnp.float32)
        + b_down.astype(jnp.float32)
    )
    term_count = mixing_offsets.shape[0]
    coefficient = mixing_offsets + (jnp.arange(term_count) == term_count - 1).astype(jnp.float32)
    history_part = jnp.einsum(
        "j,jrtd->rtd", coefficient[:-1], history, preferred_element_type=jnp.float32
    )
    mixed = (history_part + coefficient[-1] * block_out).astype(jnp.bfloat16)
    grad_mixed = cotangent.astype(jnp.float32)
    grad_history = coefficient[:-1, None, None, None] * grad_mixed[None]
    history_terms = jnp.einsum(
        "jrtd,rtd->j", history, grad_mixed, preferred_element_type=jnp.float32
    )
    mixing_terms = jnp.concatenate([history_terms, jnp.sum(block_out * grad_mixed)[None]])
    mixing_grad = lax.psum(mixing_terms, ("dp", "tok")) / tokens_all
    grad_block = coefficient[-1] * grad_mixed
    grad_branch = grad_block.astype(jnp.bfloat16)
    grad_w_down = jnp.einsum("rtf,rtd->fd", active, grad_branch, preferred_element_type=jnp.float32)
    grad_b_down = jnp.sum(grad_branch.astype(jnp.float32), axis=(0, 1))
    grad_active = jnp.einsum("rtd,fd->rtf", grad_branch, w_down, preferred_element_type=jnp.float32)
    grad_up = jax.vjp(jax.nn.gelu, up_value)[1](grad_active)[0].astype(jnp.bfloat16)
    grad_w_up = jnp.einsum("rtd,rtf->df", normed_two, grad_up, preferred_element_type=jnp.float32)
    grad_b_up = jnp.sum(grad_up.astype(jnp.float32), axis=(0, 1))
    grad_normed_two = jnp.einsum("rtf,df->rtd", grad_up, w_up, preferred_element_type=jnp.float32)
    grad_hidden_norm, grad_gain_two, grad_shift_two = jax.vjp(
        layer_norm, hidden, gain_two, shift_two
    )[1](grad_normed_two)
    grad_hidden = grad_block + grad_hidden_norm
    feedforward_grad = jnp.concatenate(
        [
            grad_gain_two,
            grad_shift_two,
            grad_w_up.reshape(-1),
            grad_b_up,
            grad_w_down.reshape(-1),
            grad_b_down,
        ]
    )
    feedforward_share = lax.psum_scatter(
        feedforward_grad, ("dp", "tok"), scatter_dimension=0, tiled=True
    )
    grad_attn = grad_hidden.astype(jnp.bfloat16)
    grad_w_out = jnp.einsum("rtd,rte->de", attended, grad_attn, preferred_element_type=jnp.float32)
    grad_b_out = jnp.sum(grad_attn.astype(jnp.float32), axis=(0, 1))
    grad_attended = jnp.einsum(
        "rte,de->rtd", grad_attn, w_out, preferred_element_type=jnp.float32
    ).astype(jnp.bfloat16)
    head_grads = lax.all_to_all(
        to_groups(grad_attended, subsets), "tok", split_axis=0, concat_axis=2, tiled=True
    )
    head_back = attend_back(head_qkv, head_segment, log_totals, head_grads)
    token_back = from_groups(
        lax.all_to_all(head_back, "tok", split_axis=2, concat_axis=0, tiled=True), subsets
    )
    token_back = token_back.astype(jnp.float32).reshape(row_count, token_span, 3, HEADS, HEAD_DIM)
    grad_project = jnp.stack(
        [
            turn_back(token_back[:, :, 0], position),
            turn_back(token_back[:, :, 1], position),
            token_back[:, :, 2],
        ],
        axis=2,
    )
    grad_project = grad_project.reshape(row_count, token_span, 3 * model_width).astype(jnp.bfloat16)
    grad_w_qkv = jnp.einsum(
        "rtd,rte->de", normed_one, grad_project, preferred_element_type=jnp.float32
    )
    grad_b_qkv = jnp.sum(grad_project.astype(jnp.float32), axis=(0, 1))
    grad_normed_one = jnp.einsum(
        "rte,de->rtd", grad_project, w_qkv, preferred_element_type=jnp.float32
    )
    grad_current, grad_gain_one, grad_shift_one = jax.vjp(layer_norm, current, gain_one, shift_one)[
        1
    ](grad_normed_one)
    grad_inputs = grad_hidden + grad_current
    attention_grad = jnp.concatenate(
        [
            grad_gain_one,
            grad_shift_one,
            grad_w_qkv.reshape(-1),
            grad_b_qkv,
            grad_w_out.reshape(-1),
            grad_b_out,
        ]
    )
    attention_share = lax.psum_scatter(
        attention_grad, ("dp", "tok"), scatter_dimension=0, tiled=True
    )
    count_now = step_count[0]
    shard_index = lax.axis_index(("dp", "tok"))
    attention_places = shard_index * attention_params.shape[0] + jnp.arange(
        attention_params.shape[0], dtype=jnp.int32
    )
    feedforward_places = shard_index * feedforward_params.shape[0] + jnp.arange(
        feedforward_params.shape[0], dtype=jnp.int32
    )
    attention_step = adam_update(
        attention_params,
        attention_share / tokens_all,
        attention_first,
        attention_second,
        count_now,
        decay_mask(attention_places, attention_shapes()),
    )
    feedforward_step = adam_update(
        feedforward_params,
        feedforward_share / tokens_all,
        feedforward_first,
        feedforward_second,
        count_now,
        decay_mask(feedforward_places, feedforward_shapes()),
    )
    mixing_step = adam_update(
        mixing_offsets, mixing_grad, mixing_first, mixing_second, count_now, 0.0
    )
    return (
        mixed,
        grad_inputs,
        grad_history,
        attention_step[0],
        attention_step[1],
        attention_step[2],
        feedforward_step[0],
        feedforward_step[1],
        feedforward_step[2],
        mixing_step[0],
        mixing_step[1],
        mixing_step[2],
    )


def solution(mesh):
    in_specs = (
        P("dp", "tok", None),
        P(None, "dp", "tok", None),
        P("dp", None),
        P("dp", "tok", None),
        P(("dp", "tok")),
        P(("dp", "tok")),
        P(("dp", "tok")),
        P(("dp", "tok")),
        P(("dp", "tok")),
        P(("dp", "tok")),
        P(),
        P(),
        P(),
        P(),
    )
    out_specs = (
        P("dp", "tok", None),
        P("dp", "tok", None),
        P(None, "dp", "tok", None),
        P(("dp", "tok")),
        P(("dp", "tok")),
        P(("dp", "tok")),
        P(("dp", "tok")),
        P(("dp", "tok")),
        P(("dp", "tok")),
        P(),
        P(),
        P(),
    )
    return jax.shard_map(shards, mesh=mesh, in_specs=in_specs, out_specs=out_specs, check_vma=False)
```

profile of v0, /device:TPU:0, one launch (start us, length us, event | category | flops | bytes accessed | tf_op | source)
XLA Modules:
  0.0 1650.7 jit_solution(15164035626026914960)
XLA Ops:
  13.4 5.9 dynamic-update-slice.1
  28.7 249.7 %all-reduce.15.cloned.1.call-done = (bf16[2363904]{0:T(1024)(128)(2,1)}, bf16[4723968]{0:T(1024)(128)(2,1)}) async-done(((bf16[2363904]{0:T(1024)(128)(2,1)}, bf16[4723968]{0:T(1024)(128)(2,1)}), (bf16[2363904]{0:T(1024)(128)(2,1)}, bf16[4723968]{0:T(1024)(128)(2,1)})) %all-reduce.15.cloned.1.call-update) | async-done | bytes 14175760
  288.7 10.4 convolution_add_fusion
  299.0 9.6 copy.177
  318.4 6.6 copy.180
  330.2 53.8 %all-to-all-done = bf16[4,2,256,3,384]{4,2,3,1,0:T(8,128)(2,1)} async-done(((bf16[4,2,256,3,384]{4,2,3,1,0:T(8,128)(2,1)}), bf16[4,2,256,3,384]{4,2,3,1,0:T(8,128)(2,1)}, u32[]{:S(2)}, u32[]{:S(2)}) %all-to-all-start) | async-done | bytes 4718624 | tf_op jit(solution)/shard_map/all_to_all | solution.py:284
  388.0 39.7 %fusion.38 = f32[1,4,256,768]{3,0,2,1:T(1,128)} fusion(bf16[24,4,256,768]{3,2,1,0:T(8,128)(2,1)} %param.21, f32[25]{0:T(128)S(1)} %fusion.79), kind=kOutput, calls=%fused_computation.69 | convolution fusion | flops 37748736 | bytes 40894564 | tf_op jit(solution)/shard_map/j,jrtd->rtd/dot_general | solution.py:307
  428.3 8.4 copy.181
  436.7 8.7 reshape.549
  445.5 72.2 %while.40 = (s32[]{:T(128)}, bf16[4,512,384]{2,1,0:T(8,128)(2,1)}, f32[4,6,512]{2,1,0:T(8,128)}, s32[4]{0:T(128)S(1)}, bf16[2,1024,3,6,64]{1,4,3,2,0:T(8,128)(2,...) while((s32[]{:T(128)}, bf16[4,512,384]{2,1,0:T(8,128)(2,1)}, ...), condition=%wide.region_8.9_spmd, body=%wide.region_5.8_spmd.sunk | while | flops 846395904 | bytes 50206144 | solution.py:165
  525.6 9.2 fusion.85
  538.2 8.2 reshape.575
  546.4 9.2 reshape.576
  564.8 8.2 fusion.76
  573.0 16.2 convert_reduce_fusion
  589.2 10.8 multiply_reduce_fusion.3
  618.6 7.9 convolution_bitcast_fusion.2
  632.2 6.5 all-to-all-done.3
  643.8 191.8 %while.42 = (s32[]{:T(128)}, bf16[2,1024,3,6,64]{1,4,3,2,0:T(8,128)(2,1)}, bf16[2,1024,3,6,64]{1,4,3,2,0:T(8,128)(2,1)}, bf16[2,1024,6,64]{1,3,2,0:T(8,128)(2,1)...) while((s32[]{:T(128)}, ...), condition=%wide.region_17.18_spmd, body=%wide.region_13.17_spmd.sunk | while | flops 2073623040 | bytes 216241552 | solution.py:227
  651.2 83.1 %while.43 = (s32[]{:T(128)}, f32[1024,6,64]{0,2,1:T(8,128)}, f32[1024,6,64]{0,2,1:T(8,128)}, bf16[2,512,6,64]{1,3,2,0:T(8,128)(2,1)}, bf16[1024,3,6,64]{0,3,2,1:...) while((s32[]{:T(128)}, f32[1024,6,64]{0,2,1:T(8,128)}, ...), condition=%wide.region_16.16_spmd.clone, body=%wide.region_14.15_spmd.clone.sunk | while | flops 2065758720 | bytes 181514736 | solution.py:221
  654.6 6.4 fusion.137
  662.7 7.7 multiply_reduce_fusion.7
  684.7 7.7 bitcast_add_fusion.6
  695.7 6.4 fusion.137
  703.8 7.7 multiply_reduce_fusion.7
  726.2 8.1 bitcast_add_fusion.6
  747.0 83.1 %while.43 = (s32[]{:T(128)}, f32[1024,6,64]{0,2,1:T(8,128)}, f32[1024,6,64]{0,2,1:T(8,128)}, bf16[2,512,6,64]{1,3,2,0:T(8,128)(2,1)}, bf16[1024,3,6,64]{0,3,2,1:...) while((s32[]{:T(128)}, f32[1024,6,64]{0,2,1:T(8,128)}, ...), condition=%wide.region_16.16_spmd.clone, body=%wide.region_14.15_spmd.clone.sunk | while | flops 2065758720 | bytes 181514736 | solution.py:221
  750.3 6.4 fusion.137
  758.5 7.7 multiply_reduce_fusion.7
  780.4 7.7 bitcast_add_fusion.6
  791.4 6.4 fusion.137
  799.6 7.7 multiply_reduce_fusion.7
  821.9 8.1 bitcast_add_fusion.6
  835.6 12.6 copy.189
  853.3 13.9 convolution_bitcast_fusion
  867.2 10.7 reshape.563
  885.4 80.6 %dynamic-update-slice.4 = f32[4723968]{0:T(1024)} dynamic-update-slice(f32[4723968]{0:T(1024)} %constant_dynamic-update-slice_fusion.2, f32[2359296]{0:T(1024)} %bitcast.229, s32[]{} %constant.327) | dynamic-update-slice | bytes 18874372
  967.3 80.0 %dynamic-update-slice.6 = f32[4723968]{0:T(1024)} dynamic-update-slice(f32[4723968]{0:T(1024)} %constant_dynamic-update-slice_fusion.8, f32[2359296]{0:T(1024)} %reshape.563, s32[]{} %constant.329) | dynamic-update-slice | bytes 18874372
  1055.1 9.6 copy.192
  1080.7 6.6 convolution_bitcast_fusion.1
  1088.9 8.2 reshape.560
  1097.2 18.3 %multiply_reduce_fusion.2 = (f32[]{:T(128)}, f32[768]{0:T(1024)S(1)}, bf16[4,256,768]{2,1,0:T(8,128)(2,1)}, f32[4,256,768]{2,1,0:T(8,128)}) fusion(bf16[4,256,768]{2,1,0:T(8,128)(2,1)} %param.23, f32[]{:T(128)} %bitcast.23, f32[1,4,256,768]{3,0,2,1:T(1,128)} %fusion.38, f32[4,256]{1,0:T(4,128)S(1)} %negate_multiply_fusion, ...), kind=kOutput, calls=%fused_computation.115 | convolution fusion | flops 4881382400 | bytes 37790728 | tf_op jit(solution)/shard_map/dot_general | solution.py:302
  1119.4 60.9 %dynamic-update-slice.10 = f32[2363904]{0:T(1024)} dynamic-update-slice(f32[2363904]{0:T(1024)} %constant_dynamic-update-slice_fusion.1, f32[1769472]{0:T(1024)} %reshape.560, s32[]{} %constant.327) | dynamic-update-slice | bytes 14155780
  1181.6 20.0 %dynamic-update-slice.12 = f32[2363904]{0:T(1024)} dynamic-update-slice(f32[2363904]{0:T(1024)} %constant_dynamic-update-slice_fusion.6, f32[589824]{0:T(1024)S(1)} %copy-done.11, s32[]{} %constant.332) | dynamic-update-slice | bytes 4718596
  1204.9 15.3 multiply_reduce_fusion.1
  1220.3 24.8 %broadcast_multiply_fusion = f32[24,4,256,768]{3,2,1,0:T(8,128)} fusion(f32[4,256,768]{2,1,0:T(8,128)S(1)} %get-tuple-element.356, f32[24]{0:T(128)S(1)} %bitcast.257), kind=kLoop, calls=%fused_computation.71 | loop fusion | flops 18874368 | bytes 78643296 | tf_op jit(solution)/shard_map/mul | solution.py:312
  1245.9 41.1 %psum.7 = f32[25]{0:T(128)S(1)} all-reduce(f32[25]{0:T(128)S(1)} %pad_maximum_fusion.2), channel_id=1, replica_groups=mesh['dp'=8,'tok'=4] {'dp','tok'}, use_global_device_ids=true, to_apply=%region_31.32 | all-reduce | flops 25 | bytes 200 | tf_op jit(solution)/shard_map/psum | solution.py:317
  1287.5 350.8 %all-reduce.13.cloned.1.call-done = (f32[2363904]{0:T(1024)}, f32[4723968]{0:T(1024)}) async-done(((f32[2363904]{0:T(1024)}, f32[4723968]{0:T(1024)}), (f32[2363904]{0:T(1024)}, f32[4723968]{0:T(1024)})) %all-reduce.13.cloned.1.call-update) | async-done | bytes 28351504
  (408 shorter events, 303.3 us)
Async XLA Ops:
  7.2 271.2 %all-reduce.15.cloned.1.call-start = ((), (), s32[]{:S(2)}) async-start(), calls=%async_computation.6 | async-start | bytes 28356608
  26.8 261.9 %copy-start.34 = (f32[4,256]{1,0:T(4,128)}, f32[4,256]{1,0:T(4,128)S(1)}, u32[]{:S(2)}) copy-start(f32[4,256]{1,0:T(4,128)S(1)} %broadcast_multiply_fusion.2) | copy-start | bytes 12292
  27.4 251.0 %copy-start.36 = (f32[4,256]{1,0:T(4,128)}, f32[4,256]{1,0:T(4,128)S(1)}, u32[]{:S(2)}) copy-start(f32[4,256]{1,0:T(4,128)S(1)} %fusion.56) | copy-start | bytes 12292
  27.4 261.3 %copy-start.40 = (f32[4,256]{1,0:T(4,128)}, f32[4,256]{1,0:T(4,128)S(1)}, u32[]{:S(2)}) copy-start(f32[4,256]{1,0:T(4,128)S(1)} %fusion.77) | copy-start | bytes 12292
  325.0 58.9 %all-to-all-start = ((bf16[4,2,256,3,384]{4,2,3,1,0:T(8,128)(2,1)}), bf16[4,2,256,3,384]{4,2,3,1,0:T(8,128)(2,1)}, u32[]{:S(2)}, u32[]{:S(2)}) async-start(bf16[4,2,256,3,384]{4,2,3,1,0:T(8,128)(2,1)} %bitcast.236), calls=%async_computation | async-start | bytes 9437184 | tf_op jit(solution)/shard_map/all_to_all | solution.py:284
  330.1 97.6 %copy-start.54 = (f32[25]{0:T(128)}, f32[25]{0:T(128)S(1)}, u32[]{:S(2)}) copy-start(f32[25]{0:T(128)S(1)} %fusion.79) | copy-start | bytes 304
  384.6 60.9 %all-to-all-start.1 = ((s32[4,2,256]{2,1,0:T(2,128)}), s32[4,2,256]{2,1,0:T(2,128)S(1)}, u32[]{:S(2)}, u32[]{:S(2)}) async-start(s32[4,2,256]{2,1,0:T(2,128)} %bitcast.34), calls=%async_computation.1 | async-start | bytes 16384 | tf_op jit(solution)/shard_map/all_to_all | solution.py:285
  521.9 34.5 %all-to-all-start.2 = ((bf16[1,2,1024,384]{3,1,0,2:T(2,128)(2,1)}), bf16[1,2,1024,384]{3,1,0,2:T(2,128)(2,1)S(1)}, u32[]{:S(2)}, u32[]{:S(2)}) async-start(bf16[1,2,1024,384]{3,1,0,2:T(2,128)(2,1)} %copy.183), calls=%async_computation.2 | async-start | bytes 3145728 | tf_op jit(solution)/shard_map/all_to_all | solution.py:287
  556.4 16.6 %copy-start.45 = (f32[3072]{0:T(1024)}, f32[3072]{0:T(1024)S(1)}, u32[]{:S(2)}) copy-start(f32[3072]{0:T(1024)S(1)} %slice_convert_fusion.1) | copy-start | bytes 36868
  564.0 54.5 %copy-start.3 = (f32[4,256,768]{2,1,0:T(8,128)}, f32[4,256,768]{2,1,0:T(8,128)S(1)}, u32[]{:S(2)}) copy-start(f32[4,256,768]{2,1,0:T(8,128)S(1)} %get-tuple-element.365) | copy-start | bytes 9437188
  564.1 8.9 slice-start.3
  564.8 8.2 copy-start.13
  564.8 8.2 slice-start.4
  589.2 10.8 copy-start.12
  614.2 24.5 %all-to-all-start.3 = ((bf16[4,2,256,384]{3,2,1,0:T(8,128)(2,1)}), bf16[4,2,256,384]{3,2,1,0:T(8,128)(2,1)}, u32[]{:S(2)}, u32[]{:S(2)}) async-start(bf16[4,2,256,384]{3,2,1,0:T(8,128)(2,1)} %bitcast.240), calls=%async_computation.3 | async-start | bytes 3145728 | tf_op jit(solution)/shard_map/all_to_all | solution.py:350
  643.9 7.2 copy-start.28
  662.7 7.7 slice-start
  662.7 7.7 slice-start.1
  662.7 8.6 slice-start.2
  703.8 7.8 slice-start
  703.8 7.8 slice-start.1
  703.8 8.6 slice-start.2
  739.7 7.2 copy-start.28
  758.4 7.8 slice-start
  758.5 7.8 slice-start.1
  758.5 8.6 slice-start.2
  799.5 7.8 slice-start
  799.5 7.8 slice-start.1
  799.6 8.6 slice-start.2
  848.2 199.2 %all-to-all-start.4 = ((bf16[1,2,1024,3,384]{4,1,3,0,2:T(2,128)(2,1)}), bf16[1,2,1024,3,384]{4,1,3,0,2:T(2,128)(2,1)}, u32[]{:S(2)}, u32[]{:S(2)}) async-start(bf16[1,2,1024,3,384]{4,1,3,0,2:T(2,128)(2,1)} %copy.189), calls=%async_computation.4 | async-start | bytes 9437184 | tf_op jit(solution)/shard_map/all_to_all | solution.py:355
  853.3 785.0 %all-reduce.13.cloned.1.call-start = ((), (), s32[]{:S(2)}) async-start(), calls=%async_computation.5 | async-start | bytes 56713216
  885.4 80.6 %copy-start.47 = (f32[3072]{0:T(1024)S(1)}, f32[3072]{0:T(1024)}, u32[]{:S(2)}) copy-start(f32[3072]{0:T(1024)} %get-tuple-element.368) | copy-start | bytes 36868
  1080.6 6.6 copy-start.17
  1088.9 8.3 copy-start.4
  1088.9 8.3 copy-start.44
  1088.9 8.3 copy-start.49
  1119.4 62.2 %copy-start.11 = (f32[589824]{0:T(1024)S(1)}, f32[589824]{0:T(1024)}, u32[]{:S(2)}) copy-start(f32[589824]{0:T(1024)} %reshape.561) | copy-start | bytes 7077892
  1180.3 21.4 %copy-start.42 = (f32[768]{0:T(1024)S(1)}, f32[768]{0:T(1024)}, u32[]{:S(2)}) copy-start(f32[768]{0:T(1024)} %get-tuple-element.320) | copy-start | bytes 9220
  1204.9 15.3 copy-start.55
  1220.2 66.8 %copy-start.57 = (f32[25]{0:T(128)S(1)}, f32[25]{0:T(128)}, u32[]{:S(2)}) copy-start(f32[25]{0:T(128)} %param.30) | copy-start | bytes 304
  1220.2 66.8 %copy-start.58 = (f32[25]{0:T(128)S(1)}, f32[25]{0:T(128)}, u32[]{:S(2)}) copy-start(f32[25]{0:T(128)} %param.32) | copy-start | bytes 304
  1220.2 66.8 %copy-start.59 = (f32[25]{0:T(128)S(1)}, f32[25]{0:T(128)}, u32[]{:S(2)}) copy-start(f32[25]{0:T(128)} %param.31) | copy-start | bytes 304
  1220.2 418.1 %copy-start.18 = (f32[147624]{0:T(1024)S(1)}, f32[147624]{0:T(1024)}, u32[]{:S(2)}) copy-start(f32[147624]{0:T(1024)} %param.27) | copy-start | bytes 1771492
  1220.3 418.1 %copy-start.26 = (f32[147624]{0:T(1024)S(1)}, f32[147624]{0:T(1024)}, u32[]{:S(2)}) copy-start(f32[147624]{0:T(1024)} %param.29) | copy-start | bytes 1771492
  1220.3 418.0 %copy-start.27 = (f32[147624]{0:T(1024)S(1)}, f32[147624]{0:T(1024)}, u32[]{:S(2)}) copy-start(f32[147624]{0:T(1024)} %param.28) | copy-start | bytes 1771492
  1245.0 396.3 %copy-start.20 = (f32[73872]{0:T(1024)S(1)}, f32[73872]{0:T(1024)}, u32[]{:S(2)}) copy-start(f32[73872]{0:T(1024)} %param.24) | copy-start | bytes 886468
  1245.0 396.3 %copy-start.32 = (f32[73872]{0:T(1024)S(1)}, f32[73872]{0:T(1024)}, u32[]{:S(2)}) copy-start(f32[73872]{0:T(1024)} %param.26) | copy-start | bytes 886468
  1245.0 396.3 %copy-start.33 = (f32[73872]{0:T(1024)S(1)}, f32[73872]{0:T(1024)}, u32[]{:S(2)}) copy-start(f32[73872]{0:T(1024)} %param.25) | copy-start | bytes 886468
  (51 other events, 156.0 us)
Sparse Core Ops, SparseCore 0:
  25.2 253.1 all-reduce.14
  1203.1 435.1 all-reduce.12
where the time goes:
time: 1680 us; the launch traced here: 1650 us
  waiting for transfers between devices  661 us (39%)
  local copies, waits for them, and re-layouts  475 us (28%)
  matrix products  290 us (17%)
  other arithmetic  125 us (7%)
  blocking collectives  41.1 us (2%)
  starting transfers between devices  21.8 us (1%)
  loops' own time  21.1 us (1%)
    unnamed x4, waiting for transfers between devices  601 us
    unnamed x128, local copies, waits for them, and re-layouts  278 us
    all_to_all x1, waiting for transfers between devices, shards(): lax.all_to_all(send_qkv, 'tok', split_axis=0, concat_axis=2, tiled=True)  53.8 us
    psum x1, blocking collectives, shards(): mixing_grad = lax.psum(mixing_terms, ('dp', 'tok')) / tokens_all  41.1 us
    dot_general x1, matrix products, shards(): jnp.einsum('j,jrtd->rtd', coefficient[:-1], history, preferred_element_ty...  39.7 us
    dot_general x8, matrix products, block_scores(): jnp.einsum('qhd,khd->hqk', queries, keys_all, preferred_element_type=jnp....  35.4 us
  transfers between devices with their start and end apart: 7, of which 4 were waited for; matrix products, arithmetic and copies ran while one was open for 21% of the time, Pallas kernels for 0%

commit v1 on v0

--- a/solution.py
+++ b/solution.py
@@ -4,6 +4,8 @@
 import jax
 import jax.numpy as jnp
 from jax import lax
+from jax.experimental import pallas as pl
+from jax.experimental.pallas import tpu as pltpu
 from jax.sharding import PartitionSpec as P
 
 D = 768
@@ -236,7 +238,7 @@
     return row_grads.reshape(1, item_count, length_all, 3, group_width)
 
 
-def shards(
+def general_shards(
     inputs,
     history,
     document_lengths,
@@ -431,6 +433,841 @@
     )
 
 
+VMEM_LIMIT = 58 * 1024 * 1024
+BF = jnp.bfloat16
+F32 = jnp.float32
+
+
+def cols(ref, first, count):
+    lead = math.prod(ref.shape[:-3]) * ref.shape[-2]
+    pieces = []
+    for at in range(first, first + count):
+        index = (slice(None),) * (len(ref.shape) - 3) + (at,)
+        pieces.append(ref[index].reshape(lead, 128))
+    return pieces[0] if count == 1 else jnp.concatenate(pieces, axis=1)
+
+
+def put_tiles(ref, row_at, col_at, value):
+    rows, width = value.shape
+    for at in range(width // 128):
+        ref[pl.ds(row_at, rows // 16), col_at + at] = value[:, 128 * at : 128 * at + 128].reshape(
+            rows // 16, 16, 128
+        )
+
+
+def norm_parts(values):
+    mean = jnp.mean(values, axis=1, keepdims=True)
+    centered = values - mean
+    inverse = lax.rsqrt(jnp.mean(centered * centered, axis=1, keepdims=True) + norm_epsilon)
+    return centered, inverse
+
+
+def nt_dot(left, right):
+    return lax.dot_general(left, right, (((1,), (1,)), ((), ())), preferred_element_type=F32)
+
+
+def nn_dot(left, right):
+    return lax.dot_general(left, right, (((1,), (0,)), ((), ())), preferred_element_type=F32)
+
+
+def swap_halves(values):
+    width = values.shape[1]
+    lane = lax.broadcasted_iota(jnp.int32, values.shape, 1)
+    return jnp.where(
+        lane % HEAD_DIM < HEAD_DIM // 2,
+        pltpu.roll(values, width - HEAD_DIM // 2, 1),
+        pltpu.roll(values, HEAD_DIM // 2, 1),
+    )
+
+
+def project_kernel(x_ref, w_ref, vec_ref, cos_ref, sin_ref, n1_ref, q_ref, k_ref, v_ref):
+    width = x_ref.shape[1]
+    centered, inverse = norm_parts(x_ref[...].astype(F32))
+    normed = (centered * inverse * vec_ref[0:1, :width] + vec_ref[1:2, :width]).astype(BF)
+    n1_ref[...] = normed
+    cosine = jnp.concatenate([cos_ref[...]] * 2, axis=1)
+    sine = jnp.concatenate([sin_ref[...]] * 2, axis=1)
+    per_part = width // 256
+    for at in range(3 * per_part):
+        part = nn_dot(normed, cols(w_ref, 2 * at, 2)) + vec_ref[2:3, 256 * at : 256 * at + 256]
+        spot = slice(256 * (at % per_part), 256 * (at % per_part) + 256)
+        if at < 2 * per_part:
+            part = part * cosine + swap_halves(part) * sine
+        if at < per_part:
+            q_ref[:, spot] = (part * HEAD_DIM ** (-0.5)).astype(BF)
+        elif at < 2 * per_part:
+            k_ref[:, spot] = part.astype(BF)
+        else:
+            v_ref[:, spot] = part.astype(BF)
+
+
+def project(x_row, w_qkv, vectors, cosine, sine):
+    length, width = x_row.shape
+    tile = 256
+    whole = pl.BlockSpec(w_qkv.shape, lambda i: (0,) * w_qkv.ndim)
+    rows = pl.BlockSpec((tile, width), lambda i: (i, 0))
+    trig = pl.BlockSpec((tile, 128), lambda i: (i, 0))
+    out = jax.ShapeDtypeStruct((length, width), BF)
+    return pl.pallas_call(
+        project_kernel,
+        grid=(length // tile,),
+        in_specs=[rows, whole, pl.BlockSpec(vectors.shape, lambda i: (0, 0)), trig, trig],
+        out_specs=[rows] * 4,
+        out_shape=[out] * 4,
+        compiler_params=pltpu.CompilerParams(vmem_limit_bytes=VMEM_LIMIT),
+        name="project",
+    )(x_row, w_qkv, vectors, cosine, sine)
+
+
+def key_range(block, block_rows, reach):
+    return max(0, block * block_rows - reach), (block + 1) * block_rows
+
+
+def fill_bias(bias_ref, seg_col_ref, seg_row_ref, block_rows, reach):
+    length = seg_row_ref.shape[1]
+    at = 0
+    for block in range(length // block_rows):
+        low, high = key_range(block, block_rows, reach)
+        shape = (high - low, block_rows)
+        key_place = low + lax.broadcasted_iota(jnp.int32, shape, 0)
+        query_place = block * block_rows + lax.broadcasted_iota(jnp.int32, shape, 1)
+        key_seg = seg_col_ref[low:high, :]
+        query_seg = seg_row_ref[:, block * block_rows : (block + 1) * block_rows]
+        allowed = (key_place <= query_place) & (key_seg == query_seg)
+        allowed = allowed & ((key_seg < DOCS) | (key_place == query_place))
+        bias_ref[at : at + high - low, :] = jnp.where(allowed, 0.0, masked_score)
+        at = at + high - low
+
+
+def bias_rows(length, block_rows, reach):
+    return sum(
+        high - low
+        for low, high in (key_range(b, block_rows, reach) for b in range(length // block_rows))
+    )
+
+
+def head_mask(values, head):
+    lane = lax.broadcasted_iota(jnp.int32, values.shape, 1)
+    keep = lane < HEAD_DIM if head == 0 else lane >= HEAD_DIM
+    return jnp.where(keep, values, jnp.zeros_like(values))
+
+
+def attend_kernel(block_rows, reach, q_ref, k_ref, v_ref, sc_ref, sr_ref, o_ref, lse_ref, bias_ref):
+    length = q_ref.shape[0]
+
+    @pl.when(pl.program_id(0) == 0)
+    def _():
+        fill_bias(bias_ref, sc_ref, sr_ref, block_rows, reach)
+
+    keys = k_ref[...]
+    key_heads = [head_mask(keys, 0), head_mask(keys, 1)]
+    value_turned = v_ref[...].T
+    at = 0
+    for block in range(length // block_rows):
+        low, high = key_range(block, block_rows, reach)
+        spot = slice(block * block_rows, (block + 1) * block_rows)
+        queries = q_ref[spot, :]
+        bias = bias_ref[at : at + high - low, :]
+        at = at + high - low
+        halves = []
+        for head in range(2):
+            scores = nt_dot(key_heads[head][low:high], queries) + bias
+            top = jnp.max(scores, axis=0, keepdims=True)
+            exponent = jnp.exp(scores - top)
+            total = jnp.sum(exponent, axis=0, keepdims=True)
+            probs = (exponent * (1.0 / total)).astype(BF)
+            lse_ref[0, head : head + 1, spot] = top + jnp.log(total)
+            turned = value_turned[HEAD_DIM * head : HEAD_DIM * head + HEAD_DIM, low:high]
+            halves.append(nn_dot(turned, probs))
+        o_ref[spot, :] = jnp.concatenate(halves, axis=0).T.astype(BF)
+
+
+def row_attend(queries, keys, values, seg_col, seg_row, reach):
+    length, width = queries.shape
+    block_rows = 256
+    pairs = width // 128
+    pair = pl.BlockSpec((length, 128), lambda p: (0, p))
+    return pl.pallas_call(
+        partial(attend_kernel, block_rows, reach),
+        grid=(pairs,),
+        in_specs=[
+            pair,
+            pair,
+            pair,
+            pl.BlockSpec(seg_col.shape, lambda p: (0, 0)),
+            pl.BlockSpec(seg_row.shape, lambda p: (0, 0)),
+        ],
+        out_specs=[pair, pl.BlockSpec((1, 2, length), lambda p: (p, 0, 0))],
+        out_shape=[
+            jax.ShapeDtypeStruct((length, width), BF),
+            jax.ShapeDtypeStruct((pairs, 2, length), F32),
+        ],
+        scratch_shapes=[pltpu.VMEM((bias_rows(length, block_rows, reach), block_rows), F32)],
+        compiler_params=pltpu.CompilerParams(vmem_limit_bytes=VMEM_LIMIT),
+        name="attend",
+    )(queries, keys, values, seg_col, seg_row)
+
+
+def attend_back_kernel(
+    block_rows, reach, q_ref, k_ref, v_ref, g_ref, lse_ref, sc_ref, sr_ref, cos_ref, sin_ref,
+    gq_ref, gk_ref, gv_ref, bias_ref, dq_acc, dk_acc, dv_acc,
+):
+    length = q_ref.shape[0]
+
+    @pl.when(pl.program_id(0) == 0)
+    def _():
+        fill_bias(bias_ref, sc_ref, sr_ref, block_rows, reach)
+
+    keys = k_ref[...]
+    key_heads = [head_mask(keys, 0), head_mask(keys, 1)]
+    key_turned = keys.T
+    vals = v_ref[...]
+    value_heads = [head_mask(vals, 0), head_mask(vals, 1)]
+    dk_acc[...] = jnp.zeros_like(dk_acc)
+    dv_acc[...] = jnp.zeros_like(dv_acc)
+    at = 0
+    for block in range(length // block_rows):
+        low, high = key_range(block, block_rows, reach)
+        spot = slice(block * block_rows, (block + 1) * block_rows)
+        queries = q_ref[spot, :]
+        grads = g_ref[spot, :]
+        bias = bias_ref[at : at + high - low, :]
+        at = at + high - low
+        halves = []
+        for head in range(2):
+            scores = nt_dot(key_heads[head][low:high], queries) + bias
+            probs = jnp.exp(scores - lse_ref[0, head : head + 1, spot])
+            dprobs = nt_dot(value_heads[head][low:high], grads)
+            inner = jnp.sum(probs * dprobs, axis=0, keepdims=True)
+            dscores = (probs * (dprobs - inner)).astype(BF)
+            turned = key_turned[HEAD_DIM * head : HEAD_DIM * head + HEAD_DIM, low:high]
+            halves.append(nn_dot(turned, dscores))
+            dk_acc[low:high, :] += nn_dot(dscores, head_mask(queries, head))
+            dv_acc[low:high, :] += nn_dot(probs.astype(BF), head_mask(grads, head))
+        dq_acc[spot, :] = jnp.concatenate(halves, axis=0).T * HEAD_DIM ** (-0.5)
+    cosine = cos_ref[...]
+    sine = sin_ref[...]
+    grad_query = dq_acc[...].astype(BF).astype(F32)
+    grad_key = dk_acc[...].astype(BF).astype(F32)
+    gq_ref[...] = (grad_query * cosine - swap_halves(grad_query) * sine).astype(BF)
+    gk_ref[...] = (grad_key * cosine - swap_halves(grad_key) * sine).astype(BF)
+    gv_ref[...] = dv_acc[...].astype(BF)
+
+
+def row_attend_back(queries, keys, values, grads, lse, seg_col, seg_row, cosine, sine, reach):
+    length, width = queries.shape
+    block_rows = 256
+    pair = pl.BlockSpec((length, 128), lambda p: (0, p))
+    trig = pl.BlockSpec((length, 128), lambda p: (0, 0))
+    out = jax.ShapeDtypeStruct((length, width), BF)
+    return pl.pallas_call(
+        partial(attend_back_kernel, block_rows, reach),
+        grid=(width // 128,),
+        in_specs=[
+            pair, pair, pair, pair,
+            pl.BlockSpec((1, 2, length), lambda p: (p, 0, 0)),
+            pl.BlockSpec(seg_col.shape, lambda p: (0, 0)),
+            pl.BlockSpec(seg_row.shape, lambda p: (0, 0)),
+            trig, trig,
+        ],
+        out_specs=[pair] * 3,
+        out_shape=[out] * 3,
+        scratch_shapes=[pltpu.VMEM((bias_rows(length, block_rows, reach), block_rows), F32)]
+        + [pltpu.VMEM((length, 128), F32)] * 3,
+        compiler_params=pltpu.CompilerParams(vmem_limit_bytes=VMEM_LIMIT),
+        name="attend_back",
+    )(queries, keys, values, grads, lse, seg_col, seg_row, cosine, sine)
+
+
+gelu_root = math.sqrt(2.0 / math.pi)
+
+
+def middle_kernel(
+    x_ref, att_ref, cot_ref, wout_ref, wup_ref, wdown_ref, vec_ref, bup_ref, c_ref,
+    bout_ref, gatt_ref, ghid_ref, gwup_ref, gwdown_ref, gwout_ref, gbup_ref, gvec_ref,
+    hidden_ref, n2_ref, n2t_ref, gb_ref, acc_out, acc_gn, act_ref, gup_ref,
+):
+    step = pl.program_id(0)
+    steps = pl.num_programs(0)
+    length, width = x_ref.shape
+    tile = 256
+    tiles = length // tile
+    mix = c_ref[0]
+
+    @pl.when(step == 0)
+    def _():
+        @pl.loop(0, tiles)
+        def _(t):
+            rows = pl.ds(pl.multiple_of(t * tile, tile), tile)
+            attended = att_ref[rows, :]
+            hidden = x_ref[rows, :].astype(F32) + nn_dot(attended, cols(wout_ref, 0, width // 128))
+            hidden = hidden + vec_ref[2:3, :]
+            hidden_ref[rows, :] = hidden
+            centered, inverse = norm_parts(hidden)
+            normed = (centered * inverse * vec_ref[0:1, :] + vec_ref[1:2, :]).astype(BF)
+            n2_ref[rows, :] = normed
+            n2t_ref[:, rows] = normed.T
+            gb_ref[rows, :] = (mix * cot_ref[rows, :].astype(F32)).astype(BF)
+            acc_out[rows, :] = jnp.zeros((tile, width), F32)
+            acc_gn[rows, :] = jnp.zeros((tile, width), F32)
+
+        gvec_ref[...] = jnp.zeros_like(gvec_ref)
+
+    w_up = cols(wup_ref, 0, 2)
+    w_down = cols(wdown_ref, 0, width // 128)
+    gbup_ref[...] = jnp.zeros_like(gbup_ref)
+
+    @pl.loop(0, tiles)
+    def _(t):
+        rows = pl.ds(pl.multiple_of(t * tile, tile), tile)
+        up = nn_dot(n2_ref[rows, :], w_up) + bup_ref[0:1, :]
+        square = up * up
+        turn = jnp.tanh(gelu_root * up * (1.0 + 0.044715 * square))
+        half = 0.5 * (1.0 + turn)
+        active = (up * half).astype(BF)
+        act_ref[rows, :] = active
+        acc_out[rows, :] += nn_dot(active, w_down)
+        slope = half + (0.5 * gelu_root) * up * (1.0 - turn * turn) * (
+            1.0 + (3.0 * 0.044715) * square
+        )
+        grad_up = (nt_dot(gb_ref[rows, :], w_down) * slope).astype(BF)
+        gup_ref[rows, :] = grad_up
+        acc_gn[rows, :] += nt_dot(grad_up, w_up)
+        gbup_ref[0:1, :] += jnp.sum(grad_up.astype(F32), axis=0, keepdims=True)
+
+    grad_up_all = gup_ref[...]
+    for r in range(width // 256):
+        put_tiles(
+            gwup_ref, 16 * r, 0, nn_dot(n2t_ref[256 * r : 256 * r + 256, :], grad_up_all).astype(BF)
+        )
+    active_turned = act_ref[...].T
+    for r in range(width // 256):
+        put_tiles(
+            gwdown_ref, 0, 2 * r, nn_dot(active_turned, gb_ref[:, 256 * r : 256 * r + 256]).astype(BF)
+        )
+
+    @pl.when(step == steps - 1)
+    def _():
+        @pl.loop(0, tiles)
+        def _(t):
+            rows = pl.ds(pl.multiple_of(t * tile, tile), tile)
+            hidden = hidden_ref[rows, :]
+            cot = cot_ref[rows, :].astype(F32)
+            block_out = hidden + acc_out[rows, :] + vec_ref[3:4, :]
+            bout_ref[rows, :] = block_out.astype(bout_ref.dtype)
+            gvec_ref[4:5, :] += jnp.sum(block_out * cot, axis=0, keepdims=True)
+            centered, inverse = norm_parts(hidden)
+            normed = centered * inverse
+            grad_norm = acc_gn[rows, :]
+            gvec_ref[0:1, :] += jnp.sum(normed * grad_norm, axis=0, keepdims=True)
+            gvec_ref[1:2, :] += jnp.sum(grad_norm, axis=0, keepdims=True)
+            scaled = grad_norm * vec_ref[0:1, :]
+            grad_value = inverse * (
+                scaled
+                - jnp.mean(scaled, axis=1, keepdims=True)
+                - normed * jnp.mean(scaled * normed, axis=1, keepdims=True)
+            )
+            grad_hidden = mix * cot + grad_value
+            ghid_ref[rows, :] = grad_hidden
+            grad_attn = grad_hidden.astype(BF)
+            n2_ref[rows, :] = grad_attn
+            n2t_ref[:, rows] = att_ref[rows, :].T
+            gvec_ref[2:3, :] += jnp.sum(grad_attn.astype(F32), axis=0, keepdims=True)
+            gvec_ref[3:4, :] += jnp.sum(gb_ref[rows, :].astype(F32), axis=0, keepdims=True)
+            gatt_ref[rows, :] = nt_dot(grad_attn, cols(wout_ref, 0, width // 128)).astype(BF)
+
+        grad_attn_all = n2_ref[...]
+        for r in range(width // 256):
+            for k in range(width // 256):
+                put_tiles(
+                    gwout_ref, 16 * r, 2 * k,
+                    nn_dot(
+                        n2t_ref[256 * r : 256 * r + 256, :],
+                        grad_attn_all[:, 256 * k : 256 * k + 256],
+                    ).astype(BF),
+                )
+
+
+def middle(x_row, attended, cot_row, w_out, w_up, w_down, vectors, b_up, mix):
+    length, width = x_row.shape
+    (up_array, up_rows), (down_array, down_first) = w_up, w_down
+    inner = b_up.shape[1]
+    steps = inner // 256
+    once = pl.Buffered(1)
+
+    def const(shape):
+        return pl.BlockSpec(shape, lambda i: (0,) * len(shape), pipeline_mode=once)
+
+    rows = const((length, width))
+    row_tiles, col_tiles = width // 16, width // 128
+    return pl.pallas_call(
+        middle_kernel,
+        grid=(steps,),
+        in_specs=[
+            rows, rows, rows, const(w_out.shape),
+            pl.BlockSpec((up_rows, up_array.shape[1], 2, 16, 128), lambda i: (0, 0, i, 0, 0)),
+            pl.BlockSpec((16, col_tiles, 16, 128), lambda i: (i + down_first, 0, 0, 0)),
+            const(vectors.shape),
+            pl.BlockSpec((1, 256), lambda i: (0, i)),
+            pl.BlockSpec(memory_space=pltpu.SMEM),
+        ],
+        out_specs=[
+            rows, rows, rows,
+            pl.BlockSpec((row_tiles, 2, 16, 128), lambda i: (0, i, 0, 0)),
+            pl.BlockSpec((16, col_tiles, 16, 128), lambda i: (i, 0, 0, 0)),
+            const((row_tiles, col_tiles, 16, 128)),
+            pl.BlockSpec((8, 256), lambda i: (0, i)),
+            const((8, width)),
+        ],
+        out_shape=[
+            jax.ShapeDtypeStruct((length, width), BF),
+            jax.ShapeDtypeStruct((length, width), BF),
+            jax.ShapeDtypeStruct((length, width), F32),
+            jax.ShapeDtypeStruct((row_tiles, inner // 128, 16, 128), BF),
+            jax.ShapeDtypeStruct((inner // 16, col_tiles, 16, 128), BF),
+            jax.ShapeDtypeStruct((row_tiles, col_tiles, 16, 128), BF),
+            jax.ShapeDtypeStruct((8, inner), F32),
+            jax.ShapeDtypeStruct((8, width), F32),
+        ],
+        scratch_shapes=[
+            pltpu.VMEM((length, width), F32),
+            pltpu.VMEM((length, width), BF),
+            pltpu.VMEM((width, length), BF),
+            pltpu.VMEM((length, width), BF),
+            pltpu.VMEM((length, width), F32),
+            pltpu.VMEM((length, width), F32),
+            pltpu.VMEM((length, 256), BF),
+            pltpu.VMEM((length, 256), BF),
+        ],
+        compiler_params=pltpu.CompilerParams(vmem_limit_bytes=VMEM_LIMIT),
+        name="middle",
+    )(x_row, attended, cot_row, w_out, up_array, down_array, vectors, b_up, mix)
+
+
+def last_kernel(
+    x_ref, n1_ref, ghid_ref, gq_ref, gk_ref, gv_ref, w_ref, vec_ref,
+    gx_ref, gw_ref, gb_ref, gvec_ref, n1t_ref, acc_ref,
+):
+    step = pl.program_id(0)
+    steps = pl.num_programs(0)
+    length, width = x_ref.shape
+    tile = 256
+    tiles = length // tile
+    per_part = steps // 3
+
+    @pl.when(step == 0)
+    def _():
+        @pl.loop(0, tiles)
+        def _(t):
+            rows = pl.ds(pl.multiple_of(t * tile, tile), tile)
+            n1t_ref[:, rows] = n1_ref[rows, :].T
+            acc_ref[rows, :] = jnp.zeros((tile, width), F32)
+
+        gvec_ref[...] = jnp.zeros_like(gvec_ref)
+
+    def one(grad_ref):
+        grads = grad_ref[...]
+        for r in range(width // 256):
+            put_tiles(gw_ref, 16 * r, 0, nn_dot(n1t_ref[256 * r : 256 * r + 256, :], grads).astype(BF))
+        gb_ref[0:1, :] = jnp.sum(grads.astype(F32), axis=0, keepdims=True)
+        weight = cols(w_ref, 0, 2)
+
+        @pl.loop(0, tiles)
+        def _(t):
+            rows = pl.ds(pl.multiple_of(t * tile, tile), tile)
+            acc_ref[rows, :] += nt_dot(grad_ref[rows, :], weight)
+
+    for part, grad_ref in enumerate((gq_ref, gk_ref, gv_ref)):
+        pl.when(step // per_part == part)(partial(one, grad_ref))
+
+    @pl.when(step == steps - 1)
+    def _():
+        @pl.loop(0, tiles)
+        def _(t):
+            rows = pl.ds(pl.multiple_of(t * tile, tile), tile)
+            centered, inverse = norm_parts(x_ref[rows, :].astype(F32))
+            normed = centered * inverse
+            grad_norm = acc_ref[rows, :]
+            gvec_ref[0:1, :] += jnp.sum(normed * grad_norm, axis=0, keepdims=True)
+            gvec_ref[1:2, :] += jnp.sum(grad_norm, axis=0, keepdims=True)
+            scaled = grad_norm * vec_ref[0:1, :]
+            grad_value = inverse * (
+                scaled
+                - jnp.mean(scaled, axis=1, keepdims=True)
+                - normed * jnp.mean(scaled * normed, axis=1, keepdims=True)
+            )
+            gx_ref[rows, :] = (ghid_ref[rows, :] + grad_value).astype(gx_ref.dtype)
+
+
+def last(x_row, n1, grad_hidden, gq, gk, gv, w_qkv, vectors):
+    length, width = x_row.shape
+    array, lead = w_qkv
+    steps = 3 * width // 256
+    per_part = width // 256
+    once = pl.Buffered(1)
+
+    def const(shape):
+        return pl.BlockSpec(shape, lambda i: (0,) * len(shape), pipeline_mode=once)
+
+    def part_spec(part):
+        return pl.BlockSpec(
+            (length, 256), lambda i: (0, jnp.clip(i - part * per_part, 0, per_part - 1))
+        )
+
+    rows = const((length, width))
+    row_tiles = width // 16
+    return pl.pallas_call(
+        last_kernel,
+        grid=(steps,),
+        in_specs=[
+            rows, rows, rows, part_spec(0), part_spec(1), part_spec(2),
+            pl.BlockSpec((lead, array.shape[1], 2, 16, 128), lambda i: (0, 0, i, 0, 0)),
+            const(vectors.shape),
+        ],
+        out_specs=[
+            rows,
+            pl.BlockSpec((row_tiles, 2, 16, 128), lambda i: (0, i, 0, 0)),
+            pl.BlockSpec((8, 256), lambda i: (0, i)),
+            const((8, width)),
+        ],
+        out_shape=[
+            jax.ShapeDtypeStruct((length, width), BF),
+            jax.ShapeDtypeStruct((row_tiles, 3 * width // 128, 16, 128), BF),
+            jax.ShapeDtypeStruct((8, 3 * width), F32),
+            jax.ShapeDtypeStruct((8, width), F32),
+        ],
+        scratch_shapes=[pltpu.VMEM((width, length), BF), pltpu.VMEM((length, width), F32)],
+        compiler_params=pltpu.CompilerParams(vmem_limit_bytes=VMEM_LIMIT),
+        name="last",
+    )(x_row, n1, grad_hidden, gq, gk, gv, array, vectors)
+
+
+def history_kernel(hist_ref, cot_ref, c_ref, part_ref, grad_ref, dots_ref):
+    group = hist_ref.shape[0]
+    first = pl.program_id(1) * group
+    cot = cot_ref[...].astype(F32)
+    rows, width = cot.shape
+
+    @pl.when(pl.program_id(1) == 0)
+    def _():
+        part_ref[...] = jnp.zeros_like(part_ref)
+
+    total = part_ref[...]
+    for j in range(group):
+        mix = c_ref[first + j]
+        past = hist_ref[j].astype(F32)
+        total = total + mix * past
+        grad_ref[j] = mix * cot
+        dots = jnp.sum((past * cot).reshape(rows // 8, 8, width), axis=0)
+        dots_ref[0, 8 * j : 8 * j + 8, :] = sum(
+            dots[:, 128 * k : 128 * k + 128] for k in range(width // 128)
+        )
+    part_ref[...] = total
+
+
+def history_pass(history, cotangent, coefficient):
+    terms, tokens, width = history.shape
+    tile, group = 128, 6
+    return pl.pallas_call(
+        history_kernel,
+        grid=(tokens // tile, terms // group),
+        in_specs=[
+            pl.BlockSpec((group, tile, width), lambda t, j: (j, t, 0)),
+            pl.BlockSpec((tile, width), lambda t, j: (t, 0)),
+            pl.BlockSpec(memory_space=pltpu.SMEM),
+        ],
+        out_specs=[
+            pl.BlockSpec((tile, width), lambda t, j: (t, 0)),
+            pl.BlockSpec((group, tile, width), lambda t, j: (j, t, 0)),
+            pl.BlockSpec((1, 8 * group, 128), lambda t, j: (t, j, 0)),
+        ],
+        out_shape=[
+            jax.ShapeDtypeStruct((tokens, width), F32),
+            jax.ShapeDtypeStruct((terms, tokens, width), F32),
+            jax.ShapeDtypeStruct((tokens // tile, 8 * terms, 128), F32),
+        ],
+        compiler_params=pltpu.CompilerParams(vmem_limit_bytes=VMEM_LIMIT),
+        name="history",
+    )(history, cotangent, coefficient)
+
+
+HALO = 2048
+
+
+class Plan:
+    def __init__(self, devices, shape_list):
+        sizes = [math.prod(shape) for shape in shape_list]
+        starts = [sum(sizes[:i]) for i in range(len(sizes))]
+        self.total = sum(sizes)
+        self.devices = devices
+        self.own = self.total // devices
+        self.matrices = [(starts[i], shape_list[i]) for i in (2, 4)]
+        self.vectors = [(0, sizes[0] + sizes[1]), (starts[3], sizes[3]), (starts[5], sizes[5])]
+        first, second = (math.prod(shape) for _, shape in self.matrices)
+        self.block = (first + second) // devices
+        self.split = devices * first // (first + second)
+        self.rows = [
+            shape[0] // n if n else 0
+            for (_, shape), n in zip(self.matrices, (self.split, devices - self.split))
+        ]
+        self.fits = self.total % devices == 0 and (first + second) % devices == 0
+        for (_, shape), n, rows in zip(
+            self.matrices, (self.split, devices - self.split), self.rows
+        ):
+            self.fits = self.fits and n > 0 and rows * n == shape[0] and rows % 16 == 0
+            self.fits = self.fits and rows * shape[1] == self.block
+        self.owners = [at // self.own for at, _ in self.vectors]
+        if self.fits:
+            for s in range(devices):
+                shift = self.block_start(s) - self.own * s
+                self.fits = self.fits and -HALO <= shift <= HALO
+                self.fits = self.fits and shift + self.block - self.own <= HALO
+                self.fits = self.fits and self.own - self.block - shift <= HALO
+            for (at, size), owner in zip(self.vectors, self.owners):
+                self.fits = self.fits and at + size <= self.own * (owner + 1) + HALO
+            self.fits = self.fits and len(set(self.owners)) == len(self.owners)
+
+    def block_start(self, s):
+        (first, _), (second, _) = self.matrices
+        if isinstance(s, int):
+            return first + self.block * s if s < self.split else second + self.block * (s - self.split)
+        return jnp.where(
+            s < self.split, first + self.block * s, second + self.block * (s - self.split)
+        )
+
+    def tile_shapes(self):
+        return [
+            (rows // 16, shape[1] // 128) for (_, shape), rows in zip(self.matrices, self.rows)
+        ]
+
+    def to_tiles(self, flat, s):
+        forms = [
+            flat.reshape(rt, 16, ct, 128).transpose(0, 2, 1, 3).reshape(rt * ct, 16, 128)
+            for rt, ct in self.tile_shapes()
+        ]
+        return jnp.where(s < self.split, forms[0], forms[1])
+
+    def from_tiles(self, tiles, s):
+        forms = [
+            tiles.reshape(rt, ct, 16, 128).transpose(0, 2, 1, 3).reshape(-1)
+            for rt, ct in self.tile_shapes()
+        ]
+        return jnp.where(s < self.split, forms[0], forms[1])
+
+    def vector_rows(self):
+        return -(-max(size for _, size in self.vectors) // 1024) * 8
+
+    def blocks(self, flat, before, after, s):
+        room = self.vector_rows() * 128
+        joined = jnp.concatenate([before, flat, after, jnp.zeros((room,), flat.dtype)])
+        aligned = lax.dynamic_slice(
+            joined, (HALO + self.block_start(s) - self.own * s,), (self.block,)
+        )
+        place = jnp.int32(0)
+        for (at, _), owner in zip(self.vectors, self.owners):
+            place = jnp.where(s == owner, at - self.own * owner, place)
+        extra = lax.dynamic_slice(joined, (HALO + place,), (room,))
+        return self.to_tiles(aligned, s), extra.reshape(-1, 128)
+
+    def shard(self, aligned, before, after, vectors, s):
+        room = self.vector_rows() * 128
+        edge = jnp.zeros((room,), aligned.dtype)
+        joined = jnp.concatenate([edge, before, aligned, after, edge])
+        begin = self.block_start(s)
+        for (at, size), value in zip(self.vectors, vectors):
+            place = jnp.clip(room + HALO + at - begin, 0, joined.shape[0] - size)
+            joined = lax.dynamic_update_slice(joined, value, (place,))
+        return lax.dynamic_slice(joined, (room + HALO + self.own * s - begin,), (self.own,))
+
+
+def neighbour_edges(values_list, count):
+    axes = ("dp", "tok")
+    tails = jnp.stack([v[-HALO:] for v in values_list])
+    heads = jnp.stack([v[:HALO] for v in values_list])
+    before = lax.ppermute(tails, axes, [(i, (i + 1) % count) for i in range(count)])
+    after = lax.ppermute(heads, axes, [(i, (i - 1) % count) for i in range(count)])
+    return before, after
+
+
+def plans(devices):
+    return Plan(devices, attention_shapes()), Plan(devices, feedforward_shapes())
+
+
+def row_tables(lengths_row, length):
+    places = jnp.arange(length, dtype=jnp.int32)
+    segment, position = layout(lengths_row[None], places)
+    lane = jnp.arange(128, dtype=jnp.int32) % HEAD_DIM
+    half_dim = HEAD_DIM // 2
+    frequency = jnp.exp(
+        (lane % half_dim).astype(jnp.float32) * (-2.0 * math.log(10000.0) / HEAD_DIM)
+    )
+    angle = position[0].astype(jnp.float32)[:, None] * frequency[None, :]
+    sine = jnp.where(lane < half_dim, -1.0, 1.0)[None, :] * jnp.sin(angle)
+    return segment[0], jnp.cos(angle), sine
+
+
+def row_shards(
+    inputs,
+    history,
+    document_lengths,
+    cotangent,
+    attention_params,
+    attention_first,
+    attention_second,
+    feedforward_params,
+    feedforward_first,
+    feedforward_second,
+    mixing_offsets,
+    mixing_first,
+    mixing_second,
+    step_count,
+):
+    row_count, span, width = inputs.shape
+    tok_size = lax.axis_size("tok")
+    devices = lax.axis_size("dp") * tok_size
+    length = span * tok_size
+    tokens_all = row_count * span * devices
+    axes = ("dp", "tok")
+    s = lax.axis_index(axes)
+    plan_a, plan_f = plans(devices)
+    reach = length // 2
+
+    low_a, low_f = attention_params.astype(BF), feedforward_params.astype(BF)
+    before, after = neighbour_edges([low_a, low_f], devices)
+    tiles_a, extra_a = plan_a.blocks(low_a, before[0], after[0], s)
+    tiles_f, extra_f = plan_f.blocks(low_f, before[1], after[1], s)
+    extra = jnp.concatenate([extra_a, extra_f]).reshape(-1, 16, 128)
+    count_a, count_f = tiles_a.shape[0], tiles_f.shape[0]
+    got_a = lax.all_gather(jnp.concatenate([tiles_a, extra]), axes, axis=0, tiled=False)
+    got_f = lax.all_gather(tiles_f, axes, axis=0, tiled=False)
+    extras = got_a[:, count_a:].reshape(devices, -1).astype(F32)
+    room_a = plan_a.vector_rows() * 128
+
+    def pick(plan, which, at):
+        return extras[plan.owners[which], at : at + plan.vectors[which][1]]
+
+    gain_one, shift_one = jnp.split(pick(plan_a, 0, 0), 2)
+    b_qkv, b_out = pick(plan_a, 1, 0), pick(plan_a, 2, 0)
+    gain_two, shift_two = jnp.split(pick(plan_f, 0, room_a), 2)
+    b_up, b_down = pick(plan_f, 1, room_a), pick(plan_f, 2, room_a)
+    (rq, cq), (ro, co) = plan_a.tile_shapes()
+    (ru, cu), (rd, cd) = plan_f.tile_shapes()
+    w_qkv = got_a[: plan_a.split, :count_a].reshape(plan_a.split, rq, cq, 16, 128)
+    w_out = got_a[plan_a.split :, :count_a].reshape(devices - plan_a.split, ro, co, 16, 128)
+    w_up = (got_f.reshape(devices * ru * cu // (ru * cu), ru, cu, 16, 128), plan_f.split)
+    w_down = (got_f.reshape(devices * rd, cd, 16, 128), plan_f.split * rd // 16)
+
+    def stack(vectors, wide):
+        vectors = [jnp.pad(v, (0, wide - v.shape[0])) for v in vectors]
+        vectors = vectors + [jnp.zeros((wide,), F32)] * (8 - len(vectors))
+        return jnp.stack(vectors)
+
+    def to_row(values):
+        return lax.all_to_all(values, "tok", split_axis=0, concat_axis=1, tiled=True).reshape(
+            length, width
+        )
+
+    def from_row(values):
+        return lax.all_to_all(
+            values.reshape(1, length, width), "tok", split_axis=1, concat_axis=0, tiled=True
+        )
+
+    x_row, cot_row = to_row(inputs), to_row(cotangent)
+    own_lengths = lax.dynamic_index_in_dim(document_lengths, lax.axis_index("tok"), 0, False)
+    segment, cosine, sine = row_tables(own_lengths, length)
+    seg_col, seg_row = segment[:, None], segment[None, :]
+
+    term_count = mixing_offsets.shape[0]
+    coefficient = mixing_offsets + (jnp.arange(term_count) == term_count - 1).astype(F32)
+    tokens = row_count * span
+    history_part, grad_history, history_dots = history_pass(
+        history.reshape(term_count - 1, tokens, width), cotangent.reshape(tokens, width), coefficient
+    )
+
+    normed_one, queries, keys, values = project(
+        x_row, w_qkv, stack([gain_one, shift_one, b_qkv], 3 * width), cosine, sine
+    )
+    attended, lse = row_attend(queries, keys, values, seg_col, seg_row, reach)
+    block_out, grad_attended, grad_hidden, gw_up, gw_down, gw_out, gb_up, gvec_two = middle(
+        x_row, attended, cot_row, w_out, w_up, w_down,
+        stack([gain_two, shift_two, b_out, b_down], width), b_up[None, :], coefficient[-1:],
+    )
+    gq, gk, gv = row_attend_back(
+        queries, keys, values, grad_attended, lse, seg_col, seg_row, cosine, sine, reach
+    )
+    grad_row, gw_qkv, gb_qkv, gvec_one = last(
+        x_row, normed_one, grad_hidden, gq, gk, gv, (w_qkv, plan_a.split), stack([gain_one], width)
+    )
+    mixed = history_part.reshape(row_count, span, width) + coefficient[-1] * from_row(
+        block_out
+    ).astype(F32)
+    grad_inputs = from_row(grad_row).astype(F32)
+
+    small = jnp.concatenate(
+        [
+            gvec_one[0], gvec_one[1], gb_qkv[0], gvec_two[2],
+            gvec_two[0], gvec_two[1], gb_up[0], gvec_two[3],
+            jnp.sum(history_dots.reshape(-1, term_count - 1, 8 * 128), axis=(0, 2)),
+            jnp.sum(gvec_two[4])[None],
+        ]
+    )
+    small = lax.psum(small, axes) / tokens_all
+    scale = 1.0 / tokens_all
+    sent_a = jnp.concatenate(
+        [gw_qkv.reshape(plan_a.split, -1, 16, 128), gw_out.reshape(devices - plan_a.split, -1, 16, 128)]
+    )
+    sent_f = jnp.concatenate(
+        [gw_up.reshape(plan_f.split, -1, 16, 128), gw_down.reshape(devices - plan_f.split, -1, 16, 128)]
+    )
+    sum_a = lax.psum_scatter(sent_a, axes, scatter_dimension=0, tiled=False)
+    sum_f = lax.psum_scatter(sent_f, axes, scatter_dimension=0, tiled=False)
+    flat_a = plan_a.from_tiles(sum_a.astype(F32) * scale, s)
+    flat_f = plan_f.from_tiles(sum_f.astype(F32) * scale, s)
+    before, after = neighbour_edges([flat_a, flat_f], devices)
+    at = 0
+    parts = []
+    for plan in (plan_a, plan_f):
+        for _, size in plan.vectors:
+            parts.append(small[at : at + size])
+            at = at + size
+    attention_share = plan_a.shard(flat_a, before[0], after[0], parts[:3], s)
+    feedforward_share = plan_f.shard(flat_f, before[1], after[1], parts[3:], s)
+    mixing_grad = small[at:]
+
+    count_now = step_count[0]
+    attention_places = s * plan_a.own + jnp.arange(plan_a.own, dtype=jnp.int32)
+    feedforward_places = s * plan_f.own + jnp.arange(plan_f.own, dtype=jnp.int32)
+    attention_step = adam_update(
+        attention_params, attention_share, attention_first, attention_second, count_now,
+        decay_mask(attention_places, attention_shapes()),
+    )
+    feedforward_step = adam_update(
+        feedforward_params, feedforward_share, feedforward_first, feedforward_second, count_now,
+        decay_mask(feedforward_places, feedforward_shapes()),
+    )
+    mixing_step = adam_update(
+        mixing_offsets, mixing_grad, mixing_first, mixing_second, count_now, 0.0
+    )
+    return (
+        mixed.astype(BF),
+        grad_inputs,
+        grad_history.reshape(history.shape),
+        *attention_step,
+        *feedforward_step,
+        *mixing_step,
+    )
+
+
+def shards(inputs, *others):
+    row_count, span, width = inputs.shape
+    tok_size = lax.axis_size("tok")
+    devices = lax.axis_size("dp") * tok_size
+    by_rows = row_count == tok_size and width == D and (span * tok_size) % 256 == 0
+    if by_rows and all(plan.fits for plan in plans(devices)):
+        return row_shards(inputs, *others)
+    return general_shards(inputs, *others)
+
+
 def solution(mesh):
     in_specs = (
         P("dp", "tok", None),

time: 1680 us -> 595 us (0.35); the launches traced: 1650 us -> 590 us
  waiting for transfers between devices: 661 us -> 177 us
  local copies, waits for them, and re-layouts: 475 us -> 51.3 us
  matrix products: 290 us -> 0 us
  Pallas kernels: 0 us -> 215 us
  other arithmetic: 125 us -> 60.5 us
  loops' own time: 21.1 us -> 0 us
    unnamed x4, waiting for transfers between devices: 601 us -> 0.07 us
    dot_general x41 -> x0, matrix products: 290 us -> none  [the longest x1 39.7 us: shards(): jnp.einsum('j,jrtd->rtd', coefficient[:-1], history, preferred_element_ty...]
    unnamed x128 -> x54, local copies, waits for them, and re-layouts: 278 us -> 21.4 us
    pallas_call x0 -> x6, Pallas kernels: none -> 215 us  [the longest x1 71.4 us: middle(): pl.pallas_call(middle_kernel, grid=(steps,), in_specs=[rows, rows, rows,...]
    reduce_scatter x0 -> x2, waiting for transfers between devices: none -> 78.2 us  [the longest x1 78.2 us: row_shards(): sum_f = lax.psum_scatter(sent_f, axes, scatter_dimension=0, tiled=False)]
    all_gather x0 -> x2, waiting for transfers between devices: none -> 71.8 us  [the longest x1 37.2 us: row_shards(): got_f = lax.all_gather(tiles_f, axes, axis=0, tiled=False)]
    reshape x12 -> x9, local copies, waits for them, and re-layouts: 70.7 us -> 8.15 us  [the longest x2 7.74 us: from_row(): values.reshape(1, length, width)]
    all_to_all x5 -> x4, waiting for transfers between devices: 60.3 us -> 24.1 us  [the longest x2 19 us: to_row(): lax.all_to_all(values, 'tok', split_axis=0, concat_axis=1, tiled=True)]
  transfers between devices with their start and end apart: 7 -> 12, of which waited for: 4 -> 8; matrix products, arithmetic and copies ran while one was open for 21% -> 15% of each run, Pallas kernels for 0% -> 14%
where the time goes in v1:
time: 595 us; the launch traced here: 590 us
  Pallas kernels  215 us (36%)
  waiting for transfers between devices  177 us (30%)
  other arithmetic  60.5 us (10%)
  local copies, waits for them, and re-layouts  51.3 us (9%)
  blocking collectives  42.3 us (7%)
  starting transfers between devices  28 us (5%)
  between operations  15.5 us (3%)
    reduce_scatter x1, waiting for transfers between devices, row_shards(): sum_f = lax.psum_scatter(sent_f, axes, scatter_dimension=0, tiled=False)  78.2 us
    pallas_call x1, Pallas kernels, middle(): pl.pallas_call(middle_kernel, grid=(steps,), in_specs=[rows, rows, rows,...  71.4 us
    pallas_call x1, Pallas kernels, history_pass(): pl.pallas_call(history_kernel, grid=(tokens // tile, terms // group), in_...  46.1 us
    psum x1, blocking collectives, row_shards(): small = lax.psum(small, axes) / tokens_all  42.3 us
    all_gather x1, waiting for transfers between devices, row_shards(): got_f = lax.all_gather(tiles_f, axes, axis=0, tiled=False)  37.2 us
    all_gather x1, waiting for transfers between devices, row_shards(): lax.all_gather(jnp.concatenate([tiles_a, extra]), axes, axis=0, tiled=False)  34.6 us
    pallas_call x1, Pallas kernels, row_attend_back(): pl.pallas_call(partial(attend_back_kernel, block_rows, reach), grid=(widt...  34.3 us
    pallas_call x1, Pallas kernels, row_attend(): pl.pallas_call(partial(attend_kernel, block_rows, reach), grid=(pairs,),...  29.5 us
  transfers between devices with their start and end apart: 12, of which 8 were waited for; matrix products, arithmetic and copies ran while one was open for 15% of the time, Pallas kernels for 14%

profile of v1, /device:TPU:0, one launch (start us, length us, event | category | flops | bytes accessed | tf_op | source)
XLA Modules:
  0.0 589.8 jit_solution(4008301909270611164)
XLA Ops:
  8.3 1.1 convert_element_type.90
  10.1 6.0 %collective-permute-start.1 = (bf16[2,2048]{1,0:T(2,128)(2,1)S(1)}, bf16[2,2048]{1,0:T(2,128)(2,1)S(1)}, u32[]{:S(2)}, u32[]{:S(2)}) collective-permute-start(bf16[2,2048]{1,0:T(2,128)(2,1)S(1)} %pad_maximum_fusion.8), channel_id=1, source_target_pairs={{0,31},{1,0},{2,1},{3,2},{4,3},{5,4},{6,5},{7,6},{8,7},{9,8},{10,9... | collective-permute-start | bytes 24584 | tf_op jit(solution)/shard_map/ppermute | solution.py:1088
  16.1 1.2 collective-permute-done
  17.5 1.2 concatenate.27
  19.0 1.9 concatenate.28
  23.0 3.6 all-to-all-start
  27.7 1.0 copy.52.sc_ref
  28.8 19.0 %all-to-all-done = bf16[4,256,768]{2,1,0:T(8,128)(2,1)S(1)} async-done(((bf16[4,256,768]{2,1,0:T(8,128)(2,1)}), bf16[4,256,768]{2,1,0:T(8,128)(2,1)S(1)}, u32[]{:S(2)}, u32[]{:S(2)}) %all-to-all-start) | async-done | bytes 1572896 | tf_op jit(solution)/shard_map/all_to_all | solution.py:1166
  47.8 3.6 all-to-all-start.1
  51.4 3.2 fusion.7
  54.6 34.6 %all-gather.6.cloned.1.call-done = bf16[1248,16,128]{2,1,0:T(8,128)(2,1)} async-done(((bf16[39,16,128]{2,1,0:T(8,128)(2,1)}), bf16[1248,16,128]{2,1,0:T(8,128)(2,1)}) %all-gather.6.cloned.1.call-update) | async-done | bytes 5111824 | tf_op jit(solution)/shard_map/all_gather | solution.py:1141
  89.3 1.2 slice_convert_fusion
  91.4 2.5 slice.186
  93.9 2.8 slice.183
  98.1 8.8 %project.1 = (bf16[1024,768]{1,0:T(8,128)(2,1)}, bf16[1024,768]{1,0:T(8,128)(2,1)}, bf16[1024,768]{1,0:T(8,128)(2,1)}, bf16[1024,768]{1,0:T(8,128)(2,1)}) custom-call(bf16[1024,768]{1,0:T(8,128)(2,1)} %bitcast.92, bf16[24,2,18,16,128]{4,3,2,1,0:T(8,128)(2,1)} %bitcast.90, f32[8,2304]{1,0:T(8,128)} %stack.72.vec_ref, f32[1024,128]{1,0:T(8,128)} %get-tuple-element.106.cos_ref, ...), custom_call_target="tpu_custom_call" | custom-call | tf_op jit(solution)/shard_map/project/pallas_call | solution.py:511
  106.9 29.5 %attend.1 = (bf16[1024,768]{1,0:T(8,128)(2,1)}, f32[6,2,1024]{2,1,0:T(2,128)}) custom-call(bf16[1024,768]{1,0:T(8,128)(2,1)} %get-tuple-element.37.q_ref, bf16[1024,768]{1,0:T(8,128)(2,1)} %get-tuple-element.38.k_ref, bf16[1024,768]{1,0:T(8,128)(2,1)} %get-tuple-element.39.v_ref, s32[1024,1]{1,0:T(8,128)} %copy.52.sc_ref, s32[1,1024]{1,0:T(1,128)} %bitcast.129), custom_call_target="tpu_custom_call" | custom-call | tf_op jit(solution)/shard_map/attend/pallas_call | solution.py:590
  137.1 37.2 %all-gather.4.cloned.1.call-done = bf16[32,72,16,128]{3,2,1,0:T(8,128)(2,1)} async-done(((bf16[1,72,16,128]{3,2,1,0:T(8,128)(2,1)}), bf16[32,72,16,128]{3,2,1,0:T(8,128)(2,1)}) %all-gather.4.cloned.1.call-update) | async-done | bytes 9437200 | tf_op jit(solution)/shard_map/all_gather | solution.py:1142
  174.4 71.4 %middle.1 = (bf16[1024,768]{1,0:T(8,128)(2,1)}, bf16[1024,768]{1,0:T(8,128)(2,1)}, f32[1024,768]{1,0:T(8,128)}, bf16[48,24,16,128]{3,2,1,0:T(8,128)(2,1)}, bf16[...) custom-call(bf16[1024,768]{1,0:T(8,128)(2,1)} %bitcast.93, ...), custom_call_target="tpu_custom_call" | custom-call | tf_op jit(solution)/shard_map/middle/pallas_call | solution.py:803
  245.7 34.3 %attend_back.1 = (bf16[1024,768]{1,0:T(8,128)(2,1)}, bf16[1024,768]{1,0:T(8,128)(2,1)}, bf16[1024,768]{1,0:T(8,128)(2,1)}) custom-call(bf16[1024,768]{1,0:T(8,128)(2,1)} %get-tuple-element.37.q_ref, bf16[1024,768]{1,0:T(8,128)(2,1)} %get-tuple-element.38.k_ref, bf16[1024,768]{1,0:T(8,128)(2,1)} %get-tuple-element.39.v_ref, ...), custom_call_target="tpu_custom_call" | custom-call | tf_op jit(solution)/shard_map/attend_back/pallas_call | solution.py:663
  280.1 25.3 %last.1 = (bf16[1024,768]{1,0:T(8,128)(2,1)}, bf16[48,18,16,128]{3,2,1,0:T(8,128)(2,1)}, f32[8,2304]{1,0:T(8,128)}, f32[8,768]{1,0:T(8,128)}) custom-call(bf16[1024,768]{1,0:T(8,128)(2,1)} %bitcast.94, bf16[1024,768]{1,0:T(8,128)(2,1)} %get-tuple-element.42.n1_ref, f32[1024,768]{1,0:T(8,128)} %get-tuple-element.43.ghid_ref, ...), custom_call_target="tpu_custom_call" | custom-call | tf_op jit(solution)/shard_map/last/pallas_call | solution.py:919
  305.4 4.5 pad_maximum_fusion.1
  310.0 9.5 %pad_maximum_fusion = bf16[32,72,16,128]{3,2,1,0:T(8,128)(2,1)} fusion(bf16[16,72,16,128]{3,2,1,0:T(8,128)(2,1)} %bitcast.108, bf16[16,72,16,128]{3,2,1,0:T(8,128)(2,1)} %bitcast.107), kind=kLoop, calls=%fused_computation | loop fusion | flops 4718592 | bytes 18874368 | tf_op jit(solution)/shard_map/concatenate | solution.py:1219
  319.5 3.9 copy.69
  323.9 11.6 %reduce.32 = bf16[1024,768]{1,0:T(8,128)(2,1)} reduce(bf16[1024,1,768]{2,1,0:T(2,128)(2,1)S(1)} %bitcast.95, bf16[]{:T(256)} %broadcast.274), dimensions={1}, to_apply=%bitcast.83.reduce_sub_computation | reduce | bytes 3145730
  335.5 3.7 reshape.393
  339.2 4.4 all-to-all-start.3
  343.6 3.9 copy.70
  347.4 11.6 %reduce.31 = bf16[1024,768]{1,0:T(8,128)(2,1)} reduce(bf16[1024,1,768]{2,1,0:T(2,128)(2,1)S(1)} %bitcast.96, bf16[]{:T(256)} %broadcast.274), dimensions={1}, to_apply=%bitcast.84.reduce_sub_computation | reduce | bytes 3145730
  359.0 3.7 reshape.391
  362.8 5.1 all-to-all-done.3
  367.9 4.3 all-to-all-start.2
  373.6 46.1 %history.1 = (f32[1024,768]{1,0:T(8,128)}, f32[24,1024,768]{2,1,0:T(8,128)}, f32[8,192,128]{2,1,0:T(8,128)}) custom-call(bf16[24,1024,768]{2,1,0:T(8,128)(2,1)} %bitcast.87, bf16[1024,768]{1,0:T(8,128)(2,1)} %bitcast.100, f32[25]{0:T(128)} %copy-done.17), custom_call_target="tpu_custom_call" | custom-call | tf_op jit(solution)/shard_map/history/pallas_call | solution.py:971
  419.7 1.3 reduce_sum.48
  425.9 42.3 %psum.7 = f32[10009]{0:T(1024)S(1)} all-reduce(f32[10009]{0:T(1024)S(1)} %concatenate.34), channel_id=1, replica_groups=mesh['dp'=8,'tok'=4] {'dp','tok'}, use_global_device_ids=true, to_apply=%region_8.9 | all-reduce | flops 10009 | bytes 80072 | tf_op jit(solution)/shard_map/psum | solution.py:1214
  468.7 3.1 reshape.394
  471.8 1.9 copy.63
  473.7 3.1 reshape.392
  476.7 3.9 convert_multiply_fusion
  480.8 1.7 copy-done.3
  482.5 1.4 add_convert_fusion
  485.2 78.2 %reduce-scatter.5.cloned.1.call-done = bf16[1,72,16,128]{3,2,1,0:T(8,128)(2,1)} async-done(((bf16[32,72,16,128]{3,2,1,0:T(8,128)(2,1)}), bf16[1,72,16,128]{3,2,1,0:T(8,128)(2,1)}) %reduce-scatter.5.cloned.1.call-update) | async-done | bytes 294928 | tf_op jit(solution)/shard_map/reduce_scatter | solution.py:1223
  565.1 5.4 collective-permute-start.3
  570.5 1.3 collective-permute-done.2
  574.5 1.4 slice_dynamic-update-slice_fusion.2
  576.0 1.4 slice_dynamic-update-slice_fusion.1
  577.4 1.4 slice_dynamic-update-slice_fusion.4
  578.8 2.3 multiply_subtract_fusion.1
  581.1 2.0 multiply_subtract_fusion
  (144 shorter events, 20.8 us)
Async XLA Ops:
  7.2 82.1 %all-gather.6.cloned.1.call-start = ((), (), s32[]{:S(2)}) async-start(), calls=%async_computation.9 | async-start | bytes 5271552 | tf_op jit(solution)/shard_map/all_gather | solution.py:1141
  9.5 7.8 %collective-permute-start = (bf16[2,2048]{1,0:T(2,128)(2,1)S(1)}, bf16[2,2048]{1,0:T(2,128)(2,1)S(1)}, u32[]{:S(2)}, u32[]{:S(2)}) collective-permute-start(bf16[2,2048]{1,0:T(2,128)(2,1)S(1)} %pad_maximum_fusion.7), channel_id=1, source_target_pairs={{0,1},{1,2},{2,3},{3,4},{4,5},{5,6},{6,7},{7,8},{8,9},{9,10},{10,1... | collective-permute-start | bytes 24584 | tf_op jit(solution)/shard_map/ppermute | solution.py:1087
  10.1 7.4 %collective-permute-start.1 = (bf16[2,2048]{1,0:T(2,128)(2,1)S(1)}, bf16[2,2048]{1,0:T(2,128)(2,1)S(1)}, u32[]{:S(2)}, u32[]{:S(2)}) collective-permute-start(bf16[2,2048]{1,0:T(2,128)(2,1)S(1)} %pad_maximum_fusion.8), channel_id=1, source_target_pairs={{0,31},{1,0},{2,1},{3,2},{4,3},{5,4},{6,5},{7,6},{8,7},{9,8},{10,9... | collective-permute-start | bytes 24584 | tf_op jit(solution)/shard_map/ppermute | solution.py:1088
  21.7 152.7 %all-gather.4.cloned.1.call-start = ((), (), s32[]{:S(2)}) async-start(), calls=%async_computation.6 | async-start | bytes 9732096 | tf_op jit(solution)/shard_map/all_gather | solution.py:1142
  22.0 4.6 copy-start.14
  22.0 5.2 copy-start.18
  23.0 24.8 %all-to-all-start = ((bf16[4,256,768]{2,1,0:T(8,128)(2,1)}), bf16[4,256,768]{2,1,0:T(8,128)(2,1)S(1)}, u32[]{:S(2)}, u32[]{:S(2)}) async-start(bf16[4,256,768]{2,1,0:T(8,128)(2,1)} %param.14), calls=%async_computation | async-start | bytes 3145728 | tf_op jit(solution)/shard_map/all_to_all | solution.py:1166
  26.6 64.1 %copy-start.17 = (f32[25]{0:T(128)}, f32[25]{0:T(128)S(1)}, u32[]{:S(2)}) copy-start(f32[25]{0:T(128)S(1)} %fusion.17.c_ref) | copy-start | bytes 304
  27.7 63.1 %copy-start.12 = (s32[1024]{0:T(1024)}, s32[1024]{0:T(1024)S(1)}, u32[]{:S(2)}) copy-start(s32[1024]{0:T(1024)S(1)} %fusion.15) | copy-start | bytes 12292
  47.8 43.0 %copy-start = (bf16[4,256,768]{2,1,0:T(8,128)(2,1)}, bf16[4,256,768]{2,1,0:T(8,128)(2,1)S(1)}, u32[]{:S(2)}) copy-start(bf16[4,256,768]{2,1,0:T(8,128)(2,1)S(1)} %all-to-all-done) | copy-start | bytes 4718596
  47.8 89.4 %all-to-all-start.1 = ((bf16[4,256,768]{2,1,0:T(8,128)(2,1)}), bf16[4,256,768]{2,1,0:T(8,128)(2,1)S(1)}, u32[]{:S(2)}, u32[]{:S(2)}) async-start(bf16[4,256,768]{2,1,0:T(8,128)(2,1)} %param.17), calls=%async_computation.1 | async-start | bytes 3145728 | tf_op jit(solution)/shard_map/all_to_all | solution.py:1166
  51.3 432.6 %reduce-scatter.3.cloned.1.call-start = ((), (), s32[]{:S(2)}) async-start(), calls=%async_computation.7 | async-start | bytes 4866048 | tf_op jit(solution)/shard_map/reduce_scatter | solution.py:1222
  89.2 4.6 copy-start.2
  137.1 37.2 %copy-start.1 = (bf16[4,256,768]{2,1,0:T(8,128)(2,1)}, bf16[4,256,768]{2,1,0:T(8,128)(2,1)S(1)}, u32[]{:S(2)}) copy-start(bf16[4,256,768]{2,1,0:T(8,128)(2,1)S(1)} %all-to-all-done.1) | copy-start | bytes 4718596
  280.1 25.3 %copy-start.6 = (bf16[48,6,16,128]{3,2,1,0:T(8,128)(2,1)S(1)}, bf16[48,6,16,128]{3,2,1,0:T(8,128)(2,1)}, u32[]{:S(2)}) copy-start(bf16[48,6,16,128]{3,2,1,0:T(8,128)(2,1)} %get-tuple-element.52) | copy-start | bytes 3538948
  309.9 253.4 %reduce-scatter.5.cloned.1.call-start = ((), (), s32[]{:S(2)}) async-start(), calls=%async_computation.8 | async-start | bytes 9732096 | tf_op jit(solution)/shard_map/reduce_scatter | solution.py:1223
  339.2 28.7 %all-to-all-start.3 = ((bf16[4,2,98304]{2,1,0:T(2,128)(2,1)}), bf16[4,2,98304]{2,1,0:T(2,128)(2,1)}, u32[]{:S(2)}, u32[]{:S(2)}) async-start(bf16[4,2,98304]{2,1,0:T(2,128)(2,1)} %reshape.393), calls=%async_computation.3 | async-start | bytes 3145728 | tf_op jit(solution)/shard_map/all_to_all | solution.py:1171
  367.9 105.8 %all-to-all-start.2 = ((bf16[4,2,98304]{2,1,0:T(2,128)(2,1)}), bf16[4,2,98304]{2,1,0:T(2,128)(2,1)}, u32[]{:S(2)}, u32[]{:S(2)}) async-start(bf16[4,2,98304]{2,1,0:T(2,128)(2,1)} %reshape.391), calls=%async_computation.2 | async-start | bytes 3145728 | tf_op jit(solution)/shard_map/all_to_all | solution.py:1171
  373.6 50.9 %copy-start.13 = (f32[8,768]{1,0:T(8,128)S(1)}, f32[8,768]{1,0:T(8,128)}, u32[]{:S(2)}) copy-start(f32[8,768]{1,0:T(8,128)} %get-tuple-element.57) | copy-start | bytes 73732
  373.6 94.6 %copy-start.15 = (f32[25]{0:T(128)S(1)}, f32[25]{0:T(128)}, u32[]{:S(2)}) copy-start(f32[25]{0:T(128)} %param.26) | copy-start | bytes 304
  373.6 94.5 %copy-start.16 = (f32[25]{0:T(128)S(1)}, f32[25]{0:T(128)}, u32[]{:S(2)}) copy-start(f32[25]{0:T(128)} %param.25) | copy-start | bytes 304
  480.6 1.9 copy-start.3
  564.4 7.5 %copy-start.9 = (f32[157696]{0:T(1024)S(1)}, f32[157696]{0:T(1024)}, u32[]{:S(2)}) copy-start(f32[157696]{0:T(1024)} %constant_dynamic-update-slice_fusion.5) | copy-start | bytes 1892356
  564.6 14.2 %copy-start.5 = (f32[73872]{0:T(1024)S(1)}, f32[73872]{0:T(1024)}, u32[]{:S(2)}) copy-start(f32[73872]{0:T(1024)} %param.18) | copy-start | bytes 886468
  564.6 14.2 %copy-start.10 = (f32[73872]{0:T(1024)S(1)}, f32[73872]{0:T(1024)}, u32[]{:S(2)}) copy-start(f32[73872]{0:T(1024)} %param.20) | copy-start | bytes 886468
  564.9 13.9 %copy-start.11 = (f32[73872]{0:T(1024)S(1)}, f32[73872]{0:T(1024)}, u32[]{:S(2)}) copy-start(f32[73872]{0:T(1024)} %param.19) | copy-start | bytes 886468
  564.9 16.2 %copy-start.4 = (f32[147624]{0:T(1024)S(1)}, f32[147624]{0:T(1024)}, u32[]{:S(2)}) copy-start(f32[147624]{0:T(1024)} %param.21) | copy-start | bytes 1771492
  564.9 16.2 %copy-start.7 = (f32[147624]{0:T(1024)S(1)}, f32[147624]{0:T(1024)}, u32[]{:S(2)}) copy-start(f32[147624]{0:T(1024)} %param.23) | copy-start | bytes 1771492
  564.9 16.1 %copy-start.8 = (f32[147624]{0:T(1024)S(1)}, f32[147624]{0:T(1024)}, u32[]{:S(2)}) copy-start(f32[147624]{0:T(1024)} %param.22) | copy-start | bytes 1771492
  565.0 6.8 %collective-permute-start.2 = (f32[2,2048]{1,0:T(2,128)S(1)}, f32[2,2048]{1,0:T(2,128)S(1)}, u32[]{:S(2)}, u32[]{:S(2)}) collective-permute-start(f32[2,2048]{1,0:T(2,128)S(1)} %pad_maximum_fusion.4), channel_id=1, source_target_pairs={{0,1},{1,2},{2,3},{3,4},{4,5},{5,6},{6,7},{7,8},{8,9},{9,10},{10,1... | collective-permute-start | bytes 49160 | tf_op jit(solution)/shard_map/ppermute | solution.py:1087
  565.1 8.1 %collective-permute-start.3 = (f32[2,2048]{1,0:T(2,128)S(1)}, f32[2,2048]{1,0:T(2,128)S(1)}, u32[]{:S(2)}, u32[]{:S(2)}) collective-permute-start(f32[2,2048]{1,0:T(2,128)S(1)} %pad_maximum_fusion.5), channel_id=1, source_target_pairs={{0,31},{1,0},{2,1},{3,2},{4,3},{5,4},{6,5},{7,6},{8,7},{9,8},{10,9... | collective-permute-start | bytes 49160 | tf_op jit(solution)/shard_map/ppermute | solution.py:1088
Sparse Core Ops, SparseCore 0:
  21.8 67.3 all-gather.5
  92.7 81.5 all-gather.3
  310.0 111.7 reduce-scatter.2
  428.6 134.7 reduce-scatter.4

commit v2 on v1

--- a/solution.py
+++ b/solution.py
@@ -503,8 +503,11 @@
 
 def project(x_row, w_qkv, vectors, cosine, sine):
     length, width = x_row.shape
+    array, lead = w_qkv
     tile = 256
-    whole = pl.BlockSpec(w_qkv.shape, lambda i: (0,) * w_qkv.ndim)
+    whole = pl.BlockSpec(
+        (lead,) + array.shape[1:], lambda i: (0,) * array.ndim, pipeline_mode=pl.Buffered(1)
+    )
     rows = pl.BlockSpec((tile, width), lambda i: (i, 0))
     trig = pl.BlockSpec((tile, 128), lambda i: (i, 0))
     out = jax.ShapeDtypeStruct((length, width), BF)
@@ -516,7 +519,7 @@
         out_shape=[out] * 4,
         compiler_params=pltpu.CompilerParams(vmem_limit_bytes=VMEM_LIMIT),
         name="project",
-    )(x_row, w_qkv, vectors, cosine, sine)
+    )(x_row, array, vectors, cosine, sine)
 
 
 def key_range(block, block_rows, reach):
@@ -683,8 +686,8 @@
 
 
 def middle_kernel(
-    x_ref, att_ref, cot_ref, wout_ref, wup_ref, wdown_ref, vec_ref, bup_ref, c_ref,
-    bout_ref, gatt_ref, ghid_ref, gwup_ref, gwdown_ref, gwout_ref, gbup_ref, gvec_ref,
+    x_ref, att_ref, cot_ref, wout_ref, wup_ref, wdown_ref, vec_ref, bup_ref, own_cot_ref, c_ref,
+    ghist_ref, bout_ref, gatt_ref, ghid_ref, gwup_ref, gwdown_ref, gwout_ref, gbup_ref, gvec_ref,
     hidden_ref, n2_ref, n2t_ref, gb_ref, acc_out, acc_gn, act_ref, gup_ref,
 ):
     step = pl.program_id(0)
@@ -692,7 +695,8 @@
     length, width = x_ref.shape
     tile = 256
     tiles = length // tile
-    mix = c_ref[0]
+    mix = c_ref[c_ref.shape[0] - 1]
+    group = ghist_ref.shape[0]
 
     @pl.when(step == 0)
     def _():
@@ -734,6 +738,9 @@
         gup_ref[rows, :] = grad_up
         acc_gn[rows, :] += nt_dot(grad_up, w_up)
         gbup_ref[0:1, :] += jnp.sum(grad_up.astype(F32), axis=0, keepdims=True)
+        own_cot = own_cot_ref[rows, :].astype(F32)
+        for j in range(group):
+            ghist_ref[j, rows, :] = c_ref[step * group + j] * own_cot
 
     grad_up_all = gup_ref[...]
     for r in range(width // 256):
@@ -788,11 +795,13 @@
                 )
 
 
-def middle(x_row, attended, cot_row, w_out, w_up, w_down, vectors, b_up, mix):
+def middle(x_row, attended, cot_row, w_out, w_up, w_down, vectors, b_up, own_cot, coefficient):
     length, width = x_row.shape
-    (up_array, up_rows), (down_array, down_first) = w_up, w_down
+    (up_array, up_rows), (down_array, down_first), (out_array, out_rows) = w_up, w_down, w_out
+    out_first = out_array.shape[0] // out_rows - 1
     inner = b_up.shape[1]
     steps = inner // 256
+    terms = coefficient.shape[0] - 1
     once = pl.Buffered(1)
 
     def const(shape):
@@ -804,14 +813,19 @@
         middle_kernel,
         grid=(steps,),
         in_specs=[
-            rows, rows, rows, const(w_out.shape),
+            rows, rows, rows,
+            pl.BlockSpec(
+                (out_rows,) + out_array.shape[1:], lambda i: (out_first, 0, 0, 0, 0), pipeline_mode=once
+            ),
             pl.BlockSpec((up_rows, up_array.shape[1], 2, 16, 128), lambda i: (0, 0, i, 0, 0)),
             pl.BlockSpec((16, col_tiles, 16, 128), lambda i: (i + down_first, 0, 0, 0)),
             const(vectors.shape),
             pl.BlockSpec((1, 256), lambda i: (0, i)),
+            const(own_cot.shape),
             pl.BlockSpec(memory_space=pltpu.SMEM),
         ],
         out_specs=[
+            pl.BlockSpec((terms // steps,) + own_cot.shape, lambda i: (i, 0, 0)),
             rows, rows, rows,
             pl.BlockSpec((row_tiles, 2, 16, 128), lambda i: (0, i, 0, 0)),
             pl.BlockSpec((16, col_tiles, 16, 128), lambda i: (i, 0, 0, 0)),
@@ -820,6 +834,7 @@
             const((8, width)),
         ],
         out_shape=[
+            jax.ShapeDtypeStruct((terms,) + own_cot.shape, F32),
             jax.ShapeDtypeStruct((length, width), BF),
             jax.ShapeDtypeStruct((length, width), BF),
             jax.ShapeDtypeStruct((length, width), F32),
@@ -841,7 +856,7 @@
         ],
         compiler_params=pltpu.CompilerParams(vmem_limit_bytes=VMEM_LIMIT),
         name="middle",
-    )(x_row, attended, cot_row, w_out, up_array, down_array, vectors, b_up, mix)
+    )(x_row, attended, cot_row, out_array, up_array, down_array, vectors, b_up, own_cot, coefficient)
 
 
 def last_kernel(
@@ -942,53 +957,508 @@
     )(x_row, n1, grad_hidden, gq, gk, gv, array, vectors)
 
 
-def history_kernel(hist_ref, cot_ref, c_ref, part_ref, grad_ref, dots_ref):
-    group = hist_ref.shape[0]
-    first = pl.program_id(1) * group
-    cot = cot_ref[...].astype(F32)
-    rows, width = cot.shape
+def history_step(hist_ref, cot_ref, c_ref, first_term, part_ref, dots_ref):
+    group, tile, width = hist_ref.shape
+    mixes = [c_ref[first_term + j] for j in range(group)]
+
+    def chunk(r, dots):
+        rows = pl.ds(pl.multiple_of(r * 16, 16), 16)
+        total = part_ref[rows, :]
+        cot = cot_ref[rows, :].astype(F32)
+        new = []
+        for j in range(group):
+            past = hist_ref[j, rows, :].astype(F32)
+            total = total + mixes[j] * past
+            both = past * cot
+            both = both[:8] + both[8:]
+            added = dots[j]
+            for k in range(width // 128):
+                added = added + both[:, 128 * k : 128 * k + 128]
+            new.append(added)
+        part_ref[rows, :] = total
+        return tuple(new)
+
+    dots = lax.fori_loop(0, tile // 16, chunk, tuple(jnp.zeros((8, 128), F32) for _ in range(group)))
+    for j in range(group):
+        dots_ref[0, 8 * j : 8 * j + 8, :] = dots[j]
+
+
+MESH_ID = pl.DeviceIdType.MESH
+
+
+class Place:
+    def __init__(self, depth):
+        dp, tok = lax.axis_index("dp"), lax.axis_index("tok")
+        self.depth = depth
+        self.z, self.x, self.y, self.c = dp // 2, dp % 2, tok // 2, tok % 2
+        self.dp, self.tok = dp, tok
+        self.along_x = (self.z * 2 + 1 - self.x, tok)
+        self.along_y = (dp, (1 - self.y) * 2 + self.c)
+        self.along_c = (dp, self.y * 2 + 1 - self.c)
+        self.near_z = ((self.z + 1 - 2 * (self.z % 2)) * 2 + self.x, tok)
+        self.mid_z = ((depth - 1 - self.z) * 2 + self.x, tok)
+        self.across = (dp, (1 - self.y) * 2 + 1 - self.c)
+
+    def along_z(self, step):
+        return (lax.rem(self.z + step, self.depth) * 2 + self.x, self.tok)
+
+    def partners(self):
+        steps = [self.along_z(r) for r in range(1, self.depth)]
+        return [self.along_x, self.along_y, self.along_c, self.across] + steps
+
+    def row_partners(self):
+        return [self.along_c, self.along_y, self.across]
+
+
+def greet(place):
+    barrier = pltpu.get_barrier_semaphore()
+    for partner in place.partners():
+        pl.semaphore_signal(barrier, inc=1, device_id=partner, device_id_type=MESH_ID)
+    pl.semaphore_wait(barrier, len(place.partners()))
+
+
+def remote(src, dst, send, recv, target):
+    return pltpu.make_async_remote_copy(
+        src_ref=src, dst_ref=dst, send_sem=send, recv_sem=recv,
+        device_id=target, device_id_type=MESH_ID,
+    )
+
+
+def gather_kernel(
+    depth, items, spread, ahead, second_rows, hist_ref, cot_ref, c_ref, *refs,
+):
+    arrays = 1 + max(item[0] for item in items)
+    blocks = refs[:arrays]
+    rows_in = refs[arrays : arrays + 2]
+    part_ref, dots_ref = refs[arrays + 2 : arrays + 4]
+    gathered = refs[arrays + 4 : 2 * arrays + 4]
+    rows_out = refs[2 * arrays + 4 : 2 * arrays + 6]
+    z_send, z_recv, m_send, m_recv, c_send, c_recv, r_send, r_recv, local = refs[2 * arrays + 6 :]
+    step = pl.program_id(0) * pl.num_programs(1) + pl.program_id(1)
+    me = Place(depth)
+    own = (me.z, me.x, me.y, me.c)
+    span = rows_in[0].shape[1]
+
+    inner = (me.z == 1) | (me.z == 2)
+    half = me.z // 2
+
+    def z_copy(i, hop):
+        which, low, _, high = items[i]
+        spot = pl.ds(low, high - low)
+        sems = (z_send.at[i, hop], z_recv.at[i, hop])
+        if hop == 0:
+            return remote(blocks[which].at[spot], gathered[which].at[own + (spot,)], *sems, me.near_z)
+        first_block = 2 * half if hop == 1 else 2 * (1 - half)
+        view = gathered[which].at[pl.ds(first_block, 2), me.x, me.y, me.c, spot]
+        return remote(view, view, *sems, me.mid_z if hop == 1 else me.near_z)
+
+    def middle_copy(i, stage, part):
+        which, low, mid, high = items[i]
+        spot = pl.ds(low, mid - low) if part == 0 else pl.ds(mid, high - mid)
+        every = slice(None)
+        if stage == 0:
+            index = (every, me.x, me.y, me.c, spot)
+        elif part == 0:
+            index = (every, every, me.y, me.c, spot)
+        else:
+            index = (every, me.x, every, me.c, spot)
+        target = me.along_x if stage == part else me.along_y
+        view = gathered[which].at[index]
+        at = 2 * stage + part
+        return remote(view, view, m_send.at[i, at], m_recv.at[i, at], target)
+
+    def core_copy(i):
+        which, low, _, high = items[i]
+        every = slice(None)
+        view = gathered[which].at[every, every, every, me.c, pl.ds(low, high - low)]
+        return remote(view, view, c_send.at[i], c_recv.at[i], me.along_c)
+
+    def row_copy(k, p):
+        target = me.row_partners()[p]
+        return remote(
+            rows_in[k].at[target[1]], rows_out[k].at[pl.ds(me.tok * span, span)],
+            r_send.at[k, p], r_recv.at[k, p], target,
+        )
+
+    def row_own(k):
+        return pltpu.make_async_copy(
+            rows_in[k].at[me.tok], rows_out[k].at[pl.ds(me.tok * span, span)], local.at[k]
+        )
+
+    def block_own(which):
+        return pltpu.make_async_copy(blocks[which], gathered[which].at[own], local.at[2 + which])
+
+    def parts(i):
+        _, low, mid, high = items[i]
+        return [part for part, size in ((0, mid - low), (1, high - mid)) if size]
+
+    def begin():
+        greet(me)
+        for which in range(arrays):
+            block_own(which).start()
+        for i in range(min(ahead, len(items))):
+            line(i)
+        for k in range(2):
+            row_own(k).start()
+        rows(0)
+
+    def line(i):
+        z_copy(i, 0).start()
+
+    def inner_hop(i):
+        if i == 0:
+            for which in range(arrays):
+                block_own(which).wait()
+        z_copy(i, 0).wait_recv()
+        pl.when(inner)(lambda: z_copy(i, 1).start())
+
+    def outer_hop(i):
+        @pl.when(inner)
+        def _():
+            z_copy(i, 1).wait_recv()
+            z_copy(i, 2).start()
+
+    def rows(k):
+        for p in range(3):
+            row_copy(k, p).start()
+
+    def first(i):
+        if i + ahead < len(items):
+            line(i + ahead)
+        if i == second_rows:
+            rows(1)
+        pl.when(jnp.logical_not(inner))(lambda: z_copy(i, 2).wait_recv())
+        for part in parts(i):
+            middle_copy(i, 0, part).start()
+
+    def second(i):
+        for part in parts(i):
+            middle_copy(i, 0, part).wait_recv()
+            middle_copy(i, 1, part).start()
+
+    def third(i):
+        for part in parts(i):
+            middle_copy(i, 1, part).wait_recv()
+        core_copy(i).start()
+
+    def finish():
+        for i in range(len(items)):
+            core_copy(i).wait_recv()
+        for k in range(2):
+            row_own(k).wait()
+            for p in range(3):
+                row_copy(k, p).wait()
+        for i in range(len(items)):
+            z_copy(i, 0).wait_send()
+
+            @pl.when(inner)
+            def _():
+                z_copy(i, 1).wait_send()
+                z_copy(i, 2).wait_send()
+
+            for part in parts(i):
+                middle_copy(i, 0, part).wait_send()
+                middle_copy(i, 1, part).wait_send()
+            core_copy(i).wait_send()
+
+    stages = (inner_hop, outer_hop, first, second, third)
+    work = []
+    for i in range(len(items) + len(stages) - 1):
+        for at, stage in enumerate(stages):
+            if 0 <= i - at < len(items):
+                work.append(partial(stage, i - at))
+    work.append(finish)
+    pl.when(step == 0)(begin)
 
     @pl.when(pl.program_id(1) == 0)
     def _():
         part_ref[...] = jnp.zeros_like(part_ref)
 
-    total = part_ref[...]
-    for j in range(group):
-        mix = c_ref[first + j]
-        past = hist_ref[j].astype(F32)
-        total = total + mix * past
-        grad_ref[j] = mix * cot
-        dots = jnp.sum((past * cot).reshape(rows // 8, 8, width), axis=0)
-        dots_ref[0, 8 * j : 8 * j + 8, :] = sum(
-            dots[:, 128 * k : 128 * k + 128] for k in range(width // 128)
-        )
-    part_ref[...] = total
-
-
-def history_pass(history, cotangent, coefficient):
+    group = hist_ref.shape[0]
+    history_step(hist_ref, cot_ref, c_ref, pl.program_id(1) * group, part_ref, dots_ref)
+    for at, one in enumerate(work):
+        pl.when(step == spread[at])(one)
+
+
+def gather(blocks, items, inputs, history, cotangent, coefficient, depth, ahead, second_rows):
     terms, tokens, width = history.shape
+    row_count, span, _ = inputs.shape
+    length = span * row_count
     tile, group = 128, 6
+    steps = (tokens // tile) * (terms // group)
+    work = 5 * len(items) + 1
+    spread = [min(steps - 1, 1 + at * 1) for at in range(work)]
+    spread[-1] = steps - 1
+    n, arrays = len(items), len(blocks)
+    hbm = pl.BlockSpec(memory_space=pl.ANY)
+    dma = pltpu.SemaphoreType.DMA
     return pl.pallas_call(
-        history_kernel,
+        partial(gather_kernel, depth, items, spread, ahead, second_rows),
         grid=(tokens // tile, terms // group),
         in_specs=[
             pl.BlockSpec((group, tile, width), lambda t, j: (j, t, 0)),
             pl.BlockSpec((tile, width), lambda t, j: (t, 0)),
             pl.BlockSpec(memory_space=pltpu.SMEM),
-        ],
+        ]
+        + [hbm] * (arrays + 2),
         out_specs=[
             pl.BlockSpec((tile, width), lambda t, j: (t, 0)),
-            pl.BlockSpec((group, tile, width), lambda t, j: (j, t, 0)),
             pl.BlockSpec((1, 8 * group, 128), lambda t, j: (t, j, 0)),
-        ],
+        ]
+        + [hbm] * (arrays + 2),
         out_shape=[
             jax.ShapeDtypeStruct((tokens, width), F32),
-            jax.ShapeDtypeStruct((terms, tokens, width), F32),
             jax.ShapeDtypeStruct((tokens // tile, 8 * terms, 128), F32),
+        ]
+        + [jax.ShapeDtypeStruct((depth, 2, 2, 2) + b.shape, b.dtype) for b in blocks]
+        + [jax.ShapeDtypeStruct((length, width), BF)] * 2,
+        scratch_shapes=[
+            dma((n, 3)), dma((n, 3)), dma((n, 4)), dma((n, 4)),
+            dma((n,)), dma((n,)), dma((2, 3)), dma((2, 3)), dma((2 + arrays,)),
         ],
-        compiler_params=pltpu.CompilerParams(vmem_limit_bytes=VMEM_LIMIT),
-        name="history",
-    )(history, cotangent, coefficient)
+        compiler_params=pltpu.CompilerParams(
+            vmem_limit_bytes=VMEM_LIMIT, collective_id=0, has_side_effects=True
+        ),
+        name="gather",
+    )(history, cotangent.reshape(tokens, width), coefficient, *blocks, inputs, cotangent)
+
+
+def finish_kernel(
+    depth, sources, items, mid, small_ref, *refs,
+):
+    grads = refs[: len(sources)]
+    rows_in = refs[len(sources) : len(sources) + 2]
+    refs = refs[len(sources) + 2 :]
+    out_ref, small_out, back_0, back_1 = refs[:4]
+    rows_out = (back_0, back_1)
+    (
+        own_buf, core_buf, s1a, s1b, r1a, r1b, s2a, s2b, r2a, r2b, s3, r3,
+        v_buf, v_recv, v_line,
+        c_send, c_recv, m_send, m_recv, z_send, z_recv, r_send, r_recv, v_send, v_sem, local,
+    ) = refs[4:]
+    me = Place(depth)
+    span = rows_out[0].shape[1]
+    sends1, recvs1, sends2, recvs2 = (s1a, s1b), (r1a, r1b), (s2a, s2b), (r2a, r2b)
+    width = items[0][2]
+    tiles = (slice(0, mid), slice(mid, width))
+    first_bit, second_bit = (me.y, me.x), (me.x, me.y)
+    first_way, second_way = (me.along_y, me.along_x), (me.along_x, me.along_y)
+
+    def pieces(i):
+        group, low, count = items[i]
+        at = 0
+        for which, (of, lead) in enumerate(sources):
+            if of == group:
+                yield which, at, lead, pl.ds(low, count)
+                at = at + lead
+
+    def core_copies(i):
+        for n, (which, at, lead, spot) in enumerate(pieces(i)):
+            yield remote(
+                grads[which].at[:, 1 - me.c, spot], core_buf.at[i, pl.ds(at, lead)],
+                c_send.at[i, n], c_recv.at[i, n], me.along_c,
+            )
+
+    def own_copies(i):
+        for n, (which, at, lead, spot) in enumerate(pieces(i)):
+            yield pltpu.make_async_copy(
+                grads[which].at[:, me.c, spot], own_buf.at[i, pl.ds(at, lead)], local.at[i, n]
+            )
+
+    def side_copy(i, part, stage):
+        send, recv = (sends1, recvs1) if stage == 0 else (sends2, recvs2)
+        way = (first_way, second_way)[stage][part]
+        at = 2 * stage + part
+        return remote(send[part].at[i], recv[part].at[i], m_send.at[i, at], m_recv.at[i, at], way)
+
+    def line_copy(i, r):
+        return remote(
+            s3.at[i, r - 1], r3.at[i, r - 1], z_send.at[i, r - 1], z_recv.at[i, r - 1], me.along_z(r)
+        )
+
+    def row_copy(k, p):
+        target = me.row_partners()[p]
+        return remote(
+            rows_in[k].at[pl.ds(target[1] * span, span)], rows_out[k].at[me.tok],
+            r_send.at[k, p], r_recv.at[k, p], target,
+        )
+
+    def row_own(k):
+        return pltpu.make_async_copy(
+            rows_in[k].at[pl.ds(me.tok * span, span)], rows_out[k].at[me.tok], local.at[k, 2]
+        )
+
+    ways = (me.along_c, me.along_y, me.along_x)
+
+    def small_copy(n):
+        return remote(v_buf.at[n], v_recv.at[n], v_send.at[n], v_sem.at[n], ways[n])
+
+    def small_line(r):
+        return remote(
+            v_buf.at[3], v_line.at[me.z], v_send.at[2 + r], v_sem.at[2 + r], me.along_z(r)
+        )
+
+    def begin():
+        greet(me)
+        v_buf[0] = small_ref[...]
+        small_copy(0).start()
+        for i in range(len(items)):
+            for copy in core_copies(i):
+                copy.start()
+            for copy in own_copies(i):
+                copy.start()
+        for k in range(2):
+            row_own(k).start()
+        for p in range(3):
+            row_copy(0, p).start()
+
+    def core_stage(i):
+        for copy in core_copies(i):
+            copy.wait_recv()
+        for copy in own_copies(i):
+            copy.wait()
+
+        for part in range(2):
+
+            def one(j, _, part=part):
+                slot = first_slot(part, j, 1 - first_bit[part])
+                sends1[part][i, j] = pair_sum(i, part, slot).astype(BF)
+                return 0
+
+            lax.fori_loop(0, 2 * depth, one, 0)
+            side_copy(i, part, 0).start()
+
+    def first_slot(part, j, bit):
+        return 2 * j + bit if part == 0 else (j // 2) * 4 + 2 * bit + j % 2
+
+    def pair_sum(i, part, slot):
+        spot = tiles[part]
+        return own_buf[i, slot, spot].astype(F32) + core_buf[i, slot, spot].astype(F32)
+
+    def plane_sum(i, part, j):
+        slot = first_slot(part, j, first_bit[part])
+        return pair_sum(i, part, slot) + recvs1[part][i, j].astype(F32)
+
+    def first_stage(i):
+        for part in range(2):
+            side_copy(i, part, 0).wait_recv()
+
+            def one(k, _, part=part):
+                sends2[part][i, k] = plane_sum(i, part, 2 * k + 1 - second_bit[part]).astype(BF)
+                return 0
+
+            lax.fori_loop(0, depth, one, 0)
+            side_copy(i, part, 1).start()
+
+    def chip_sum(i, part, k):
+        return plane_sum(i, part, 2 * k + second_bit[part]) + recvs2[part][i, k].astype(F32)
+
+    def second_stage(i):
+        for part in range(2):
+            side_copy(i, part, 1).wait_recv()
+        for r in range(1, depth):
+            other = lax.rem(me.z + r, depth)
+            for part in range(2):
+                s3[i, r - 1, tiles[part]] = chip_sum(i, part, other).astype(BF)
+            line_copy(i, r).start()
+
+    def line_stage(i):
+        for r in range(1, depth):
+            line_copy(i, r).wait_recv()
+        for part in range(2):
+            total = chip_sum(i, part, me.z)
+            for r in range(1, depth):
+                total = total + r3[i, r - 1, tiles[part]].astype(F32)
+            out_ref[i, tiles[part]] = total
+
+    def small_stage(n):
+        if n < 3:
+            small_copy(n).wait_recv()
+            v_buf[n + 1] = v_buf[n] + v_recv[n]
+            if n < 2:
+                small_copy(n + 1).start()
+            else:
+                v_line[me.z] = v_buf[3]
+                for r in range(1, depth):
+                    small_line(r).start()
+            if n == 0:
+                for p in range(3):
+                    row_copy(1, p).start()
+        else:
+            for r in range(1, depth):
+                small_line(r).wait_recv()
+            total = v_line[0]
+            for z in range(1, depth):
+                total = total + v_line[z]
+            small_out[...] = total
+
+    def last_stage():
+        for k in range(2):
+            row_own(k).wait()
+            for p in range(3):
+                row_copy(k, p).wait()
+        for n in range(3):
+            small_copy(n).wait_send()
+        for r in range(1, depth):
+            small_line(r).wait_send()
+        for i in range(len(items)):
+            for copy in core_copies(i):
+                copy.wait_send()
+            for part in range(2):
+                side_copy(i, part, 0).wait_send()
+                side_copy(i, part, 1).wait_send()
+            for r in range(1, depth):
+                line_copy(i, r).wait_send()
+
+    begin()
+    stages = (core_stage, first_stage, second_stage, line_stage)
+    for i in range(max(len(items) + len(stages) - 1, 4)):
+        for at, stage in enumerate(stages):
+            if 0 <= i - at < len(items):
+                stage(i - at)
+        if i < 4:
+            small_stage(i)
+    last_stage()
+
+
+def finish(sources, items, mid, rows, small, row_count, depth):
+    length, width = rows[0].shape
+    span = length // row_count
+    n = len(items)
+    count = items[0][2]
+    hbm = pl.BlockSpec(memory_space=pl.ANY)
+    vmem = pl.BlockSpec(memory_space=pltpu.VMEM)
+    dma = pltpu.SemaphoreType.DMA
+
+    def tiles(lead, size):
+        return pltpu.VMEM((n, lead, size, 16, 128), BF)
+
+    sizes = (mid, count - mid)
+    scratch = [tiles(4 * depth, count), tiles(4 * depth, count)]
+    for lead in (2 * depth, depth):
+        scratch += [tiles(lead, size) for size in sizes] * 2
+    scratch += [tiles(depth - 1, count), tiles(depth - 1, count)]
+    scratch += [pltpu.VMEM((4,) + small.shape, F32), pltpu.VMEM((3,) + small.shape, F32)]
+    scratch += [pltpu.VMEM((depth,) + small.shape, F32)]
+    scratch += [
+        dma((n, 2)), dma((n, 2)), dma((n, 4)), dma((n, 4)), dma((n, depth - 1)), dma((n, depth - 1)),
+        dma((2, 3)), dma((2, 3)), dma((2 + depth,)), dma((2 + depth,)), dma((n, 3)),
+    ]
+    return pl.pallas_call(
+        partial(finish_kernel, depth, [(g, a.shape[0]) for g, a in sources], items, mid),
+        in_specs=[vmem] + [hbm] * (len(sources) + 2),
+        out_specs=[vmem, vmem, hbm, hbm],
+        out_shape=[
+            jax.ShapeDtypeStruct((n, count, 16, 128), F32),
+            jax.ShapeDtypeStruct(small.shape, F32),
+        ]
+        + [jax.ShapeDtypeStruct((row_count, span, width), r.dtype) for r in rows],
+        scratch_shapes=scratch,
+        compiler_params=pltpu.CompilerParams(
+            vmem_limit_bytes=VMEM_LIMIT, collective_id=1, has_side_effects=True
+        ),
+        name="finish",
+    )(small, *[a for _, a in sources], *rows)
 
 
 HALO = 2048
@@ -1132,15 +1602,28 @@
     plan_a, plan_f = plans(devices)
     reach = length // 2
 
+    depth = lax.axis_size("dp") // 2
+    tokens = row_count * span
+    term_count = mixing_offsets.shape[0]
+    coefficient = mixing_offsets + (jnp.arange(term_count) == term_count - 1).astype(F32)
+
     low_a, low_f = attention_params.astype(BF), feedforward_params.astype(BF)
     before, after = neighbour_edges([low_a, low_f], devices)
     tiles_a, extra_a = plan_a.blocks(low_a, before[0], after[0], s)
     tiles_f, extra_f = plan_f.blocks(low_f, before[1], after[1], s)
     extra = jnp.concatenate([extra_a, extra_f]).reshape(-1, 16, 128)
     count_a, count_f = tiles_a.shape[0], tiles_f.shape[0]
-    got_a = lax.all_gather(jnp.concatenate([tiles_a, extra]), axes, axis=0, tiled=False)
     got_f = lax.all_gather(tiles_f, axes, axis=0, tiled=False)
-    extras = got_a[:, count_a:].reshape(devices, -1).astype(F32)
+    part = count_a // 3
+    items = [(1, 0, extra.shape[0], extra.shape[0])] + [
+        (0, low, low + part // 4, low + part) for low in range(0, count_a, part)
+    ]
+    history_part, history_dots, got_a, got_e, x_row, cot_row = gather(
+        [tiles_a, extra], items, inputs, history.reshape(term_count - 1, tokens, width), cotangent,
+        coefficient, depth, 4, 1,
+    )
+    got_a = got_a.reshape(devices, count_a, 16, 128)
+    extras = got_e.reshape(devices, -1).astype(F32)
     room_a = plan_a.vector_rows() * 128
 
     def pick(plan, which, at):
@@ -1152,9 +1635,9 @@
     b_up, b_down = pick(plan_f, 1, room_a), pick(plan_f, 2, room_a)
     (rq, cq), (ro, co) = plan_a.tile_shapes()
     (ru, cu), (rd, cd) = plan_f.tile_shapes()
-    w_qkv = got_a[: plan_a.split, :count_a].reshape(plan_a.split, rq, cq, 16, 128)
-    w_out = got_a[plan_a.split :, :count_a].reshape(devices - plan_a.split, ro, co, 16, 128)
-    w_up = (got_f.reshape(devices * ru * cu // (ru * cu), ru, cu, 16, 128), plan_f.split)
+    w_qkv = (got_a.reshape(devices, rq, cq, 16, 128), plan_a.split)
+    w_out = (got_a.reshape(devices, ro, co, 16, 128), devices - plan_a.split)
+    w_up = (got_f.reshape(devices, ru, cu, 16, 128), plan_f.split)
     w_down = (got_f.reshape(devices * rd, cd, 16, 128), plan_f.split * rd // 16)
 
     def stack(vectors, wide):
@@ -1162,47 +1645,25 @@
         vectors = vectors + [jnp.zeros((wide,), F32)] * (8 - len(vectors))
         return jnp.stack(vectors)
 
-    def to_row(values):
-        return lax.all_to_all(values, "tok", split_axis=0, concat_axis=1, tiled=True).reshape(
-            length, width
-        )
-
-    def from_row(values):
-        return lax.all_to_all(
-            values.reshape(1, length, width), "tok", split_axis=1, concat_axis=0, tiled=True
-        )
-
-    x_row, cot_row = to_row(inputs), to_row(cotangent)
     own_lengths = lax.dynamic_index_in_dim(document_lengths, lax.axis_index("tok"), 0, False)
     segment, cosine, sine = row_tables(own_lengths, length)
     seg_col, seg_row = segment[:, None], segment[None, :]
 
-    term_count = mixing_offsets.shape[0]
-    coefficient = mixing_offsets + (jnp.arange(term_count) == term_count - 1).astype(F32)
-    tokens = row_count * span
-    history_part, grad_history, history_dots = history_pass(
-        history.reshape(term_count - 1, tokens, width), cotangent.reshape(tokens, width), coefficient
-    )
-
     normed_one, queries, keys, values = project(
         x_row, w_qkv, stack([gain_one, shift_one, b_qkv], 3 * width), cosine, sine
     )
     attended, lse = row_attend(queries, keys, values, seg_col, seg_row, reach)
-    block_out, grad_attended, grad_hidden, gw_up, gw_down, gw_out, gb_up, gvec_two = middle(
+    grad_history, block_out, grad_attended, grad_hidden, gw_up, gw_down, gw_out, gb_up, gvec_two = middle(
         x_row, attended, cot_row, w_out, w_up, w_down,
-        stack([gain_two, shift_two, b_out, b_down], width), b_up[None, :], coefficient[-1:],
+        stack([gain_two, shift_two, b_out, b_down], width), b_up[None, :],
+        cotangent.reshape(tokens, width), coefficient,
     )
     gq, gk, gv = row_attend_back(
         queries, keys, values, grad_attended, lse, seg_col, seg_row, cosine, sine, reach
     )
     grad_row, gw_qkv, gb_qkv, gvec_one = last(
-        x_row, normed_one, grad_hidden, gq, gk, gv, (w_qkv, plan_a.split), stack([gain_one], width)
-    )
-    mixed = history_part.reshape(row_count, span, width) + coefficient[-1] * from_row(
-        block_out
-    ).astype(F32)
-    grad_inputs = from_row(grad_row).astype(F32)
-
+        x_row, normed_one, grad_hidden, gq, gk, gv, w_qkv, stack([gain_one], width)
+    )
     small = jnp.concatenate(
         [
             gvec_one[0], gvec_one[1], gb_qkv[0], gvec_two[2],
@@ -1211,18 +1672,29 @@
             jnp.sum(gvec_two[4])[None],
         ]
     )
-    small = lax.psum(small, axes) / tokens_all
+    small_size = small.shape[0]
+    small = jnp.pad(small, (0, -small_size % 1024)).reshape(-1, 128)
     scale = 1.0 / tokens_all
-    sent_a = jnp.concatenate(
-        [gw_qkv.reshape(plan_a.split, -1, 16, 128), gw_out.reshape(devices - plan_a.split, -1, 16, 128)]
-    )
-    sent_f = jnp.concatenate(
-        [gw_up.reshape(plan_f.split, -1, 16, 128), gw_down.reshape(devices - plan_f.split, -1, 16, 128)]
-    )
-    sum_a = lax.psum_scatter(sent_a, axes, scatter_dimension=0, tiled=False)
-    sum_f = lax.psum_scatter(sent_f, axes, scatter_dimension=0, tiled=False)
-    flat_a = plan_a.from_tiles(sum_a.astype(F32) * scale, s)
-    flat_f = plan_f.from_tiles(sum_f.astype(F32) * scale, s)
+    sources = [
+        (group, array.reshape(-1, 2, *shape))
+        for group, array, shape in (
+            (0, gw_qkv, tiles_a.shape), (0, gw_out, tiles_a.shape),
+            (1, gw_up, tiles_f.shape), (1, gw_down, tiles_f.shape),
+        )
+    ]
+    part_f = count_a // 2
+    items = [(1, low, part_f) for low in range(0, count_f, part_f)]
+    items = items + [(0, low, part_f) for low in range(0, count_a, part_f)]
+    sums, small, block_back, grad_back = finish(
+        sources, items, part_f * 5 // 18, [block_out, grad_row], small, row_count, depth
+    )
+    small = small.reshape(-1)[:small_size] / tokens_all
+    sum_f = sums[: count_f // part_f].reshape(tiles_f.shape)
+    sum_a = sums[count_f // part_f :].reshape(tiles_a.shape)
+    mixed = history_part.reshape(row_count, span, width) + coefficient[-1] * block_back.astype(F32)
+    grad_inputs = grad_back.astype(F32)
+    flat_a = plan_a.from_tiles(sum_a * scale, s)
+    flat_f = plan_f.from_tiles(sum_f * scale, s)
     before, after = neighbour_edges([flat_a, flat_f], devices)
     at = 0
     parts = []
@@ -1262,7 +1734,7 @@
     row_count, span, width = inputs.shape
     tok_size = lax.axis_size("tok")
     devices = lax.axis_size("dp") * tok_size
-    by_rows = row_count == tok_size and width == D and (span * tok_size) % 256 == 0
+    by_rows = row_count == tok_size == 4 and lax.axis_size("dp") == 8 and width == D
     if by_rows and all(plan.fits for plan in plans(devices)):
         return row_shards(inputs, *others)
     return general_shards(inputs, *others)

time: 595 us -> 444 us (0.75)
  waiting for transfers between devices: 177 us -> 2.64 us
  Pallas kernels: 215 us -> 369 us
  blocking collectives: 42.3 us -> 0 us
  other arithmetic: 60.5 us -> 23.3 us
  local copies, waits for them, and re-layouts: 51.3 us -> 19.4 us
  starting transfers between devices: 28 us -> 11.9 us
    pallas_call x1 -> x2, Pallas kernels: 46.1 us -> 196 us  [the longest x1 99 us: finish(): pl.pallas_call(partial(finish_kernel, depth, [(g, a.shape[0]) for g, a in...]
    reduce_scatter x2 -> x0, waiting for transfers between devices: 78.2 us -> none  [the longest x1 78.2 us: row_shards(): sum_f = lax.psum_scatter(sent_f, axes, scatter_dimension=0, tiled=False)]
    psum x1 -> x0, blocking collectives: 42.3 us -> none  [row_shards(): small = lax.psum(small, axes) / tokens_all]
    all_gather x1, waiting for transfers between devices: 37.2 us -> 0.01 us  [row_shards(): got_f = lax.all_gather(tiles_f, axes, axis=0, tiled=False)]
    all_gather x1 -> x0, waiting for transfers between devices: 34.6 us -> none  [row_shards(): lax.all_gather(jnp.concatenate([tiles_a, extra]), axes, axis=0, tiled=False)]
    all_to_all x4 -> x0, waiting for transfers between devices: 24.1 us -> none  [the longest x2 19 us: to_row(): lax.all_to_all(values, 'tok', split_axis=0, concat_axis=1, tiled=True)]
    unnamed x2 -> x0, other arithmetic: 23.2 us -> none
    unnamed x54 -> x50, local copies, waits for them, and re-layouts: 21.4 us -> 2.16 us
  transfers between devices with their start and end apart: 12 -> 5, of which waited for: 8 -> 3; matrix products, arithmetic and copies ran while one was open for 15% -> 5% of each run, Pallas kernels for 14% -> 31%
where the time goes in v2:
time: 444 us; the launch traced here: 442 us
  Pallas kernels  369 us (83%)
  other arithmetic  23.3 us (5%)
  local copies, waits for them, and re-layouts  19.4 us (4%)
  between operations  15.5 us (3%)
  starting transfers between devices  11.9 us (3%)
    pallas_call x1, Pallas kernels, finish(): pl.pallas_call(partial(finish_kernel, depth, [(g, a.shape[0]) for g, a in...  99 us
    pallas_call x1, Pallas kernels, gather(): pl.pallas_call(partial(gather_kernel, depth, items, spread, ahead, second...  96.9 us
    pallas_call x1, Pallas kernels, middle(): pl.pallas_call(middle_kernel, grid=(steps,), in_specs=[rows, rows, rows,...  75.8 us
    pallas_call x1, Pallas kernels, row_attend_back(): pl.pallas_call(partial(attend_back_kernel, block_rows, reach), grid=(widt...  34.1 us
    pallas_call x1, Pallas kernels, row_attend(): pl.pallas_call(partial(attend_kernel, block_rows, reach), grid=(pairs,),...  29.6 us
    pallas_call x1, Pallas kernels, last(): pl.pallas_call(last_kernel, grid=(steps,), in_specs=[rows, rows, rows, pa...  25.4 us
    ppermute x2, starting transfers between devices, neighbour_edges(): lax.ppermute(heads, axes, [(i, (i - 1) % count) for i in range(count)])  11.3 us
  transfers between devices with their start and end apart: 5, of which 3 were waited for; matrix products, arithmetic and copies ran while one was open for 5% of the time, Pallas kernels for 31%

profile of v2, /device:TPU:0, one launch (start us, length us, event | category | flops | bytes accessed | tf_op | source)
XLA Modules:
  0.0 442.2 jit_solution(10055604888800008535)
XLA Ops:
  7.2 1.1 convert_element_type.74
  8.4 1.0 convert_element_type.73
  9.5 0.5 collective-permute-start
  10.1 6.0 %collective-permute-start.1 = (bf16[2,2048]{1,0:T(2,128)(2,1)S(1)}, bf16[2,2048]{1,0:T(2,128)(2,1)S(1)}, u32[]{:S(2)}, u32[]{:S(2)}) collective-permute-start(bf16[2,2048]{1,0:T(2,128)(2,1)S(1)} %pad_maximum_fusion.5), channel_id=1, source_target_pairs={{0,31},{1,0},{2,1},{3,2},{4,3},{5,4},{6,5},{7,6},{8,7},{9,8},{10,9... | collective-permute-start | bytes 24584 | tf_op jit(solution)/shard_map/ppermute | solution.py:1558
  16.1 1.2 collective-permute-done
  17.5 1.9 concatenate.19
  19.8 0.7 bitcast_select_fusion
  20.9 1.0 copy.56.sc_ref
  22.1 0.6 slice.141
  23.5 0.6 constant_dynamic-update-slice_fusion.5
  24.1 0.6 constant_dynamic-update-slice_fusion.4
  24.8 3.1 fusion.7
  27.9 1.2 concatenate.18
  29.5 0.6 pad_maximum_fusion.3
  30.1 0.7 bitcast_select_fusion.1.refs_0_
  30.8 96.9 %gather.1 = (f32[1024,768]{1,0:T(8,128)}, f32[8,192,128]{2,1,0:T(8,128)}, bf16[4,2,2,2,36,16,128]{6,5,4,3,2,1,0:T(8,128)(2,1)}, bf16[4,2,2,2,3,16,128]{6,5,4,3,2...) custom-call(bf16[24,1024,768]{2,1,0:T(8,128)(2,1)} %bitcast.77, bf16[1024,768]{1,0:T(8,128)(2,1)} %bitcast.78, ...), custom_call_target="tpu_custom_call" | custom-call | tf_op jit(solution)/shard_map/gather/pallas_call | solution.py:1195
  127.7 1.2 reshape.335
  128.9 0.6 slice.185.bup_ref
  130.0 0.7 stack.72.vec_ref
  130.7 8.7 %project.1 = (bf16[1024,768]{1,0:T(8,128)(2,1)}, bf16[1024,768]{1,0:T(8,128)(2,1)}, bf16[1024,768]{1,0:T(8,128)(2,1)}, bf16[1024,768]{1,0:T(8,128)(2,1)}) custom-call(bf16[1024,768]{1,0:T(8,128)(2,1)} %get-tuple-element.45.x_ref, bf16[32,2,18,16,128]{4,3,2,1,0:T(8,128)(2,1)} %bitcast.72, f32[8,2304]{1,0:T(8,128)} %stack.72.vec_ref, ...), custom_call_target="tpu_custom_call" | custom-call | tf_op jit(solution)/shard_map/project/pallas_call | solution.py:514
  139.4 29.6 %attend.1 = (bf16[1024,768]{1,0:T(8,128)(2,1)}, f32[6,2,1024]{2,1,0:T(2,128)}) custom-call(bf16[1024,768]{1,0:T(8,128)(2,1)} %get-tuple-element.49.q_ref, bf16[1024,768]{1,0:T(8,128)(2,1)} %get-tuple-element.50.k_ref, bf16[1024,768]{1,0:T(8,128)(2,1)} %get-tuple-element.51.v_ref, s32[1024,1]{1,0:T(8,128)} %copy.56.sc_ref, s32[1,1024]{1,0:T(1,128)} %bitcast.98), custom_call_target="tpu_custom_call" | custom-call | tf_op jit(solution)/shard_map/attend/pallas_call | solution.py:593
  169.0 0.6 stack.73.vec_ref
  169.6 0.7 pad_maximum_fusion.vec_ref
  170.3 75.8 %middle.1 = (f32[24,1024,768]{2,1,0:T(8,128)}, bf16[1024,768]{1,0:T(8,128)(2,1)}, bf16[1024,768]{1,0:T(8,128)(2,1)}, f32[1024,768]{1,0:T(8,128)}, bf16[48,24,16,...) custom-call(bf16[1024,768]{1,0:T(8,128)(2,1)} %get-tuple-element.45., ...), custom_call_target="tpu_custom_call" | custom-call | tf_op jit(solution)/shard_map/middle/pallas_call | solution.py:812
  246.1 34.1 %attend_back.1 = (bf16[1024,768]{1,0:T(8,128)(2,1)}, bf16[1024,768]{1,0:T(8,128)(2,1)}, bf16[1024,768]{1,0:T(8,128)(2,1)}) custom-call(bf16[1024,768]{1,0:T(8,128)(2,1)} %get-tuple-element.49.q_ref, bf16[1024,768]{1,0:T(8,128)(2,1)} %get-tuple-element.50.k_ref, bf16[1024,768]{1,0:T(8,128)(2,1)} %get-tuple-element.51.v_ref, ...), custom_call_target="tpu_custom_call" | custom-call | tf_op jit(solution)/shard_map/attend_back/pallas_call | solution.py:666
  280.2 25.4 %last.1 = (bf16[1024,768]{1,0:T(8,128)(2,1)}, bf16[48,18,16,128]{3,2,1,0:T(8,128)(2,1)}, f32[8,2304]{1,0:T(8,128)}, f32[8,768]{1,0:T(8,128)}) custom-call(bf16[1024,768]{1,0:T(8,128)(2,1)} %get-tuple-element.45.x_ref, bf16[1024,768]{1,0:T(8,128)(2,1)} %get-tuple-element.48.n1_ref, f32[1024,768]{1,0:T(8,128)} %get-tuple-element.54.ghid_ref, ...), custom_call_target="tpu_custom_call" | custom-call | tf_op jit(solution)/shard_map/last/pallas_call | solution.py:934
  305.5 0.8 slice_reduce_fusion.11
  306.4 0.9 slice_reduce_fusion
  307.3 0.6 slice_reduce_fusion.6
  307.9 0.9 slice.153
  308.8 0.7 concatenate.21
  309.5 0.6 pad_bitcast_fusion.small_ref
  310.2 99.0 %finish.1 = (f32[6,18,16,128]{3,2,1,0:T(8,128)}, f32[80,128]{1,0:T(8,128)}, bf16[4,256,768]{2,1,0:T(8,128)(2,1)}, bf16[4,256,768]{2,1,0:T(8,128)(2,1)}) custom-call(f32[80,128]{1,0:T(8,128)} %pad_bitcast_fusion.small_ref, bf16[12,2,36,16,128]{4,3,2,1,0:T(8,128)(2,1)} %bitcast.84, bf16[4,2,36,16,128]{4,3,2,1,0:T(8,128)(2,1)} %bitcast.94, ...), custom_call_target="tpu_custom_call" | custom-call | tf_op jit(solution)/shard_map/finish/pallas_call | solution.py:1447
  409.2 1.1 slice_multiply_fusion
  410.3 1.7 slice_multiply_fusion.1
  412.6 0.8 copy-done.1
  413.5 0.7 reshape.330
  414.3 1.4 copy.67
  415.6 0.7 reshape.331
  416.4 1.0 broadcast_select_fusion.1
  417.5 0.8 slice_multiply_fusion.2
  418.3 3.7 add_convert_fusion
  422.0 0.5 multiply_subtract_fusion.2
  422.6 1.9 convert_element_type.82
  424.5 5.3 %collective-permute-start.3 = (f32[2,2048]{1,0:T(2,128)S(1)}, f32[2,2048]{1,0:T(2,128)S(1)}, u32[]{:S(2)}, u32[]{:S(2)}) collective-permute-start(f32[2,2048]{1,0:T(2,128)S(1)} %pad_maximum_fusion.2), channel_id=1, source_target_pairs={{0,31},{1,0},{2,1},{3,2},{4,3},{5,4},{6,5},{7,6},{8,7},{9,8},{10,9... | collective-permute-start | bytes 49160 | tf_op jit(solution)/shard_map/ppermute | solution.py:1558
  430.0 1.3 collective-permute-done.3
  432.1 1.3 multiply_subtract_fusion.1
  433.4 2.0 multiply_subtract_fusion
  (115 shorter events, 3.8 us)
Async XLA Ops:
  7.2 163.1 %all-gather.2.cloned.1.call-start = ((), (), s32[]{:S(2)}) async-start(), calls=%async_computation | async-start | bytes 9732096 | tf_op jit(solution)/shard_map/all_gather | solution.py:1616
  9.5 7.8 %collective-permute-start = (bf16[2,2048]{1,0:T(2,128)(2,1)S(1)}, bf16[2,2048]{1,0:T(2,128)(2,1)S(1)}, u32[]{:S(2)}, u32[]{:S(2)}) collective-permute-start(bf16[2,2048]{1,0:T(2,128)(2,1)S(1)} %pad_maximum_fusion.4), channel_id=1, source_target_pairs={{0,1},{1,2},{2,3},{3,4},{4,5},{5,6},{6,7},{7,8},{8,9},{9,10},{10,1... | collective-permute-start | bytes 24584 | tf_op jit(solution)/shard_map/ppermute | solution.py:1557
  10.1 7.4 %collective-permute-start.1 = (bf16[2,2048]{1,0:T(2,128)(2,1)S(1)}, bf16[2,2048]{1,0:T(2,128)(2,1)S(1)}, u32[]{:S(2)}, u32[]{:S(2)}) collective-permute-start(bf16[2,2048]{1,0:T(2,128)(2,1)S(1)} %pad_maximum_fusion.5), channel_id=1, source_target_pairs={{0,31},{1,0},{2,1},{3,2},{4,3},{5,4},{6,5},{7,6},{8,7},{9,8},{10,9... | collective-permute-start | bytes 24584 | tf_op jit(solution)/shard_map/ppermute | solution.py:1558
  19.6 1.0 copy-start.20
  19.7 2.4 copy-start.16
  20.9 8.4 %copy-start.13 = (s32[1024]{0:T(1024)}, s32[1024]{0:T(1024)S(1)}, u32[]{:S(2)}) copy-start(s32[1024]{0:T(1024)S(1)} %fusion.15) | copy-start | bytes 12292
  22.1 7.2 %copy-start.15 = (f32[25]{0:T(128)}, f32[25]{0:T(128)S(1)}, u32[]{:S(2)}) copy-start(f32[25]{0:T(128)S(1)} %fusion.17.c_ref) | copy-start | bytes 304
  127.7 2.0 copy-start.6
  280.2 27.1 %copy-start.14 = (f32[8,768]{1,0:T(8,128)S(1)}, f32[8,768]{1,0:T(8,128)}, u32[]{:S(2)}) copy-start(f32[8,768]{1,0:T(8,128)} %get-tuple-element.62) | copy-start | bytes 73732
  412.6 0.8 copy-start.1
  413.5 4.8 %copy-start = (f32[1024,768]{1,0:T(8,128)S(1)}, f32[1024,768]{1,0:T(8,128)}, u32[]{:S(2)}) copy-start(f32[1024,768]{1,0:T(8,128)} %get-tuple-element.44) | copy-start | bytes 9437188
  417.4 12.4 %collective-permute-start.2 = (f32[2,2048]{1,0:T(2,128)S(1)}, f32[2,2048]{1,0:T(2,128)S(1)}, u32[]{:S(2)}, u32[]{:S(2)}) collective-permute-start(f32[2,2048]{1,0:T(2,128)S(1)} %pad_maximum_fusion.1), channel_id=1, source_target_pairs={{0,1},{1,2},{2,3},{3,4},{4,5},{5,6},{6,7},{7,8},{8,9},{9,10},{10,1... | collective-permute-start | bytes 49160 | tf_op jit(solution)/shard_map/ppermute | solution.py:1557
  418.3 3.7 copy-start.17
  418.3 3.7 copy-start.18
  418.3 3.7 copy-start.19
  418.3 4.2 copy-start.4
  422.6 7.3 %copy-start.9 = (f32[157696]{0:T(1024)S(1)}, f32[157696]{0:T(1024)}, u32[]{:S(2)}) copy-start(f32[157696]{0:T(1024)} %constant_dynamic-update-slice_fusion.5) | copy-start | bytes 1892356
  422.6 7.3 %copy-start.2 = (f32[147456]{0:T(1024)S(1)}, f32[147456]{0:T(1024)}, u32[]{:S(2)}) copy-start(f32[147456]{0:T(1024)} %copy-done.1) | copy-start | bytes 1769476
  422.6 8.8 %copy-start.12 = (f32[83968]{0:T(1024)S(1)}, f32[83968]{0:T(1024)}, u32[]{:S(2)}) copy-start(f32[83968]{0:T(1024)} %constant_dynamic-update-slice_fusion.4) | copy-start | bytes 1007620
  424.5 7.5 %copy-start.5 = (f32[73872]{0:T(1024)S(1)}, f32[73872]{0:T(1024)}, u32[]{:S(2)}) copy-start(f32[73872]{0:T(1024)} %param.18) | copy-start | bytes 886468
  424.5 7.5 %copy-start.10 = (f32[73872]{0:T(1024)S(1)}, f32[73872]{0:T(1024)}, u32[]{:S(2)}) copy-start(f32[73872]{0:T(1024)} %param.20) | copy-start | bytes 886468
  424.5 7.6 %copy-start.11 = (f32[73872]{0:T(1024)S(1)}, f32[73872]{0:T(1024)}, u32[]{:S(2)}) copy-start(f32[73872]{0:T(1024)} %param.19) | copy-start | bytes 886468
  424.5 6.8 %collective-permute-start.3 = (f32[2,2048]{1,0:T(2,128)S(1)}, f32[2,2048]{1,0:T(2,128)S(1)}, u32[]{:S(2)}, u32[]{:S(2)}) collective-permute-start(f32[2,2048]{1,0:T(2,128)S(1)} %pad_maximum_fusion.2), channel_id=1, source_target_pairs={{0,31},{1,0},{2,1},{3,2},{4,3},{5,4},{6,5},{7,6},{8,7},{9,8},{10,9... | collective-permute-start | bytes 49160 | tf_op jit(solution)/shard_map/ppermute | solution.py:1558
  430.0 3.4 copy-start.3
  430.0 3.4 copy-start.7
  430.0 3.4 copy-start.8
Sparse Core Ops, SparseCore 0:
  20.7 101.1 all-gather.1

commit v3 on v1

--- a/solution.py
+++ b/solution.py
@@ -480,45 +480,6 @@
     )
 
 
-def project_kernel(x_ref, w_ref, vec_ref, cos_ref, sin_ref, n1_ref, q_ref, k_ref, v_ref):
-    width = x_ref.shape[1]
-    centered, inverse = norm_parts(x_ref[...].astype(F32))
-    normed = (centered * inverse * vec_ref[0:1, :width] + vec_ref[1:2, :width]).astype(BF)
-    n1_ref[...] = normed
-    cosine = jnp.concatenate([cos_ref[...]] * 2, axis=1)
-    sine = jnp.concatenate([sin_ref[...]] * 2, axis=1)
-    per_part = width // 256
-    for at in range(3 * per_part):
-        part = nn_dot(normed, cols(w_ref, 2 * at, 2)) + vec_ref[2:3, 256 * at : 256 * at + 256]
-        spot = slice(256 * (at % per_part), 256 * (at % per_part) + 256)
-        if at < 2 * per_part:
-            part = part * cosine + swap_halves(part) * sine
-        if at < per_part:
-            q_ref[:, spot] = (part * HEAD_DIM ** (-0.5)).astype(BF)
-        elif at < 2 * per_part:
-            k_ref[:, spot] = part.astype(BF)
-        else:
-            v_ref[:, spot] = part.astype(BF)
-
-
-def project(x_row, w_qkv, vectors, cosine, sine):
-    length, width = x_row.shape
-    tile = 256
-    whole = pl.BlockSpec(w_qkv.shape, lambda i: (0,) * w_qkv.ndim)
-    rows = pl.BlockSpec((tile, width), lambda i: (i, 0))
-    trig = pl.BlockSpec((tile, 128), lambda i: (i, 0))
-    out = jax.ShapeDtypeStruct((length, width), BF)
-    return pl.pallas_call(
-        project_kernel,
-        grid=(length // tile,),
-        in_specs=[rows, whole, pl.BlockSpec(vectors.shape, lambda i: (0, 0)), trig, trig],
-        out_specs=[rows] * 4,
-        out_shape=[out] * 4,
-        compiler_params=pltpu.CompilerParams(vmem_limit_bytes=VMEM_LIMIT),
-        name="project",
-    )(x_row, w_qkv, vectors, cosine, sine)
-
-
 def key_range(block, block_rows, reach):
     return max(0, block * block_rows - reach), (block + 1) * block_rows
 
@@ -552,139 +513,12 @@
     return jnp.where(keep, values, jnp.zeros_like(values))
 
 
-def attend_kernel(block_rows, reach, q_ref, k_ref, v_ref, sc_ref, sr_ref, o_ref, lse_ref, bias_ref):
-    length = q_ref.shape[0]
-
-    @pl.when(pl.program_id(0) == 0)
-    def _():
-        fill_bias(bias_ref, sc_ref, sr_ref, block_rows, reach)
-
-    keys = k_ref[...]
-    key_heads = [head_mask(keys, 0), head_mask(keys, 1)]
-    value_turned = v_ref[...].T
-    at = 0
-    for block in range(length // block_rows):
-        low, high = key_range(block, block_rows, reach)
-        spot = slice(block * block_rows, (block + 1) * block_rows)
-        queries = q_ref[spot, :]
-        bias = bias_ref[at : at + high - low, :]
-        at = at + high - low
-        halves = []
-        for head in range(2):
-            scores = nt_dot(key_heads[head][low:high], queries) + bias
-            top = jnp.max(scores, axis=0, keepdims=True)
-            exponent = jnp.exp(scores - top)
-            total = jnp.sum(exponent, axis=0, keepdims=True)
-            probs = (exponent * (1.0 / total)).astype(BF)
-            lse_ref[0, head : head + 1, spot] = top + jnp.log(total)
-            turned = value_turned[HEAD_DIM * head : HEAD_DIM * head + HEAD_DIM, low:high]
-            halves.append(nn_dot(turned, probs))
-        o_ref[spot, :] = jnp.concatenate(halves, axis=0).T.astype(BF)
-
-
-def row_attend(queries, keys, values, seg_col, seg_row, reach):
-    length, width = queries.shape
-    block_rows = 256
-    pairs = width // 128
-    pair = pl.BlockSpec((length, 128), lambda p: (0, p))
-    return pl.pallas_call(
-        partial(attend_kernel, block_rows, reach),
-        grid=(pairs,),
-        in_specs=[
-            pair,
-            pair,
-            pair,
-            pl.BlockSpec(seg_col.shape, lambda p: (0, 0)),
-            pl.BlockSpec(seg_row.shape, lambda p: (0, 0)),
-        ],
-        out_specs=[pair, pl.BlockSpec((1, 2, length), lambda p: (p, 0, 0))],
-        out_shape=[
-            jax.ShapeDtypeStruct((length, width), BF),
-            jax.ShapeDtypeStruct((pairs, 2, length), F32),
-        ],
-        scratch_shapes=[pltpu.VMEM((bias_rows(length, block_rows, reach), block_rows), F32)],
-        compiler_params=pltpu.CompilerParams(vmem_limit_bytes=VMEM_LIMIT),
-        name="attend",
-    )(queries, keys, values, seg_col, seg_row)
-
-
-def attend_back_kernel(
-    block_rows, reach, q_ref, k_ref, v_ref, g_ref, lse_ref, sc_ref, sr_ref, cos_ref, sin_ref,
-    gq_ref, gk_ref, gv_ref, bias_ref, dq_acc, dk_acc, dv_acc,
-):
-    length = q_ref.shape[0]
-
-    @pl.when(pl.program_id(0) == 0)
-    def _():
-        fill_bias(bias_ref, sc_ref, sr_ref, block_rows, reach)
-
-    keys = k_ref[...]
-    key_heads = [head_mask(keys, 0), head_mask(keys, 1)]
-    key_turned = keys.T
-    vals = v_ref[...]
-    value_heads = [head_mask(vals, 0), head_mask(vals, 1)]
-    dk_acc[...] = jnp.zeros_like(dk_acc)
-    dv_acc[...] = jnp.zeros_like(dv_acc)
-    at = 0
-    for block in range(length // block_rows):
-        low, high = key_range(block, block_rows, reach)
-        spot = slice(block * block_rows, (block + 1) * block_rows)
-        queries = q_ref[spot, :]
-        grads = g_ref[spot, :]
-        bias = bias_ref[at : at + high - low, :]
-        at = at + high - low
-        halves = []
-        for head in range(2):
-            scores = nt_dot(key_heads[head][low:high], queries) + bias
-            probs = jnp.exp(scores - lse_ref[0, head : head + 1, spot])
-            dprobs = nt_dot(value_heads[head][low:high], grads)
-            inner = jnp.sum(probs * dprobs, axis=0, keepdims=True)
-            dscores = (probs * (dprobs - inner)).astype(BF)
-            turned = key_turned[HEAD_DIM * head : HEAD_DIM * head + HEAD_DIM, low:high]
-            halves.append(nn_dot(turned, dscores))
-            dk_acc[low:high, :] += nn_dot(dscores, head_mask(queries, head))
-            dv_acc[low:high, :] += nn_dot(probs.astype(BF), head_mask(grads, head))
-        dq_acc[spot, :] = jnp.concatenate(halves, axis=0).T * HEAD_DIM ** (-0.5)
-    cosine = cos_ref[...]
-    sine = sin_ref[...]
-    grad_query = dq_acc[...].astype(BF).astype(F32)
-    grad_key = dk_acc[...].astype(BF).astype(F32)
-    gq_ref[...] = (grad_query * cosine - swap_halves(grad_query) * sine).astype(BF)
-    gk_ref[...] = (grad_key * cosine - swap_halves(grad_key) * sine).astype(BF)
-    gv_ref[...] = dv_acc[...].astype(BF)
-
-
-def row_attend_back(queries, keys, values, grads, lse, seg_col, seg_row, cosine, sine, reach):
-    length, width = queries.shape
-    block_rows = 256
-    pair = pl.BlockSpec((length, 128), lambda p: (0, p))
-    trig = pl.BlockSpec((length, 128), lambda p: (0, 0))
-    out = jax.ShapeDtypeStruct((length, width), BF)
-    return pl.pallas_call(
-        partial(attend_back_kernel, block_rows, reach),
-        grid=(width // 128,),
-        in_specs=[
-            pair, pair, pair, pair,
-            pl.BlockSpec((1, 2, length), lambda p: (p, 0, 0)),
-            pl.BlockSpec(seg_col.shape, lambda p: (0, 0)),
-            pl.BlockSpec(seg_row.shape, lambda p: (0, 0)),
-            trig, trig,
-        ],
-        out_specs=[pair] * 3,
-        out_shape=[out] * 3,
-        scratch_shapes=[pltpu.VMEM((bias_rows(length, block_rows, reach), block_rows), F32)]
-        + [pltpu.VMEM((length, 128), F32)] * 3,
-        compiler_params=pltpu.CompilerParams(vmem_limit_bytes=VMEM_LIMIT),
-        name="attend_back",
-    )(queries, keys, values, grads, lse, seg_col, seg_row, cosine, sine)
-
-
 gelu_root = math.sqrt(2.0 / math.pi)
 
 
 def middle_kernel(
-    x_ref, att_ref, cot_ref, wout_ref, wup_ref, wdown_ref, vec_ref, bup_ref, c_ref,
-    bout_ref, gatt_ref, ghid_ref, gwup_ref, gwdown_ref, gwout_ref, gbup_ref, gvec_ref,
+    x_ref, att_ref, cot_ref, wout_ref, wup_ref, wdown_ref, vec_ref, bup_ref, own_cot_ref, c_ref,
+    ghist_ref, bout_ref, gatt_ref, ghid_ref, gwup_ref, gwdown_ref, gwout_ref, gbup_ref, gvec_ref,
     hidden_ref, n2_ref, n2t_ref, gb_ref, acc_out, acc_gn, act_ref, gup_ref,
 ):
     step = pl.program_id(0)
@@ -692,7 +526,8 @@
     length, width = x_ref.shape
     tile = 256
     tiles = length // tile
-    mix = c_ref[0]
+    mix = c_ref[c_ref.shape[0] - 1]
+    group = ghist_ref.shape[0]
 
     @pl.when(step == 0)
     def _():
@@ -734,6 +569,9 @@
         gup_ref[rows, :] = grad_up
         acc_gn[rows, :] += nt_dot(grad_up, w_up)
         gbup_ref[0:1, :] += jnp.sum(grad_up.astype(F32), axis=0, keepdims=True)
+        own_cot = own_cot_ref[rows, :].astype(F32)
+        for j in range(group):
+            ghist_ref[j, rows, :] = c_ref[step * group + j] * own_cot
 
     grad_up_all = gup_ref[...]
     for r in range(width // 256):
@@ -788,11 +626,13 @@
                 )
 
 
-def middle(x_row, attended, cot_row, w_out, w_up, w_down, vectors, b_up, mix):
+def middle(x_row, attended, cot_row, w_out, w_up, w_down, vectors, b_up, own_cot, coefficient):
     length, width = x_row.shape
-    (up_array, up_rows), (down_array, down_first) = w_up, w_down
+    (up_array, up_rows), (down_array, down_first), (out_array, out_rows) = w_up, w_down, w_out
+    out_first = out_array.shape[0] // out_rows - 1
     inner = b_up.shape[1]
     steps = inner // 256
+    terms = coefficient.shape[0] - 1
     once = pl.Buffered(1)
 
     def const(shape):
@@ -804,14 +644,19 @@
         middle_kernel,
         grid=(steps,),
         in_specs=[
-            rows, rows, rows, const(w_out.shape),
+            rows, rows, rows,
+            pl.BlockSpec(
+                (out_rows,) + out_array.shape[1:], lambda i: (out_first, 0, 0, 0, 0), pipeline_mode=once
+            ),
             pl.BlockSpec((up_rows, up_array.shape[1], 2, 16, 128), lambda i: (0, 0, i, 0, 0)),
             pl.BlockSpec((16, col_tiles, 16, 128), lambda i: (i + down_first, 0, 0, 0)),
             const(vectors.shape),
             pl.BlockSpec((1, 256), lambda i: (0, i)),
+            const(own_cot.shape),
             pl.BlockSpec(memory_space=pltpu.SMEM),
         ],
         out_specs=[
+            pl.BlockSpec((terms // steps,) + own_cot.shape, lambda i: (i, 0, 0)),
             rows, rows, rows,
             pl.BlockSpec((row_tiles, 2, 16, 128), lambda i: (0, i, 0, 0)),
             pl.BlockSpec((16, col_tiles, 16, 128), lambda i: (i, 0, 0, 0)),
@@ -820,6 +665,7 @@
             const((8, width)),
         ],
         out_shape=[
+            jax.ShapeDtypeStruct((terms,) + own_cot.shape, F32),
             jax.ShapeDtypeStruct((length, width), BF),
             jax.ShapeDtypeStruct((length, width), BF),
             jax.ShapeDtypeStruct((length, width), F32),
@@ -841,154 +687,938 @@
         ],
         compiler_params=pltpu.CompilerParams(vmem_limit_bytes=VMEM_LIMIT),
         name="middle",
-    )(x_row, attended, cot_row, w_out, up_array, down_array, vectors, b_up, mix)
-
-
-def last_kernel(
-    x_ref, n1_ref, ghid_ref, gq_ref, gk_ref, gv_ref, w_ref, vec_ref,
-    gx_ref, gw_ref, gb_ref, gvec_ref, n1t_ref, acc_ref,
+    )(x_row, attended, cot_row, out_array, up_array, down_array, vectors, b_up, own_cot, coefficient)
+
+
+def history_step(hist_ref, cot_ref, c_ref, first_term, part_ref, dots_ref):
+    group, tile, width = hist_ref.shape
+    mixes = [c_ref[first_term + j] for j in range(group)]
+
+    def chunk(r, dots):
+        rows = pl.ds(pl.multiple_of(r * 16, 16), 16)
+        total = part_ref[rows, :]
+        cot = cot_ref[rows, :].astype(F32)
+        new = []
+        for j in range(group):
+            past = hist_ref[j, rows, :].astype(F32)
+            total = total + mixes[j] * past
+            both = past * cot
+            both = both[:8] + both[8:]
+            added = dots[j]
+            for k in range(width // 128):
+                added = added + both[:, 128 * k : 128 * k + 128]
+            new.append(added)
+        part_ref[rows, :] = total
+        return tuple(new)
+
+    dots = lax.fori_loop(0, tile // 16, chunk, tuple(jnp.zeros((8, 128), F32) for _ in range(group)))
+    for j in range(group):
+        dots_ref[0, 8 * j : 8 * j + 8, :] = dots[j]
+
+
+gather_cuts, gather_share, enter_share = 2, 0.5, 3
+gather_steps = ((2, 3, 3, 4), (9, 9, 10), (15, 16, 18), (19,), (23, 24, 27), (28,), (31,))
+enter_first_steps, enter_second_steps, enter_rows_step = (4, 7, 10, 13), (16, 19, 23, 27), 14
+leave_steps, leave_share, leave_rows_steps = (4, 11, 18, 25, 31, 34, 36), 3, (0, 11, 18)
+MESH_ID = pl.DeviceIdType.MESH
+DMA = pltpu.SemaphoreType.DMA
+HBM = pl.BlockSpec(memory_space=pl.ANY)
+EVERY = slice(None)
+
+
+class Place:
+    def __init__(self, depth):
+        dp, tok = lax.axis_index("dp"), lax.axis_index("tok")
+        self.depth = depth
+        self.z, self.x, self.y, self.c = dp // 2, dp % 2, tok // 2, tok % 2
+        self.tok = tok
+        self.along_x = (self.z * 2 + 1 - self.x, tok)
+        self.along_y = (dp, (1 - self.y) * 2 + self.c)
+        self.along_c = (dp, self.y * 2 + 1 - self.c)
+        self.across = (dp, (1 - self.y) * 2 + 1 - self.c)
+        self.near_z = ((self.z + 1 - 2 * (self.z % 2)) * 2 + self.x, tok)
+        self.mid_z = ((depth - 1 - self.z) * 2 + self.x, tok)
+
+    def along_z(self, step):
+        return (lax.rem(self.z + step, self.depth) * 2 + self.x, self.tok)
+
+    def row_partners(self):
+        return [self.along_c, self.along_y, self.across]
+
+    def greet(self):
+        partners = [self.along_x] + self.row_partners()
+        partners = partners + [self.along_z(r) for r in range(1, self.depth)]
+        barrier = pltpu.get_barrier_semaphore()
+        for partner in partners:
+            pl.semaphore_signal(barrier, inc=1, device_id=partner, device_id_type=MESH_ID)
+        pl.semaphore_wait(barrier, len(partners))
+
+
+def remote(src, dst, send, recv, target):
+    return pltpu.make_async_remote_copy(
+        src_ref=src, dst_ref=dst, send_sem=send, recv_sem=recv,
+        device_id=target, device_id_type=MESH_ID,
+    )
+
+
+class LineGather:
+    def __init__(self, me, items, blocks, spots, sems):
+        self.me, self.items, self.blocks, self.spots = me, items, blocks, spots
+        self.send, self.recv, self.local = sems
+        self.inner = (me.z == 1) | (me.z == 2)
+
+    def scratch(items, arrays):
+        return [DMA((len(items), 3)), DMA((len(items), 3)), DMA((arrays,))]
+
+    def copy(self, i, hop):
+        which, low, count = self.items[i]
+        me, spot, half = self.me, pl.ds(low, count), self.me.z // 2
+        sems = (self.send.at[i, hop], self.recv.at[i, hop])
+        if hop == 0:
+            return remote(
+                self.blocks[which].at[spot], self.spots[which](me.z, spot), *sems, me.near_z
+            )
+        view = self.spots[which](pl.ds(2 * half if hop == 1 else 2 * (1 - half), 2), spot)
+        return remote(view, view, *sems, me.mid_z if hop == 1 else me.near_z)
+
+    def own(self, which):
+        whole = pl.ds(0, self.blocks[which].shape[0])
+        return pltpu.make_async_copy(
+            self.blocks[which], self.spots[which](self.me.z, whole), self.local.at[which]
+        )
+
+    def begin(self):
+        for which in range(len(self.blocks)):
+            self.own(which).start()
+
+    def first_hop(self, i):
+        self.copy(i, 0).start()
+
+    def own_wait(self):
+        for which in range(len(self.blocks)):
+            self.own(which).wait()
+
+    def inner_hop(self, i):
+        if i == 0:
+            self.own_wait()
+        self.copy(i, 0).wait_recv()
+        pl.when(self.inner)(lambda: self.copy(i, 1).start())
+
+    def outer_hop(self, i):
+        @pl.when(self.inner)
+        def _():
+            self.copy(i, 1).wait_recv()
+            self.copy(i, 2).start()
+
+    def arrived(self, i):
+        pl.when(jnp.logical_not(self.inner))(lambda: self.copy(i, 2).wait_recv())
+
+    def drain(self):
+        for i in range(len(self.items)):
+            self.copy(i, 0).wait_send()
+
+            @pl.when(self.inner)
+            def _(i=i):
+                self.copy(i, 1).wait_send()
+                self.copy(i, 2).wait_send()
+
+
+class PlaneGather:
+    def __init__(self, me, items, gathered, sems):
+        self.me, self.items, self.gathered = me, items, gathered
+        self.send, self.recv, self.core_send, self.core_recv = sems
+
+    def scratch(items):
+        n = len(items)
+        return [DMA((n, 4)), DMA((n, 4)), DMA((n,)), DMA((n,))]
+
+    def parts(self, i):
+        _, _, count, first = self.items[i]
+        return [part for part, size in ((0, first), (1, count - first)) if size]
+
+    def copy(self, i, stage, part):
+        which, low, count, first = self.items[i]
+        me = self.me
+        spot = pl.ds(low, first) if part == 0 else pl.ds(low + first, count - first)
+        if stage == 0:
+            index = (EVERY, me.x, me.y, me.c, spot)
+        elif part == 0:
+            index = (EVERY, EVERY, me.y, me.c, spot)
+        else:
+            index = (EVERY, me.x, EVERY, me.c, spot)
+        view = self.gathered[which].at[index]
+        at = 2 * stage + part
+        target = me.along_x if stage == part else me.along_y
+        return remote(view, view, self.send.at[i, at], self.recv.at[i, at], target)
+
+    def core_copy(self, i):
+        which, low, count, _ = self.items[i]
+        view = self.gathered[which].at[EVERY, EVERY, EVERY, self.me.c, pl.ds(low, count)]
+        return remote(view, view, self.core_send.at[i], self.core_recv.at[i], self.me.along_c)
+
+    def first(self, i):
+        for part in self.parts(i):
+            self.copy(i, 0, part).start()
+
+    def second(self, i):
+        for part in self.parts(i):
+            self.copy(i, 0, part).wait_recv()
+            self.copy(i, 1, part).start()
+
+    def third(self, i):
+        for part in self.parts(i):
+            self.copy(i, 1, part).wait_recv()
+        self.core_copy(i).start()
+
+    def drain(self):
+        for i in range(len(self.items)):
+            self.core_copy(i).wait_recv()
+            for part in self.parts(i):
+                self.copy(i, 0, part).wait_send()
+                self.copy(i, 1, part).wait_send()
+            self.core_copy(i).wait_send()
+
+
+class RowExchange:
+    def __init__(self, me, source, target, sems, back):
+        self.me, self.source, self.target, self.back = me, source, target, back
+        self.send, self.recv, self.local = sems
+        self.span = (target if back else source).shape[1]
+
+    def scratch():
+        return [DMA((3,)), DMA((3,)), DMA((1,))]
+
+    def views(self, tok):
+        mine = pl.ds(self.me.tok * self.span, self.span)
+        if self.back:
+            return self.source.at[pl.ds(tok * self.span, self.span)], self.target.at[self.me.tok]
+        return self.source.at[tok], self.target.at[mine]
+
+    def copy(self, p):
+        target = self.me.row_partners()[p]
+        return remote(*self.views(target[1]), self.send.at[p], self.recv.at[p], target)
+
+    def own(self):
+        return pltpu.make_async_copy(*self.views(self.me.tok), self.local.at[0])
+
+    def begin(self, parts=(0, 1, 2)):
+        for p in parts:
+            if p == 0:
+                self.own().start()
+            self.copy(p).start()
+
+    def drain(self):
+        self.own().wait()
+        for p in range(3):
+            self.copy(p).wait()
+
+
+class SmallSum:
+    def __init__(self, me, source, out, refs):
+        self.me, self.source, self.out = me, source, out
+        self.held, self.got, self.line, self.send, self.recv = refs
+        self.ways = (me.along_c, me.along_y, me.along_x)
+
+    def scratch(shape, depth):
+        return [
+            pltpu.VMEM((4,) + shape, F32), pltpu.VMEM((3,) + shape, F32),
+            pltpu.VMEM((depth,) + shape, F32), DMA((2 + depth,)), DMA((2 + depth,)),
+        ]
+
+    def copy(self, n):
+        return remote(
+            self.held.at[n], self.got.at[n], self.send.at[n], self.recv.at[n], self.ways[n]
+        )
+
+    def line_copy(self, r):
+        return remote(
+            self.held.at[3], self.line.at[self.me.z], self.send.at[2 + r], self.recv.at[2 + r],
+            self.me.along_z(r),
+        )
+
+    def begin(self):
+        self.held[0] = self.source[...]
+        self.copy(0).start()
+
+    def stage(self, n):
+        depth = self.me.depth
+        if n < 3:
+            self.copy(n).wait_recv()
+            self.held[n + 1] = self.held[n] + self.got[n]
+        if n < 2:
+            self.copy(n + 1).start()
+        elif n == 2:
+            self.line[self.me.z] = self.held[3]
+            for r in range(1, depth):
+                self.line_copy(r).start()
+        else:
+            for r in range(1, depth):
+                self.line_copy(r).wait_recv()
+            total = self.line[0]
+            for z in range(1, depth):
+                total = total + self.line[z]
+            self.out[...] = total
+
+    def drain(self):
+        for n in range(3):
+            self.copy(n).wait_send()
+        for r in range(1, self.me.depth):
+            self.line_copy(r).wait_send()
+
+
+class Reduce:
+    def __init__(self, me, items, mid, grads, out, refs):
+        self.me, self.items, self.grads, self.out = me, items, grads, out
+        (
+            self.own_buf, self.core_buf, s1a, s1b, r1a, r1b, s2a, s2b, r2a, r2b, self.s3, self.r3,
+            self.c_send, self.c_recv, self.m_send, self.m_recv, self.z_send, self.z_recv, self.local,
+        ) = refs
+        self.sends = ((s1a, s1b), (s2a, s2b))
+        self.recvs = ((r1a, r1b), (r2a, r2b))
+        self.tiles = (slice(0, mid), slice(mid, items[0][1]))
+        self.bits = ((me.y, me.x), (me.x, me.y))
+        self.ways = ((me.along_y, me.along_x), (me.along_x, me.along_y))
+
+    def scratch(items, mid, depth, arrays):
+        n, count = len(items), items[0][1]
+
+        def tiles(lead, size):
+            return pltpu.VMEM((n, lead, size, 16, 128), BF)
+
+        made = [tiles(4 * depth, count), tiles(4 * depth, count)]
+        for lead in (2 * depth, depth):
+            made += [tiles(lead, size) for size in (mid, count - mid)] * 2
+        made += [tiles(depth - 1, count), tiles(depth - 1, count)]
+        made += [DMA((n, arrays)), DMA((n, arrays)), DMA((n, 4)), DMA((n, 4))]
+        return made + [DMA((n, depth - 1)), DMA((n, depth - 1)), DMA((n, arrays))]
+
+    def pieces(self, i):
+        low, count = self.items[i]
+        at = 0
+        for n, array in enumerate(self.grads):
+            yield n, array, pl.ds(low, count), pl.ds(at, array.shape[0])
+            at = at + array.shape[0]
+
+    def core_copies(self, i):
+        for n, array, spot, place in self.pieces(i):
+            yield remote(
+                array.at[:, 1 - self.me.c, spot], self.core_buf.at[i, place],
+                self.c_send.at[i, n], self.c_recv.at[i, n], self.me.along_c,
+            )
+
+    def own_copies(self, i):
+        for n, array, spot, place in self.pieces(i):
+            yield pltpu.make_async_copy(
+                array.at[:, self.me.c, spot], self.own_buf.at[i, place], self.local.at[i, n]
+            )
+
+    def side_copy(self, i, part, stage):
+        at = 2 * stage + part
+        return remote(
+            self.sends[stage][part].at[i], self.recvs[stage][part].at[i],
+            self.m_send.at[i, at], self.m_recv.at[i, at], self.ways[part][stage],
+        )
+
+    def line_copy(self, i, r):
+        return remote(
+            self.s3.at[i, r - 1], self.r3.at[i, r - 1], self.z_send.at[i, r - 1],
+            self.z_recv.at[i, r - 1], self.me.along_z(r),
+        )
+
+    def slot(self, part, j, bit):
+        return 2 * j + bit if part == 0 else (j // 2) * 4 + 2 * bit + j % 2
+
+    def pair_sum(self, i, part, slot):
+        spot = self.tiles[part]
+        return self.own_buf[i, slot, spot].astype(F32) + self.core_buf[i, slot, spot].astype(F32)
+
+    def plane_sum(self, i, part, j):
+        slot = self.slot(part, j, self.bits[part][0])
+        return self.pair_sum(i, part, slot) + self.recvs[0][part][i, j].astype(F32)
+
+    def chip_sum(self, i, part, k):
+        total = self.plane_sum(i, part, 2 * k + self.bits[part][1])
+        return total + self.recvs[1][part][i, k].astype(F32)
+
+    def begin(self):
+        for i in range(len(self.items)):
+            for copy in self.core_copies(i):
+                copy.start()
+            for copy in self.own_copies(i):
+                copy.start()
+
+    def core_stage(self, i):
+        for copy in self.core_copies(i):
+            copy.wait_recv()
+        for copy in self.own_copies(i):
+            copy.wait()
+        for part in range(2):
+
+            def one(j, _, part=part):
+                slot = self.slot(part, j, 1 - self.bits[part][0])
+                self.sends[0][part][i, j] = self.pair_sum(i, part, slot).astype(BF)
+                return 0
+
+            lax.fori_loop(0, 2 * self.me.depth, one, 0)
+            self.side_copy(i, part, 0).start()
+
+    def first_stage(self, i):
+        for part in range(2):
+            self.side_copy(i, part, 0).wait_recv()
+
+            def one(k, _, part=part):
+                j = 2 * k + 1 - self.bits[part][1]
+                self.sends[1][part][i, k] = self.plane_sum(i, part, j).astype(BF)
+                return 0
+
+            lax.fori_loop(0, self.me.depth, one, 0)
+            self.side_copy(i, part, 1).start()
+
+    def second_stage(self, i):
+        for part in range(2):
+            self.side_copy(i, part, 1).wait_recv()
+        for r in range(1, self.me.depth):
+            other = lax.rem(self.me.z + r, self.me.depth)
+            for part in range(2):
+                self.s3[i, r - 1, self.tiles[part]] = self.chip_sum(i, part, other).astype(BF)
+            self.line_copy(i, r).start()
+
+    def line_stage(self, i):
+        for r in range(1, self.me.depth):
+            self.line_copy(i, r).wait_recv()
+        for part in range(2):
+            total = self.chip_sum(i, part, self.me.z)
+            for r in range(1, self.me.depth):
+                total = total + self.r3[i, r - 1, self.tiles[part]].astype(F32)
+            self.out[i, self.tiles[part]] = total
+
+    def drain(self):
+        for i in range(len(self.items)):
+            for copy in self.core_copies(i):
+                copy.wait_send()
+            for part in range(2):
+                self.side_copy(i, part, 0).wait_send()
+                self.side_copy(i, part, 1).wait_send()
+            for r in range(1, self.me.depth):
+                self.line_copy(i, r).wait_send()
+
+    def rounds(self):
+        n = len(self.items)
+        made = [[partial(self.core_stage, 0), partial(self.core_stage, 1)]]
+        for t in range(1, n + 3):
+            order = ((self.first_stage, t - 1), (self.core_stage, t + 1))
+            order = order + ((self.second_stage, t - 2), (self.line_stage, t - 3))
+            made.append([partial(stage, i) for stage, i in order if 0 <= i < n])
+        return made
+
+
+class Taker:
+    def __init__(self, refs):
+        self.refs, self.at = refs, 0
+
+    def __call__(self, count=None):
+        if count is None:
+            return self(1)[0]
+        self.at = self.at + count
+        return self.refs[self.at - count : self.at]
+
+
+def at_steps(step, work):
+    for when, one in work:
+        pl.when(step == when)(one)
+
+
+def kernel_params(collective_id=None):
+    if collective_id is None:
+        return pltpu.CompilerParams(vmem_limit_bytes=VMEM_LIMIT)
+    return pltpu.CompilerParams(
+        vmem_limit_bytes=VMEM_LIMIT, collective_id=collective_id, has_side_effects=True
+    )
+
+
+def gather_kernel(depth, line_items, plane_items, steps, when, hist_ref, cot_ref, c_ref, *refs):
+    take = Taker(refs)
+    blocks = take(3)
+    rows_in = take()
+    part_ref, dots_ref = take(2)
+    got_a, got_e, got_f, rows_out = take(4)
+    step = pl.program_id(0) * pl.num_programs(1) + pl.program_id(1)
+    me = Place(depth)
+    spots = [
+        lambda z, spot: got_a.at[z, me.x, me.y, me.c, spot],
+        lambda z, spot: got_e.at[z, me.x, me.y, me.c, spot],
+        lambda z, spot: got_f.at[z, me.x, me.y, me.c, spot],
+    ]
+    line = LineGather(me, line_items, blocks, spots, take(3))
+    plane = PlaneGather(me, plane_items, [got_a, got_e], take(4))
+    rows = RowExchange(me, rows_in, rows_out, take(3), False)
+
+    few = len(plane_items)
+    later = range(few, len(line_items))
+
+    def begin():
+        me.greet()
+        line.begin()
+        for i in range(few):
+            line.first_hop(i)
+        rows.begin()
+
+    def arrived(i):
+        line.arrived(i)
+        if i < few:
+            plane.first(i)
+
+    def end():
+        plane.drain()
+        rows.drain()
+        line.drain()
+
+    at_steps(step, [(0, begin)])
+
+    @pl.when(pl.program_id(1) == 0)
+    def _():
+        part_ref[...] = jnp.zeros_like(part_ref)
+
+    group = hist_ref.shape[0]
+    history_step(hist_ref, cot_ref, c_ref, pl.program_id(1) * group, part_ref, dots_ref)
+    groups = [
+        [partial(line.inner_hop, i) for i in range(few)] + [partial(line.first_hop, i) for i in later],
+        [partial(line.outer_hop, i) for i in range(few)],
+        [partial(arrived, i) for i in range(few)],
+        [partial(line.inner_hop, i) for i in later],
+        [partial(plane.second, i) for i in range(few)],
+        [partial(line.outer_hop, i) for i in later],
+        [partial(plane.third, i) for i in range(few)] + [partial(arrived, i) for i in later] + [end],
+    ]
+    work = []
+    for starts, group_work in zip(when, groups):
+        for at, one in enumerate(group_work):
+            work.append((min(starts[min(at, len(starts) - 1)], steps - 1), one))
+    at_steps(step, work)
+
+
+def gather(blocks, inputs, history, cotangent, coefficient, depth):
+    terms, tokens, width = history.shape
+    row_count, span, _ = inputs.shape
+    tile, group = 128, 6
+    count_a, count_e, count_f = (b.shape[0] for b in blocks)
+    part = count_a // gather_cuts
+    half = count_f // 2
+    line_items = [(1, 0, count_e)] + [(0, low, part) for low in range(0, count_a, part)]
+    line_items = line_items + [(2, low, half) for low in range(0, count_f, half)]
+    plane_items = [(1, 0, count_e, count_e)] + [(0, low, part, int(part * gather_share)) for low in range(0, count_a, part)]
+    everyone = (depth, 2, 2, 2)
+    return pl.pallas_call(
+        partial(
+            gather_kernel, depth, line_items, plane_items,
+            (tokens // tile) * (terms // group), gather_steps,
+        ),
+        grid=(tokens // tile, terms // group),
+        in_specs=[
+            pl.BlockSpec((group, tile, width), lambda t, j: (j, t, 0)),
+            pl.BlockSpec((tile, width), lambda t, j: (t, 0)),
+            pl.BlockSpec(memory_space=pltpu.SMEM),
+        ]
+        + [pl.BlockSpec(b.shape, lambda t, j: (0, 0, 0), pipeline_mode=pl.Buffered(1)) for b in blocks]
+        + [HBM],
+        out_specs=[
+            pl.BlockSpec((tile, width), lambda t, j: (t, 0)),
+            pl.BlockSpec((1, 8 * group, 128), lambda t, j: (t, j, 0)),
+        ]
+        + [HBM] * 4,
+        out_shape=[
+            jax.ShapeDtypeStruct((tokens, width), F32),
+            jax.ShapeDtypeStruct((tokens // tile, 8 * terms, 128), F32),
+            jax.ShapeDtypeStruct(everyone + blocks[0].shape, BF),
+            jax.ShapeDtypeStruct(everyone + blocks[1].shape, BF),
+            jax.ShapeDtypeStruct(everyone + blocks[2].shape, BF),
+            jax.ShapeDtypeStruct((span * row_count, width), BF),
+        ],
+        scratch_shapes=LineGather.scratch(line_items, 3)
+        + PlaneGather.scratch(plane_items)
+        + RowExchange.scratch(),
+        compiler_params=kernel_params(0),
+        name="gather",
+    )(history, cotangent.reshape(tokens, width), coefficient, *blocks, inputs)
+
+
+def finish_kernel(depth, items, mid, arrays, small_ref, *refs):
+    take = Taker(refs)
+    grads = take(arrays)
+    rows_in = take()
+    out_ref, small_out, rows_out = take(3)
+    me = Place(depth)
+    reduce = Reduce(me, items, mid, grads, out_ref, take(19))
+    rows = RowExchange(me, rows_in, rows_out, take(3), True)
+    small = SmallSum(me, small_ref, small_out, take(5))
+    me.greet()
+    small.begin()
+    reduce.begin()
+    rows.begin()
+    for t, stages in enumerate(reduce.rounds()):
+        for stage in stages:
+            stage()
+        if t < 4:
+            small.stage(t)
+    small.drain()
+    rows.drain()
+    reduce.drain()
+
+
+def finish(grads, small, row, row_count, depth):
+    length, width = row.shape
+    count = grads[0].shape[2]
+    size = count // 3
+    items = [(low, size) for low in range(0, count, size)]
+    mid = size // 3
+    vmem = pl.BlockSpec(memory_space=pltpu.VMEM)
+    return pl.pallas_call(
+        partial(finish_kernel, depth, items, mid, len(grads)),
+        in_specs=[vmem] + [HBM] * (len(grads) + 1),
+        out_specs=[vmem, vmem, HBM],
+        out_shape=[
+            jax.ShapeDtypeStruct((len(items), size, 16, 128), F32),
+            jax.ShapeDtypeStruct(small.shape, F32),
+            jax.ShapeDtypeStruct((row_count, length // row_count, width), row.dtype),
+        ],
+        scratch_shapes=Reduce.scratch(items, mid, depth, len(grads))
+        + RowExchange.scratch()
+        + SmallSum.scratch(small.shape, depth),
+        compiler_params=kernel_params(1),
+        name="finish",
+    )(small, *grads, row)
+
+
+def enter_kernel(depth, items, ready, rows_at, reach, x_ref, w_ref, vec_ref, cos_ref, sin_ref, sc_ref, sr_ref, *refs):
+    take = Taker(refs)
+    _, rows_in = take(2)
+    n1_ref, q_ref, k_ref, v_ref, o_ref, lse_ref, got_f, rows_out = take(8)
+    bias_ref, turned_ref = take(2)
+    me = Place(depth)
+    plane = PlaneGather(me, items, [got_f], take(4))
+    rows = RowExchange(me, rows_in, rows_out, take(3), False)
+    step = pl.program_id(0)
+    tile, width = x_ref.shape
+    length = q_ref.shape[1]
+    tiles = length // tile
+    pairs = width // 128
+    block_rows = 256
+    blocks = length // block_rows
+
+    def begin():
+        me.greet()
+        for i in range(len(items)):
+            plane.first(i)
+
+    def second(i):
+        if i == 0:
+            own.wait()
+        plane.second(i)
+    def finish_all():
+        plane.drain()
+        rows.drain()
+
+    at_steps(step, [(0, begin)])
+
+    @pl.when(step == 0)
+    def _():
+        fill_bias(bias_ref, sc_ref, sr_ref, block_rows, reach)
+
+    @pl.when(step < tiles)
+    def _():
+        centered, inverse = norm_parts(x_ref[...].astype(F32))
+        normed = (centered * inverse * vec_ref[0:1, :width] + vec_ref[1:2, :width]).astype(BF)
+        n1_ref[...] = normed
+        cosine = jnp.concatenate([cos_ref[...]] * 2, axis=1)
+        sine = jnp.concatenate([sin_ref[...]] * 2, axis=1)
+        spot = pl.ds(pl.multiple_of(step * tile, tile), tile)
+        per_part = width // 256
+        for at in range(3 * per_part):
+            part = nn_dot(normed, cols(w_ref, 2 * at, 2)) + vec_ref[2:3, 256 * at : 256 * at + 256]
+            if at < 2 * per_part:
+                part = part * cosine + swap_halves(part) * sine
+            if at < per_part:
+                part = part * HEAD_DIM ** (-0.5)
+            target = (q_ref, k_ref, v_ref)[at // per_part]
+            first = 2 * (at % per_part)
+            target[first, spot, :] = part[:, :128].astype(BF)
+            target[first + 1, spot, :] = part[:, 128:].astype(BF)
+
+    pair = jnp.maximum(step - tiles, 0) // blocks
+    current = jnp.maximum(step - tiles, 0) % blocks
+
+    def attend_block(block):
+        if block == 0:
+            turned_ref[...] = v_ref[pair].T
+        low, high = key_range(block, block_rows, reach)
+        at = sum(h - l for l, h in (key_range(b, block_rows, reach) for b in range(block)))
+        spot = slice(block * block_rows, (block + 1) * block_rows)
+        keys = k_ref[pair, low:high, :]
+        queries = q_ref[pair, spot, :]
+        bias = bias_ref[at : at + high - low, :]
+        halves = []
+        for head in range(2):
+            scores = nt_dot(head_mask(keys, head), queries) + bias
+            top = jnp.max(scores, axis=0, keepdims=True)
+            exponent = jnp.exp(scores - top)
+            total = jnp.sum(exponent, axis=0, keepdims=True)
+            probs = (exponent * (1.0 / total)).astype(BF)
+            lse_ref[pair, head : head + 1, spot] = top + jnp.log(total)
+            turned = turned_ref[HEAD_DIM * head : HEAD_DIM * head + HEAD_DIM, low:high]
+            halves.append(nn_dot(turned, probs))
+        lanes = pl.ds(pl.multiple_of(pair * 128, 128), 128)
+        o_ref[spot, lanes] = jnp.concatenate(halves, axis=0).T.astype(BF)
+
+    for block in range(blocks):
+        pl.when((step >= tiles) & (current == block))(partial(attend_block, block))
+
+    n = len(items)
+    work = [(ready[0][i], partial(plane.second, i)) for i in range(n)]
+    work += [(ready[1][i], partial(plane.third, i)) for i in range(n)]
+    work.sort(key=lambda item: item[0])
+    work += [(rows_at, rows.begin)]
+    at_steps(step, work + [(tiles + pairs * blocks - 1, finish_all)])
+
+
+def enter(x_row, w_qkv, vectors, cosine, sine, seg_col, seg_row, got_f, cotangent, reach, depth):
+    length, width = x_row.shape
+    array, lead = w_qkv
+    tile = 256
+    tiles, pairs = length // tile, width // 128
+    steps = tiles + pairs * (length // 256)
+    once = pl.Buffered(1)
+    count = got_f.shape[4]
+    size = count // 4
+    items = [(0, low, size, size // enter_share) for low in range(0, count, size)]
+    ready = (enter_first_steps, enter_second_steps)
+
+    def const(shape):
+        return pl.BlockSpec(shape, lambda i: (0,) * len(shape), pipeline_mode=once)
+
+    def rows(lanes):
+        return pl.BlockSpec((tile, lanes), lambda i: (jnp.minimum(i, tiles - 1), 0))
+
+    heads = jax.ShapeDtypeStruct((pairs, length, 128), BF)
+    return pl.pallas_call(
+        partial(enter_kernel, depth, items, ready, enter_rows_step, reach),
+        grid=(steps,),
+        in_specs=[
+            rows(width), const((lead,) + array.shape[1:]), const(vectors.shape), rows(128), rows(128),
+            const(seg_col.shape), const(seg_row.shape), HBM, HBM,
+        ],
+        out_specs=[
+            rows(width), const(heads.shape), const(heads.shape), const(heads.shape),
+            const((length, width)), const((pairs, 2, length)), HBM, HBM,
+        ],
+        out_shape=[
+            jax.ShapeDtypeStruct((length, width), BF), heads, heads, heads,
+            jax.ShapeDtypeStruct((length, width), BF),
+            jax.ShapeDtypeStruct((pairs, 2, length), F32),
+            jax.ShapeDtypeStruct(got_f.shape, BF),
+            jax.ShapeDtypeStruct((length, width), BF),
+        ],
+        scratch_shapes=[
+            pltpu.VMEM((bias_rows(length, 256, reach), 256), F32),
+            pltpu.VMEM((128, length), BF),
+        ]
+        + PlaneGather.scratch(items)
+        + RowExchange.scratch(),
+        input_output_aliases={7: 6},
+        compiler_params=kernel_params(2),
+        name="enter",
+    )(x_row, array, vectors, cosine, sine, seg_col, seg_row, got_f, cotangent)
+
+
+def leave_kernel(
+    depth, items, mid, starts, rows_at, reach, arrays,
+    q_ref, k_ref, v_ref, g_ref, lse_ref, sc_ref, sr_ref, cos_ref, sin_ref,
+    x_ref, n1_ref, ghid_ref, w_ref, vec_ref, *refs,
 ):
+    take = Taker(refs)
+    grads = take(arrays)
+    rows_in = take()
+    gx_ref, gw_ref, gb_ref, gvec_ref, out_ref, rows_out = take(6)
+    bias_ref, turned_ref, dk_acc, dv_acc, gp_ref, n1t_ref = take(6)
+    me = Place(depth)
+    reduce = Reduce(me, items, mid, grads, out_ref, take(19))
+    rows = RowExchange(me, rows_in, rows_out, take(3), True)
     step = pl.program_id(0)
-    steps = pl.num_programs(0)
     length, width = x_ref.shape
+    pairs = width // 128
+    block_rows = 256
+    blocks = length // block_rows
+    attend_steps = pairs * blocks
+    chunks = 3 * width // 256
     tile = 256
     tiles = length // tile
-    per_part = steps // 3
+
+    def begin():
+        me.greet()
+        reduce.begin()
+        rows.begin((0,))
+
+    def end():
+        rows.drain()
+        reduce.drain()
+
+    at_steps(step, [(0, begin)])
 
     @pl.when(step == 0)
+    def _():
+        fill_bias(bias_ref, sc_ref, sr_ref, block_rows, reach)
+
+    pair = jnp.minimum(step // blocks, pairs - 1)
+    current = step % blocks
+
+    def attend_block(block):
+        if block == 0:
+            turned_ref[...] = k_ref[0].T
+            dk_acc[...] = jnp.zeros_like(dk_acc)
+            dv_acc[...] = jnp.zeros_like(dv_acc)
+        low, high = key_range(block, block_rows, reach)
+        at = sum(h - l for l, h in (key_range(b, block_rows, reach) for b in range(block)))
+        spot = slice(block * block_rows, (block + 1) * block_rows)
+        keys, vals = k_ref[0, low:high, :], v_ref[0, low:high, :]
+        queries, grad = q_ref[0, spot, :], g_ref[spot, :]
+        bias = bias_ref[at : at + high - low, :]
+        halves = []
+        for head in range(2):
+            scores = nt_dot(head_mask(keys, head), queries) + bias
+            probs = jnp.exp(scores - lse_ref[0, head : head + 1, spot])
+            dprobs = nt_dot(head_mask(vals, head), grad)
+            inner = jnp.sum(probs * dprobs, axis=0, keepdims=True)
+            dscores = (probs * (dprobs - inner)).astype(BF)
+            turned = turned_ref[HEAD_DIM * head : HEAD_DIM * head + HEAD_DIM, low:high]
+            halves.append(nn_dot(turned, dscores))
+            dk_acc[low:high, :] += nn_dot(dscores, head_mask(queries, head))
+            dv_acc[low:high, :] += nn_dot(probs.astype(BF), head_mask(grad, head))
+        grad_query = jnp.concatenate(halves, axis=0).T * HEAD_DIM ** (-0.5)
+        turn(grad_query, pair, spot)
+        if block == blocks - 1:
+            turn(dk_acc[...], pairs + pair, slice(0, length))
+            gp_ref[2 * pairs + pair] = dv_acc[...].astype(BF)
+
+    def turn(values, place, spot):
+        values = values.astype(BF).astype(F32)
+        values = values * cos_ref[spot, :] - swap_halves(values) * sin_ref[spot, :]
+        gp_ref[place, spot, :] = values.astype(BF)
+
+    for block in range(blocks):
+        pl.when((step < attend_steps) & (current == block))(partial(attend_block, block))
+
+    @pl.when(step == attend_steps)
     def _():
         @pl.loop(0, tiles)
         def _(t):
-            rows = pl.ds(pl.multiple_of(t * tile, tile), tile)
-            n1t_ref[:, rows] = n1_ref[rows, :].T
-            acc_ref[rows, :] = jnp.zeros((tile, width), F32)
+            spot = pl.ds(pl.multiple_of(t * tile, tile), tile)
+            n1t_ref[:, spot] = n1_ref[spot, :].T
 
         gvec_ref[...] = jnp.zeros_like(gvec_ref)
 
-    def one(grad_ref):
-        grads = grad_ref[...]
+    @pl.when((step >= attend_steps) & (step < attend_steps + chunks))
+    def _():
+        at = jnp.clip(step - attend_steps, 0, chunks - 1)
+        grad = jnp.concatenate([gp_ref[2 * at], gp_ref[2 * at + 1]], axis=1)
         for r in range(width // 256):
-            put_tiles(gw_ref, 16 * r, 0, nn_dot(n1t_ref[256 * r : 256 * r + 256, :], grads).astype(BF))
-        gb_ref[0:1, :] = jnp.sum(grads.astype(F32), axis=0, keepdims=True)
-        weight = cols(w_ref, 0, 2)
-
-        @pl.loop(0, tiles)
-        def _(t):
-            rows = pl.ds(pl.multiple_of(t * tile, tile), tile)
-            acc_ref[rows, :] += nt_dot(grad_ref[rows, :], weight)
-
-    for part, grad_ref in enumerate((gq_ref, gk_ref, gv_ref)):
-        pl.when(step // per_part == part)(partial(one, grad_ref))
-
-    @pl.when(step == steps - 1)
+            put_tiles(gw_ref, 16 * r, 0, nn_dot(n1t_ref[256 * r : 256 * r + 256, :], grad).astype(BF))
+        gb_ref[0:1, :] = jnp.sum(grad.astype(F32), axis=0, keepdims=True)
+
+    @pl.when(step >= attend_steps + chunks)
     def _():
-        @pl.loop(0, tiles)
-        def _(t):
-            rows = pl.ds(pl.multiple_of(t * tile, tile), tile)
-            centered, inverse = norm_parts(x_ref[rows, :].astype(F32))
-            normed = centered * inverse
-            grad_norm = acc_ref[rows, :]
-            gvec_ref[0:1, :] += jnp.sum(normed * grad_norm, axis=0, keepdims=True)
-            gvec_ref[1:2, :] += jnp.sum(grad_norm, axis=0, keepdims=True)
-            scaled = grad_norm * vec_ref[0:1, :]
-            grad_value = inverse * (
-                scaled
-                - jnp.mean(scaled, axis=1, keepdims=True)
-                - normed * jnp.mean(scaled * normed, axis=1, keepdims=True)
-            )
-            gx_ref[rows, :] = (ghid_ref[rows, :] + grad_value).astype(gx_ref.dtype)
-
-
-def last(x_row, n1, grad_hidden, gq, gk, gv, w_qkv, vectors):
+        t = jnp.maximum(step - attend_steps - chunks, 0)
+        spot = pl.ds(pl.multiple_of(t * tile, tile), tile)
+        grad = jnp.concatenate([gp_ref[p, spot, :] for p in range(3 * pairs)], axis=1)
+        grad_norm = nt_dot(grad, cols(w_ref, 0, 3 * pairs))
+        centered, inverse = norm_parts(x_ref[spot, :].astype(F32))
+        normed = centered * inverse
+        gvec_ref[0:1, :] += jnp.sum(normed * grad_norm, axis=0, keepdims=True)
+        gvec_ref[1:2, :] += jnp.sum(grad_norm, axis=0, keepdims=True)
+        scaled = grad_norm * vec_ref[0:1, :]
+        grad_value = inverse * (
+            scaled
+            - jnp.mean(scaled, axis=1, keepdims=True)
+            - normed * jnp.mean(scaled * normed, axis=1, keepdims=True)
+        )
+        gx_ref[spot, :] = (ghid_ref[spot, :] + grad_value).astype(gx_ref.dtype)
+
+    work = [(when, partial(rows.begin, (p,))) for p, when in enumerate(rows_at) if p]
+    for start, stages in zip(starts, reduce.rounds()):
+        for at, stage in enumerate(stages):
+            work.append((min(start + at, attend_steps + chunks + tiles - 1), stage))
+    at_steps(step, work + [(attend_steps + chunks + tiles - 1, end)])
+
+
+def leave(
+    queries, keys, values, grad_attended, lse, seg_col, seg_row, cosine, sine,
+    x_row, n1, grad_hidden, w_qkv, vectors, grads, row, row_count, reach, depth,
+):
     length, width = x_row.shape
     array, lead = w_qkv
-    steps = 3 * width // 256
-    per_part = width // 256
+    pairs, blocks = width // 128, length // 256
+    attend_steps, chunks, tiles = pairs * blocks, 3 * width // 256, length // 256
+    steps = attend_steps + chunks + tiles
     once = pl.Buffered(1)
+    count = grads[0].shape[2]
+    size = count // 4
+    items = [(low, size) for low in range(0, count, size)]
+    mid = size // leave_share
+    starts = leave_steps
 
     def const(shape):
         return pl.BlockSpec(shape, lambda i: (0,) * len(shape), pipeline_mode=once)
 
-    def part_spec(part):
-        return pl.BlockSpec(
-            (length, 256), lambda i: (0, jnp.clip(i - part * per_part, 0, per_part - 1))
-        )
-
+    def pair_at(i):
+        return jnp.minimum(i // blocks, pairs - 1)
+
+    def chunk_at(i):
+        return jnp.clip(i - attend_steps, 0, chunks - 1)
+
+    heads = pl.BlockSpec((1, length, 128), lambda i: (pair_at(i), 0, 0))
     rows = const((length, width))
     row_tiles = width // 16
     return pl.pallas_call(
-        last_kernel,
+        partial(leave_kernel, depth, items, mid, starts, leave_rows_steps, reach, len(grads)),
         grid=(steps,),
         in_specs=[
-            rows, rows, rows, part_spec(0), part_spec(1), part_spec(2),
-            pl.BlockSpec((lead, array.shape[1], 2, 16, 128), lambda i: (0, 0, i, 0, 0)),
-            const(vectors.shape),
-        ],
+            heads, heads, heads,
+            pl.BlockSpec((length, 128), lambda i: (0, pair_at(i))),
+            pl.BlockSpec((1, 2, length), lambda i: (pair_at(i), 0, 0)),
+            const(seg_col.shape), const(seg_row.shape), const(cosine.shape), const(sine.shape),
+            rows, rows, rows, const((lead,) + array.shape[1:]), const(vectors.shape),
+        ]
+        + [HBM] * (len(grads) + 1),
         out_specs=[
             rows,
-            pl.BlockSpec((row_tiles, 2, 16, 128), lambda i: (0, i, 0, 0)),
-            pl.BlockSpec((8, 256), lambda i: (0, i)),
+            pl.BlockSpec((row_tiles, 2, 16, 128), lambda i: (0, chunk_at(i), 0, 0)),
+            pl.BlockSpec((8, 256), lambda i: (0, chunk_at(i))),
             const((8, width)),
+            const((len(items), size, 16, 128)),
+            HBM,
         ],
         out_shape=[
             jax.ShapeDtypeStruct((length, width), BF),
             jax.ShapeDtypeStruct((row_tiles, 3 * width // 128, 16, 128), BF),
             jax.ShapeDtypeStruct((8, 3 * width), F32),
             jax.ShapeDtypeStruct((8, width), F32),
+            jax.ShapeDtypeStruct((len(items), size, 16, 128), F32),
+            jax.ShapeDtypeStruct((row_count, length // row_count, width), row.dtype),
         ],
-        scratch_shapes=[pltpu.VMEM((width, length), BF), pltpu.VMEM((length, width), F32)],
-        compiler_params=pltpu.CompilerParams(vmem_limit_bytes=VMEM_LIMIT),
-        name="last",
-    )(x_row, n1, grad_hidden, gq, gk, gv, array, vectors)
-
-
-def history_kernel(hist_ref, cot_ref, c_ref, part_ref, grad_ref, dots_ref):
-    group = hist_ref.shape[0]
-    first = pl.program_id(1) * group
-    cot = cot_ref[...].astype(F32)
-    rows, width = cot.shape
-
-    @pl.when(pl.program_id(1) == 0)
-    def _():
-        part_ref[...] = jnp.zeros_like(part_ref)
-
-    total = part_ref[...]
-    for j in range(group):
-        mix = c_ref[first + j]
-        past = hist_ref[j].astype(F32)
-        total = total + mix * past
-        grad_ref[j] = mix * cot
-        dots = jnp.sum((past * cot).reshape(rows // 8, 8, width), axis=0)
-        dots_ref[0, 8 * j : 8 * j + 8, :] = sum(
-            dots[:, 128 * k : 128 * k + 128] for k in range(width // 128)
-        )
-    part_ref[...] = total
-
-
-def history_pass(history, cotangent, coefficient):
-    terms, tokens, width = history.shape
-    tile, group = 128, 6
-    return pl.pallas_call(
-        history_kernel,
-        grid=(tokens // tile, terms // group),
-        in_specs=[
-            pl.BlockSpec((group, tile, width), lambda t, j: (j, t, 0)),
-            pl.BlockSpec((tile, width), lambda t, j: (t, 0)),
-            pl.BlockSpec(memory_space=pltpu.SMEM),
-        ],
-        out_specs=[
-            pl.BlockSpec((tile, width), lambda t, j: (t, 0)),
-            pl.BlockSpec((group, tile, width), lambda t, j: (j, t, 0)),
-            pl.BlockSpec((1, 8 * group, 128), lambda t, j: (t, j, 0)),
-        ],
-        out_shape=[
-            jax.ShapeDtypeStruct((tokens, width), F32),
-            jax.ShapeDtypeStruct((terms, tokens, width), F32),
-            jax.ShapeDtypeStruct((tokens // tile, 8 * terms, 128), F32),
-        ],
-        compiler_params=pltpu.CompilerParams(vmem_limit_bytes=VMEM_LIMIT),
-        name="history",
-    )(history, cotangent, coefficient)
+        scratch_shapes=[
+            pltpu.VMEM((bias_rows(length, 256, reach), 256), F32),
+            pltpu.VMEM((128, length), BF),
+            pltpu.VMEM((length, 128), F32),
+            pltpu.VMEM((length, 128), F32),
+            pltpu.VMEM((3 * pairs, length, 128), BF),
+            pltpu.VMEM((width, length), BF),
+        ]
+        + Reduce.scratch(items, mid, depth, len(grads))
+        + RowExchange.scratch(),
+        compiler_params=kernel_params(3),
+        name="leave",
+    )(
+        queries, keys, values, grad_attended, lse, seg_col, seg_row, cosine, sine,
+        x_row, n1, grad_hidden, array, vectors, *grads, row,
+    )
 
 
 HALO = 2048
@@ -1132,15 +1762,23 @@
     plan_a, plan_f = plans(devices)
     reach = length // 2
 
+    depth = lax.axis_size("dp") // 2
+    tokens = row_count * span
+    term_count = mixing_offsets.shape[0]
+    coefficient = mixing_offsets + (jnp.arange(term_count) == term_count - 1).astype(F32)
+
     low_a, low_f = attention_params.astype(BF), feedforward_params.astype(BF)
     before, after = neighbour_edges([low_a, low_f], devices)
     tiles_a, extra_a = plan_a.blocks(low_a, before[0], after[0], s)
     tiles_f, extra_f = plan_f.blocks(low_f, before[1], after[1], s)
     extra = jnp.concatenate([extra_a, extra_f]).reshape(-1, 16, 128)
     count_a, count_f = tiles_a.shape[0], tiles_f.shape[0]
-    got_a = lax.all_gather(jnp.concatenate([tiles_a, extra]), axes, axis=0, tiled=False)
-    got_f = lax.all_gather(tiles_f, axes, axis=0, tiled=False)
-    extras = got_a[:, count_a:].reshape(devices, -1).astype(F32)
+    history_part, history_dots, got_a, got_e, got_f, x_row = gather(
+        [tiles_a, extra, tiles_f], inputs, history.reshape(term_count - 1, tokens, width), cotangent,
+        coefficient, depth,
+    )
+    got_a = got_a.reshape(devices, count_a, 16, 128)
+    extras = got_e.reshape(devices, -1).astype(F32)
     room_a = plan_a.vector_rows() * 128
 
     def pick(plan, which, at):
@@ -1152,56 +1790,37 @@
     b_up, b_down = pick(plan_f, 1, room_a), pick(plan_f, 2, room_a)
     (rq, cq), (ro, co) = plan_a.tile_shapes()
     (ru, cu), (rd, cd) = plan_f.tile_shapes()
-    w_qkv = got_a[: plan_a.split, :count_a].reshape(plan_a.split, rq, cq, 16, 128)
-    w_out = got_a[plan_a.split :, :count_a].reshape(devices - plan_a.split, ro, co, 16, 128)
-    w_up = (got_f.reshape(devices * ru * cu // (ru * cu), ru, cu, 16, 128), plan_f.split)
-    w_down = (got_f.reshape(devices * rd, cd, 16, 128), plan_f.split * rd // 16)
-
+    w_qkv = (got_a.reshape(devices, rq, cq, 16, 128), plan_a.split)
+    w_out = (got_a.reshape(devices, ro, co, 16, 128), devices - plan_a.split)
     def stack(vectors, wide):
         vectors = [jnp.pad(v, (0, wide - v.shape[0])) for v in vectors]
         vectors = vectors + [jnp.zeros((wide,), F32)] * (8 - len(vectors))
         return jnp.stack(vectors)
 
-    def to_row(values):
-        return lax.all_to_all(values, "tok", split_axis=0, concat_axis=1, tiled=True).reshape(
-            length, width
-        )
-
-    def from_row(values):
-        return lax.all_to_all(
-            values.reshape(1, length, width), "tok", split_axis=1, concat_axis=0, tiled=True
-        )
-
-    x_row, cot_row = to_row(inputs), to_row(cotangent)
     own_lengths = lax.dynamic_index_in_dim(document_lengths, lax.axis_index("tok"), 0, False)
     segment, cosine, sine = row_tables(own_lengths, length)
     seg_col, seg_row = segment[:, None], segment[None, :]
 
-    term_count = mixing_offsets.shape[0]
-    coefficient = mixing_offsets + (jnp.arange(term_count) == term_count - 1).astype(F32)
-    tokens = row_count * span
-    history_part, grad_history, history_dots = history_pass(
-        history.reshape(term_count - 1, tokens, width), cotangent.reshape(tokens, width), coefficient
-    )
-
-    normed_one, queries, keys, values = project(
-        x_row, w_qkv, stack([gain_one, shift_one, b_qkv], 3 * width), cosine, sine
-    )
-    attended, lse = row_attend(queries, keys, values, seg_col, seg_row, reach)
-    block_out, grad_attended, grad_hidden, gw_up, gw_down, gw_out, gb_up, gvec_two = middle(
+    normed_one, queries, keys, values, attended, lse, got_f, cot_row = enter(
+        x_row, w_qkv, stack([gain_one, shift_one, b_qkv], 3 * width), cosine, sine, seg_col, seg_row,
+        got_f, cotangent, reach, depth,
+    )
+    w_up = (got_f.reshape(devices, ru, cu, 16, 128), plan_f.split)
+    w_down = (got_f.reshape(devices * rd, cd, 16, 128), plan_f.split * rd // 16)
+    grad_history, block_out, grad_attended, grad_hidden, gw_up, gw_down, gw_out, gb_up, gvec_two = middle(
         x_row, attended, cot_row, w_out, w_up, w_down,
-        stack([gain_two, shift_two, b_out, b_down], width), b_up[None, :], coefficient[-1:],
-    )
-    gq, gk, gv = row_attend_back(
-        queries, keys, values, grad_attended, lse, seg_col, seg_row, cosine, sine, reach
-    )
-    grad_row, gw_qkv, gb_qkv, gvec_one = last(
-        x_row, normed_one, grad_hidden, gq, gk, gv, (w_qkv, plan_a.split), stack([gain_one], width)
-    )
-    mixed = history_part.reshape(row_count, span, width) + coefficient[-1] * from_row(
-        block_out
-    ).astype(F32)
-    grad_inputs = from_row(grad_row).astype(F32)
+        stack([gain_two, shift_two, b_out, b_down], width), b_up[None, :],
+        cotangent.reshape(tokens, width), coefficient,
+    )
+    def by_core(array, tiles):
+        return array.reshape(-1, 2, *tiles.shape)
+
+    grad_row, gw_qkv, gb_qkv, gvec_one, sum_f, block_back = leave(
+        queries, keys, values, grad_attended, lse, seg_col, seg_row, cosine, sine,
+        x_row, normed_one, grad_hidden, w_qkv, stack([gain_one], width),
+        [by_core(gw_up, tiles_f), by_core(gw_down, tiles_f)], block_out, row_count, reach, depth,
+    )
+    mixed = history_part.reshape(row_count, span, width) + coefficient[-1] * block_back.astype(F32)
 
     small = jnp.concatenate(
         [
@@ -1211,18 +1830,16 @@
             jnp.sum(gvec_two[4])[None],
         ]
     )
-    small = lax.psum(small, axes) / tokens_all
+    small_size = small.shape[0]
+    small = jnp.pad(small, (0, -small_size % 1024)).reshape(-1, 128)
     scale = 1.0 / tokens_all
-    sent_a = jnp.concatenate(
-        [gw_qkv.reshape(plan_a.split, -1, 16, 128), gw_out.reshape(devices - plan_a.split, -1, 16, 128)]
-    )
-    sent_f = jnp.concatenate(
-        [gw_up.reshape(plan_f.split, -1, 16, 128), gw_down.reshape(devices - plan_f.split, -1, 16, 128)]
-    )
-    sum_a = lax.psum_scatter(sent_a, axes, scatter_dimension=0, tiled=False)
-    sum_f = lax.psum_scatter(sent_f, axes, scatter_dimension=0, tiled=False)
-    flat_a = plan_a.from_tiles(sum_a.astype(F32) * scale, s)
-    flat_f = plan_f.from_tiles(sum_f.astype(F32) * scale, s)
+    sum_a, small, grad_back = finish(
+        [by_core(gw_qkv, tiles_a), by_core(gw_out, tiles_a)], small, grad_row, row_count, depth
+    )
+    small = small.reshape(-1)[:small_size] / tokens_all
+    grad_inputs = grad_back.astype(F32)
+    flat_a = plan_a.from_tiles(sum_a.reshape(tiles_a.shape) * scale, s)
+    flat_f = plan_f.from_tiles(sum_f.reshape(tiles_f.shape) * scale, s)
     before, after = neighbour_edges([flat_a, flat_f], devices)
     at = 0
     parts = []
@@ -1262,7 +1879,7 @@
     row_count, span, width = inputs.shape
     tok_size = lax.axis_size("tok")
     devices = lax.axis_size("dp") * tok_size
-    by_rows = row_count == tok_size and width == D and (span * tok_size) % 256 == 0
+    by_rows = row_count == tok_size == 4 and lax.axis_size("dp") == 8 and width == D
     if by_rows and all(plan.fits for plan in plans(devices)):
         return row_shards(inputs, *others)
     return general_shards(inputs, *others)

time: 595 us -> 376 us (0.63)
  waiting for transfers between devices: 177 us -> 0.01 us
  Pallas kernels: 215 us -> 322 us
  blocking collectives: 42.3 us -> 0 us
  other arithmetic: 60.5 us -> 20.6 us
  local copies, waits for them, and re-layouts: 51.3 us -> 17.9 us
  starting transfers between devices: 28 us -> 12.1 us
  between operations: 15.5 us -> 2.02 us
    pallas_call x5 -> x4, Pallas kernels: 144 us -> 246 us  [the longest x1 84.4 us: leave(): pl.pallas_call(partial(leave_kernel, depth, items, mid, starts, leave_row...]
    reduce_scatter x2 -> x0, waiting for transfers between devices: 78.2 us -> none  [the longest x1 78.2 us: row_shards(): sum_f = lax.psum_scatter(sent_f, axes, scatter_dimension=0, tiled=False)]
    all_gather x2 -> x0, waiting for transfers between devices: 71.8 us -> none  [the longest x1 37.2 us: row_shards(): got_f = lax.all_gather(tiles_f, axes, axis=0, tiled=False)]
    psum x1 -> x0, blocking collectives: 42.3 us -> none  [row_shards(): small = lax.psum(small, axes) / tokens_all]
    all_to_all x4 -> x0, waiting for transfers between devices: 24.1 us -> none  [the longest x2 19 us: to_row(): lax.all_to_all(values, 'tok', split_axis=0, concat_axis=1, tiled=True)]
    unnamed x2 -> x0, other arithmetic: 23.2 us -> none
    unnamed x54 -> x50, local copies, waits for them, and re-layouts: 21.4 us -> 2.69 us
    all_to_all x4 -> x0, starting transfers between devices: 15.9 us -> none  [the longest x2 8.73 us: from_row(): lax.all_to_all(values.reshape(1, length, width), 'tok', split_axis=1, con...]
  transfers between devices with their start and end apart: 12 -> 4, of which waited for: 8 -> 0; matrix products, arithmetic and copies ran while one was open for 15% -> 4% of each run, Pallas kernels for 14% -> 0%
where the time goes in v3:
time: 376 us; the launch traced here: 375 us
  Pallas kernels  322 us (86%)
  other arithmetic  20.6 us (5%)
  local copies, waits for them, and re-layouts  17.9 us (5%)
  starting transfers between devices  12.1 us (3%)
    pallas_call x1, Pallas kernels, leave(): pl.pallas_call(partial(leave_kernel, depth, items, mid, starts, leave_row...  84.4 us
    pallas_call x1, Pallas kernels, middle(): pl.pallas_call(middle_kernel, grid=(steps,), in_specs=[rows, rows, rows,...  75.8 us
    pallas_call x1, Pallas kernels, enter(): pl.pallas_call(partial(enter_kernel, depth, items, ready, enter_rows_step...  61.3 us
    pallas_call x1, Pallas kernels, gather(): pl.pallas_call(partial(gather_kernel, depth, line_items, plane_items, tok...  50.9 us
    pallas_call x1, Pallas kernels, finish(): pl.pallas_call(partial(finish_kernel, depth, items, mid, len(grads)), in_...  49.5 us
    ppermute x2, starting transfers between devices, neighbour_edges(): lax.ppermute(heads, axes, [(i, (i - 1) % count) for i in range(count)])  12 us
  transfers between devices with their start and end apart: 4, of which 0 were waited for; matrix products, arithmetic and copies ran while one was open for 4% of the time, Pallas kernels for 0%

profile of v3, /device:TPU:0, one launch (start us, length us, event | category | flops | bytes accessed | tf_op | source)
XLA Modules:
  0.0 374.6 jit_solution(15294185776976797859)
XLA Ops:
  0.6 1.1 convert_element_type.74
  1.8 1.0 convert_element_type.73
  2.9 6.4 %collective-permute-start.1 = (bf16[2,2048]{1,0:T(2,128)(2,1)S(1)}, bf16[2,2048]{1,0:T(2,128)(2,1)S(1)}, u32[]{:S(2)}, u32[]{:S(2)}) collective-permute-start(bf16[2,2048]{1,0:T(2,128)(2,1)S(1)} %pad_maximum_fusion.5), channel_id=1, source_target_pairs={{0,31},{1,0},{2,1},{3,2},{4,3},{5,4},{6,5},{7,6},{8,7},{9,8},{10,9... | collective-permute-start | bytes 24584 | tf_op jit(solution)/shard_map/ppermute | solution.py:1718
  9.5 0.7 constant_dynamic-slice_fusion
  10.2 0.2 reduce_window_sum.11
  10.3 0.7 subtract_bitcast_fusion
  11.0 0.6 constant_dynamic-update-slice_fusion.4
  11.6 0.7 fusion.17.c_ref
  12.5 3.1 fusion.7
  15.6 0.6 constant_dynamic-update-slice_fusion.5
  16.2 1.0 copy.41.sc_ref
  18.1 0.6 slice.135
  18.8 1.2 concatenate.18
  20.3 1.9 concatenate.19
  22.2 0.2 dynamic_slice.25
  22.6 0.8 bitcast_select_fusion.refs_2_
  23.5 0.6 pad_maximum_fusion.3
  24.1 0.7 bitcast_select_fusion.1.refs_0_
  24.8 50.9 %gather.1 = (f32[1024,768]{1,0:T(8,128)}, f32[8,192,128]{2,1,0:T(8,128)}, bf16[4,2,2,2,36,16,128]{6,5,4,3,2,1,0:T(8,128)(2,1)}, bf16[4,2,2,2,3,16,128]{6,5,4,3,2...) custom-call(bf16[24,1024,768]{2,1,0:T(8,128)(2,1)} %bitcast.77, ...), custom_call_target="tpu_custom_call" | custom-call | tf_op jit(solution)/shard_map/gather/pallas_call | solution.py:1211
  75.7 1.2 reshape.321
  76.9 0.6 slice.177.bup_ref
  77.6 0.7 pad_maximum_fusion.vec_ref
  78.3 0.6 stack.73.vec_ref
  78.9 0.7 stack.72.vec_ref
  79.6 61.3 %enter.1 = (bf16[1024,768]{1,0:T(8,128)(2,1)}, bf16[6,1024,128]{2,1,0:T(8,128)(2,1)}, bf16[6,1024,128]{2,1,0:T(8,128)(2,1)}, bf16[6,1024,128]{2,1,0:T(8,128)(2,1...) custom-call(bf16[1024,768]{1,0:T(8,128)(2,1)} %get-tuple-element.45., ...), custom_call_target="tpu_custom_call", output_to_operand_aliasing={{6}: (7, {})} | custom-call | tf_op jit(solution)/shard_map/enter/pallas_call | solution.py:1402
  141.0 75.8 %middle.1 = (f32[24,1024,768]{2,1,0:T(8,128)}, bf16[1024,768]{1,0:T(8,128)(2,1)}, bf16[1024,768]{1,0:T(8,128)(2,1)}, f32[1024,768]{1,0:T(8,128)}, bf16[48,24,16,...) custom-call(bf16[1024,768]{1,0:T(8,128)(2,1)} %get-tuple-element.45., ...), custom_call_target="tpu_custom_call" | custom-call | tf_op jit(solution)/shard_map/middle/pallas_call | solution.py:643
  216.8 84.4 %leave.1 = (bf16[1024,768]{1,0:T(8,128)(2,1)}, bf16[48,18,16,128]{3,2,1,0:T(8,128)(2,1)}, f32[8,2304]{1,0:T(8,128)}, f32[8,768]{1,0:T(8,128)}, f32[4,18,16,128]{3,2,1,0:T(8,128)}, /*index=5*/bf16[4,256,768]{2,1,0:T(8,128)(2,1)}) custom-call(bf16[6,1024,128]{2,1,0:T(8,128)(2,1)} %get-tuple-element.49.q_ref, bf16[6,1024,128]{2,1,0:T(8,128)(2,1)} %get-tuple-element.50.k_ref, ...), custom_call_target="tpu_custom_call" | custom-call | tf_op jit(solution)/shard_map/leave/pallas_call | solution.py:1579
  301.2 0.9 slice_reduce_fusion
  302.2 0.8 slice_reduce_fusion.11
  303.0 0.6 slice_reduce_fusion.6
  303.6 0.9 slice.147
  304.9 0.7 concatenate.21
  305.6 0.6 pad_bitcast_fusion.small_ref
  306.2 49.5 %finish.1 = (f32[3,12,16,128]{3,2,1,0:T(8,128)}, f32[80,128]{1,0:T(8,128)}, bf16[4,256,768]{2,1,0:T(8,128)(2,1)}) custom-call(f32[80,128]{1,0:T(8,128)} %pad_bitcast_fusion.small_ref, bf16[12,2,36,16,128]{4,3,2,1,0:T(8,128)(2,1)} %bitcast.84, bf16[4,2,36,16,128]{4,3,2,1,0:T(8,128)(2,1)} %bitcast.94, bf16[1024,768]{1,0:T(8,128)(2,1)} %get-tuple-element.70.refs_2_), custom_call_target="tpu_custom_call" | custom-call | tf_op jit(solution)/shard_map/finish/pallas_call | solution.py:1275
  355.7 1.0 broadcast_multiply_fusion.1
  357.1 0.8 copy-done.10
  357.9 0.2 copy.50
  358.2 0.2 copy.45
  358.6 5.6 %collective-permute-start.3 = (f32[2,2048]{1,0:T(2,128)S(1)}, f32[2,2048]{1,0:T(2,128)S(1)}, u32[]{:S(2)}, u32[]{:S(2)}) collective-permute-start(f32[2,2048]{1,0:T(2,128)S(1)} %pad_maximum_fusion.2), channel_id=1, source_target_pairs={{0,31},{1,0},{2,1},{3,2},{4,3},{5,4},{6,5},{7,6},{8,7},{9,8},{10,9... | collective-permute-start | bytes 49160 | tf_op jit(solution)/shard_map/ppermute | solution.py:1718
  364.2 0.8 slice_multiply_fusion
  365.1 2.4 add_convert_fusion
  367.4 0.5 multiply_subtract_fusion.2
  368.0 1.9 convert_element_type.82
  370.2 0.2 slice_dynamic-update-slice_fusion.2
  371.0 0.2 copy-done.8
  371.2 0.2 copy-done.9
  371.4 2.0 multiply_subtract_fusion
  373.3 1.3 multiply_subtract_fusion.1
  (110 shorter events, 3.1 us)
Async XLA Ops:
  2.9 15.8 %collective-permute-start.1 = (bf16[2,2048]{1,0:T(2,128)(2,1)S(1)}, bf16[2,2048]{1,0:T(2,128)(2,1)S(1)}, u32[]{:S(2)}, u32[]{:S(2)}) collective-permute-start(bf16[2,2048]{1,0:T(2,128)(2,1)S(1)} %pad_maximum_fusion.5), channel_id=1, source_target_pairs={{0,31},{1,0},{2,1},{3,2},{4,3},{5,4},{6,5},{7,6},{8,7},{9,8},{10,9... | collective-permute-start | bytes 24584 | tf_op jit(solution)/shard_map/ppermute | solution.py:1718
  9.4 9.4 %collective-permute-start = (bf16[2,2048]{1,0:T(2,128)(2,1)S(1)}, bf16[2,2048]{1,0:T(2,128)(2,1)S(1)}, u32[]{:S(2)}, u32[]{:S(2)}) collective-permute-start(bf16[2,2048]{1,0:T(2,128)(2,1)S(1)} %pad_maximum_fusion.4), channel_id=1, source_target_pairs={{0,1},{1,2},{2,3},{3,4},{4,5},{5,6},{6,7},{7,8},{8,9},{9,10},{10,1... | collective-permute-start | bytes 24584 | tf_op jit(solution)/shard_map/ppermute | solution.py:1717
  12.3 8.0 %copy-start.17 = (f32[25]{0:T(128)}, f32[25]{0:T(128)S(1)}, u32[]{:S(2)}) copy-start(f32[25]{0:T(128)S(1)} %fusion.17.c_ref) | copy-start | bytes 304
  12.4 7.9 %copy-start.15 = (s32[1024]{0:T(1024)}, s32[1024]{0:T(1024)S(1)}, u32[]{:S(2)}) copy-start(s32[1024]{0:T(1024)S(1)} %fusion.15) | copy-start | bytes 12292
  216.8 86.2 %copy-start.16 = (f32[8,768]{1,0:T(8,128)S(1)}, f32[8,768]{1,0:T(8,128)}, u32[]{:S(2)}) copy-start(f32[8,768]{1,0:T(8,128)} %get-tuple-element.65) | copy-start | bytes 73732
  216.8 87.7 %copy-start.7 = (f32[8,192,128]{2,1,0:T(8,128)S(1)}, f32[8,192,128]{2,1,0:T(8,128)}, u32[]{:S(2)}) copy-start(f32[8,192,128]{2,1,0:T(8,128)} %get-tuple-element.67) | copy-start | bytes 2359300
  356.8 1.1 copy-start.10
  357.1 1.1 copy-start.4
  357.9 7.1 %copy-start.2 = (bf16[4,256,768]{2,1,0:T(8,128)(2,1)S(1)}, bf16[4,256,768]{2,1,0:T(8,128)(2,1)}, u32[]{:S(2)}) copy-start(bf16[4,256,768]{2,1,0:T(8,128)(2,1)} %get-tuple-element.62) | copy-start | bytes 4718596
  358.2 6.8 %copy-start = (f32[1024,768]{1,0:T(8,128)S(1)}, f32[1024,768]{1,0:T(8,128)}, u32[]{:S(2)}) copy-start(f32[1024,768]{1,0:T(8,128)} %get-tuple-element.44) | copy-start | bytes 9437188
  358.5 11.4 %collective-permute-start.2 = (f32[2,2048]{1,0:T(2,128)S(1)}, f32[2,2048]{1,0:T(2,128)S(1)}, u32[]{:S(2)}, u32[]{:S(2)}) collective-permute-start(f32[2,2048]{1,0:T(2,128)S(1)} %pad_maximum_fusion.1), channel_id=1, source_target_pairs={{0,1},{1,2},{2,3},{3,4},{4,5},{5,6},{6,7},{7,8},{8,9},{9,10},{10,1... | collective-permute-start | bytes 49160 | tf_op jit(solution)/shard_map/ppermute | solution.py:1717
  358.6 11.4 %collective-permute-start.3 = (f32[2,2048]{1,0:T(2,128)S(1)}, f32[2,2048]{1,0:T(2,128)S(1)}, u32[]{:S(2)}, u32[]{:S(2)}) collective-permute-start(f32[2,2048]{1,0:T(2,128)S(1)} %pad_maximum_fusion.2), channel_id=1, source_target_pairs={{0,31},{1,0},{2,1},{3,2},{4,3},{5,4},{6,5},{7,6},{8,7},{9,8},{10,9... | collective-permute-start | bytes 49160 | tf_op jit(solution)/shard_map/ppermute | solution.py:1718
  365.0 2.4 copy-start.18
  365.0 2.4 copy-start.19
  365.1 2.4 copy-start.20
  365.1 2.9 copy-start.3
  368.0 2.0 copy-start.14
  368.0 2.0 copy-start.5
  368.0 2.1 copy-start.11
  369.9 1.1 copy-start.1
  369.9 1.2 copy-start.8
  369.9 1.4 copy-start.9
  371.4 2.0 copy-start.6
  371.4 2.0 copy-start.12
  371.4 2.0 copy-start.13

commit v4 on v3

--- a/solution.py
+++ b/solution.py
@@ -548,41 +548,41 @@
 
         gvec_ref[...] = jnp.zeros_like(gvec_ref)
 
-    w_up = cols(wup_ref, 0, 2)
+    w_up = cols(wup_ref, 0, 4)
     w_down = cols(wdown_ref, 0, width // 128)
-    gbup_ref[...] = jnp.zeros_like(gbup_ref)
+    part = step % 2
+    rows = pl.ds(pl.multiple_of(part * (length // 2), length // 2), length // 2)
+    up = nn_dot(n2_ref[rows, :], w_up) + bup_ref[0:1, :]
+    square = up * up
+    turn = jnp.tanh(gelu_root * up * (1.0 + 0.044715 * square))
+    half = 0.5 * (1.0 + turn)
+    active = (up * half).astype(BF)
+    act_ref[rows, :] = active
+    acc_out[rows, :] += nn_dot(active, w_down)
+    slope = half + (0.5 * gelu_root) * up * (1.0 - turn * turn) * (1.0 + (3.0 * 0.044715) * square)
+    grad_up = (nt_dot(gb_ref[rows, :], w_down) * slope).astype(BF)
+    gup_ref[rows, :] = grad_up
+    acc_gn[rows, :] += nt_dot(grad_up, w_up)
+    part_sum = jnp.sum(grad_up.astype(F32), axis=0, keepdims=True)
+    gbup_ref[0:1, :] = jnp.where(part == 0, 0.0, gbup_ref[0:1, :]) + part_sum
 
     @pl.loop(0, tiles)
     def _(t):
         rows = pl.ds(pl.multiple_of(t * tile, tile), tile)
-        up = nn_dot(n2_ref[rows, :], w_up) + bup_ref[0:1, :]
-        square = up * up
-        turn = jnp.tanh(gelu_root * up * (1.0 + 0.044715 * square))
-        half = 0.5 * (1.0 + turn)
-        active = (up * half).astype(BF)
-        act_ref[rows, :] = active
-        acc_out[rows, :] += nn_dot(active, w_down)
-        slope = half + (0.5 * gelu_root) * up * (1.0 - turn * turn) * (
-            1.0 + (3.0 * 0.044715) * square
-        )
-        grad_up = (nt_dot(gb_ref[rows, :], w_down) * slope).astype(BF)
-        gup_ref[rows, :] = grad_up
-        acc_gn[rows, :] += nt_dot(grad_up, w_up)
-        gbup_ref[0:1, :] += jnp.sum(grad_up.astype(F32), axis=0, keepdims=True)
         own_cot = own_cot_ref[rows, :].astype(F32)
         for j in range(group):
             ghist_ref[j, rows, :] = c_ref[step * group + j] * own_cot
 
-    grad_up_all = gup_ref[...]
-    for r in range(width // 256):
-        put_tiles(
-            gwup_ref, 16 * r, 0, nn_dot(n2t_ref[256 * r : 256 * r + 256, :], grad_up_all).astype(BF)
-        )
-    active_turned = act_ref[...].T
-    for r in range(width // 256):
-        put_tiles(
-            gwdown_ref, 0, 2 * r, nn_dot(active_turned, gb_ref[:, 256 * r : 256 * r + 256]).astype(BF)
-        )
+    @pl.when(part == 1)
+    def _():
+        grad_up_all = gup_ref[...]
+        for r in range(width // 256):
+            turned = n2t_ref[256 * r : 256 * r + 256, :]
+            put_tiles(gwup_ref, 16 * r, 0, nn_dot(turned, grad_up_all).astype(BF))
+        active_turned = act_ref[...].T
+        for r in range(width // 256):
+            columns = gb_ref[:, 256 * r : 256 * r + 256]
+            put_tiles(gwdown_ref, 0, 2 * r, nn_dot(active_turned, columns).astype(BF))
 
     @pl.when(step == steps - 1)
     def _():
@@ -631,7 +631,7 @@
     (up_array, up_rows), (down_array, down_first), (out_array, out_rows) = w_up, w_down, w_out
     out_first = out_array.shape[0] // out_rows - 1
     inner = b_up.shape[1]
-    steps = inner // 256
+    steps = 2 * inner // 512
     terms = coefficient.shape[0] - 1
     once = pl.Buffered(1)
 
@@ -648,20 +648,20 @@
             pl.BlockSpec(
                 (out_rows,) + out_array.shape[1:], lambda i: (out_first, 0, 0, 0, 0), pipeline_mode=once
             ),
-            pl.BlockSpec((up_rows, up_array.shape[1], 2, 16, 128), lambda i: (0, 0, i, 0, 0)),
-            pl.BlockSpec((16, col_tiles, 16, 128), lambda i: (i + down_first, 0, 0, 0)),
+            pl.BlockSpec((up_rows, up_array.shape[1], 4, 16, 128), lambda i: (0, 0, i // 2, 0, 0)),
+            pl.BlockSpec((32, col_tiles, 16, 128), lambda i: (i // 2 + down_first // 2, 0, 0, 0)),
             const(vectors.shape),
-            pl.BlockSpec((1, 256), lambda i: (0, i)),
+            pl.BlockSpec((1, 512), lambda i: (0, i // 2)),
             const(own_cot.shape),
             pl.BlockSpec(memory_space=pltpu.SMEM),
         ],
         out_specs=[
             pl.BlockSpec((terms // steps,) + own_cot.shape, lambda i: (i, 0, 0)),
             rows, rows, rows,
-            pl.BlockSpec((row_tiles, 2, 16, 128), lambda i: (0, i, 0, 0)),
-            pl.BlockSpec((16, col_tiles, 16, 128), lambda i: (i, 0, 0, 0)),
+            pl.BlockSpec((row_tiles, 4, 16, 128), lambda i: (0, i // 2, 0, 0)),
+            pl.BlockSpec((32, col_tiles, 16, 128), lambda i: (i // 2, 0, 0, 0)),
             const((row_tiles, col_tiles, 16, 128)),
-            pl.BlockSpec((8, 256), lambda i: (0, i)),
+            pl.BlockSpec((8, 512), lambda i: (0, i // 2)),
             const((8, width)),
         ],
         out_shape=[
@@ -682,8 +682,8 @@
             pltpu.VMEM((length, width), BF),
             pltpu.VMEM((length, width), F32),
             pltpu.VMEM((length, width), F32),
-            pltpu.VMEM((length, 256), BF),
-            pltpu.VMEM((length, 256), BF),
+            pltpu.VMEM((length, 512), BF),
+            pltpu.VMEM((length, 512), BF),
         ],
         compiler_params=pltpu.CompilerParams(vmem_limit_bytes=VMEM_LIMIT),
         name="middle",
@@ -719,7 +719,8 @@
 gather_cuts, gather_share, enter_share = 2, 0.5, 3
 gather_steps = ((2, 3, 3, 4), (9, 9, 10), (15, 16, 18), (19,), (23, 24, 27), (28,), (31,))
 enter_first_steps, enter_second_steps, enter_rows_step = (4, 7, 10, 13), (16, 19, 23, 27), 14
-leave_steps, leave_share, leave_rows_steps = (4, 11, 18, 25, 31, 34, 36), 3, (0, 11, 18)
+finish_cuts, finish_share = 3, 3
+leave_steps, leave_share, leave_rows_steps = (5, 10, 16, 22, 29, 33, 36), 3, (0, 18, 25)
 MESH_ID = pl.DeviceIdType.MESH
 DMA = pltpu.SemaphoreType.DMA
 HBM = pl.BlockSpec(memory_space=pl.ANY)
@@ -1268,9 +1269,9 @@
 def finish(grads, small, row, row_count, depth):
     length, width = row.shape
     count = grads[0].shape[2]
-    size = count // 3
+    size = count // finish_cuts
     items = [(low, size) for low in range(0, count, size)]
-    mid = size // 3
+    mid = size // finish_share
     vmem = pl.BlockSpec(memory_space=pltpu.VMEM)
     return pl.pallas_call(
         partial(finish_kernel, depth, items, mid, len(grads)),

time: 376 us -> 363 us (0.965)
  Pallas kernels: 322 us -> 309 us
    pallas_call x1, Pallas kernels: 75.8 us -> 64.7 us  [middle(): pl.pallas_call(middle_kernel, grid=(steps,), in_specs=[rows, rows, rows,...]
where the time goes in v4:
time: 363 us; the launch traced here: 362 us
  Pallas kernels  309 us (85%)
  other arithmetic  20.6 us (6%)
  local copies, waits for them, and re-layouts  17.9 us (5%)
  starting transfers between devices  12.2 us (3%)
    pallas_call x1, Pallas kernels, leave(): pl.pallas_call(partial(leave_kernel, depth, items, mid, starts, leave_row...  83.7 us
    pallas_call x1, Pallas kernels, middle(): pl.pallas_call(middle_kernel, grid=(steps,), in_specs=[rows, rows, rows,...  64.7 us
    pallas_call x1, Pallas kernels, enter(): pl.pallas_call(partial(enter_kernel, depth, items, ready, enter_rows_step...  61.3 us
    pallas_call x1, Pallas kernels, gather(): pl.pallas_call(partial(gather_kernel, depth, line_items, plane_items, tok...  50.9 us
    pallas_call x1, Pallas kernels, finish(): pl.pallas_call(partial(finish_kernel, depth, items, mid, len(grads)), in_...  48.3 us
    ppermute x2, starting transfers between devices, neighbour_edges(): lax.ppermute(heads, axes, [(i, (i - 1) % count) for i in range(count)])  12.1 us
  transfers between devices with their start and end apart: 4, of which 0 were waited for; matrix products, arithmetic and copies ran while one was open for 4% of the time, Pallas kernels for 0%

profile of v4, /device:TPU:0, one launch (start us, length us, event | category | flops | bytes accessed | tf_op | source)
XLA Modules:
  0.0 361.7 jit_solution(13183087899794085217)
XLA Ops:
  0.6 1.1 convert_element_type.74
  1.8 1.0 convert_element_type.73
  2.9 6.4 %collective-permute-start.1 = (bf16[2,2048]{1,0:T(2,128)(2,1)S(1)}, bf16[2,2048]{1,0:T(2,128)(2,1)S(1)}, u32[]{:S(2)}, u32[]{:S(2)}) collective-permute-start(bf16[2,2048]{1,0:T(2,128)(2,1)S(1)} %pad_maximum_fusion.5), channel_id=1, source_target_pairs={{0,31},{1,0},{2,1},{3,2},{4,3},{5,4},{6,5},{7,6},{8,7},{9,8},{10,9... | collective-permute-start | bytes 24584 | tf_op jit(solution)/shard_map/ppermute | solution.py:1719
  9.5 0.7 constant_dynamic-slice_fusion
  10.2 0.2 reduce_window_sum.11
  10.3 0.7 subtract_bitcast_fusion
  11.0 0.6 constant_dynamic-update-slice_fusion.4
  11.6 0.7 fusion.17.c_ref
  12.5 3.1 fusion.7
  15.6 0.6 constant_dynamic-update-slice_fusion.5
  16.2 1.0 copy.41.sc_ref
  18.1 0.6 slice.135
  18.8 1.2 concatenate.18
  20.3 1.9 concatenate.19
  22.2 0.2 dynamic_slice.25
  22.6 0.8 bitcast_select_fusion.refs_2_
  23.5 0.6 pad_maximum_fusion.3
  24.1 0.7 bitcast_select_fusion.1.refs_0_
  24.8 50.9 %gather.1 = (f32[1024,768]{1,0:T(8,128)}, f32[8,192,128]{2,1,0:T(8,128)}, bf16[4,2,2,2,36,16,128]{6,5,4,3,2,1,0:T(8,128)(2,1)}, bf16[4,2,2,2,3,16,128]{6,5,4,3,2...) custom-call(bf16[24,1024,768]{2,1,0:T(8,128)(2,1)} %bitcast.77, ...), custom_call_target="tpu_custom_call" | custom-call | tf_op jit(solution)/shard_map/gather/pallas_call | solution.py:1212
  75.7 1.2 reshape.321
  76.9 0.6 slice.177.bup_ref
  77.6 0.7 pad_maximum_fusion.vec_ref
  78.3 0.6 stack.73.vec_ref
  78.9 0.7 stack.72.vec_ref
  79.6 61.3 %enter.1 = (bf16[1024,768]{1,0:T(8,128)(2,1)}, bf16[6,1024,128]{2,1,0:T(8,128)(2,1)}, bf16[6,1024,128]{2,1,0:T(8,128)(2,1)}, bf16[6,1024,128]{2,1,0:T(8,128)(2,1...) custom-call(bf16[1024,768]{1,0:T(8,128)(2,1)} %get-tuple-element.45., ...), custom_call_target="tpu_custom_call", output_to_operand_aliasing={{6}: (7, {})} | custom-call | tf_op jit(solution)/shard_map/enter/pallas_call | solution.py:1403
  141.0 64.7 %middle.1 = (f32[24,1024,768]{2,1,0:T(8,128)}, bf16[1024,768]{1,0:T(8,128)(2,1)}, bf16[1024,768]{1,0:T(8,128)(2,1)}, f32[1024,768]{1,0:T(8,128)}, bf16[48,24,16,...) custom-call(bf16[1024,768]{1,0:T(8,128)(2,1)} %get-tuple-element.45., ...), custom_call_target="tpu_custom_call" | custom-call | tf_op jit(solution)/shard_map/middle/pallas_call | solution.py:643
  205.7 83.7 %leave.1 = (bf16[1024,768]{1,0:T(8,128)(2,1)}, bf16[48,18,16,128]{3,2,1,0:T(8,128)(2,1)}, f32[8,2304]{1,0:T(8,128)}, f32[8,768]{1,0:T(8,128)}, f32[4,18,16,128]{3,2,1,0:T(8,128)}, /*index=5*/bf16[4,256,768]{2,1,0:T(8,128)(2,1)}) custom-call(bf16[6,1024,128]{2,1,0:T(8,128)(2,1)} %get-tuple-element.49.q_ref, bf16[6,1024,128]{2,1,0:T(8,128)(2,1)} %get-tuple-element.50.k_ref, ...), custom_call_target="tpu_custom_call" | custom-call | tf_op jit(solution)/shard_map/leave/pallas_call | solution.py:1580
  289.5 0.9 slice_reduce_fusion
  290.4 0.8 slice_reduce_fusion.11
  291.3 0.6 slice_reduce_fusion.6
  291.9 0.9 slice.147
  293.1 0.7 concatenate.21
  293.9 0.6 pad_bitcast_fusion.small_ref
  294.5 48.3 %finish.1 = (f32[3,12,16,128]{3,2,1,0:T(8,128)}, f32[80,128]{1,0:T(8,128)}, bf16[4,256,768]{2,1,0:T(8,128)(2,1)}) custom-call(f32[80,128]{1,0:T(8,128)} %pad_bitcast_fusion.small_ref, bf16[12,2,36,16,128]{4,3,2,1,0:T(8,128)(2,1)} %bitcast.84, bf16[4,2,36,16,128]{4,3,2,1,0:T(8,128)(2,1)} %bitcast.94, bf16[1024,768]{1,0:T(8,128)(2,1)} %get-tuple-element.70.refs_2_), custom_call_target="tpu_custom_call" | custom-call | tf_op jit(solution)/shard_map/finish/pallas_call | solution.py:1276
  342.8 1.0 broadcast_multiply_fusion.1
  344.1 0.8 copy-done.10
  345.0 0.2 copy.50
  345.3 0.2 copy.45
  345.7 5.6 %collective-permute-start.3 = (f32[2,2048]{1,0:T(2,128)S(1)}, f32[2,2048]{1,0:T(2,128)S(1)}, u32[]{:S(2)}, u32[]{:S(2)}) collective-permute-start(f32[2,2048]{1,0:T(2,128)S(1)} %pad_maximum_fusion.2), channel_id=1, source_target_pairs={{0,31},{1,0},{2,1},{3,2},{4,3},{5,4},{6,5},{7,6},{8,7},{9,8},{10,9... | collective-permute-start | bytes 49160 | tf_op jit(solution)/shard_map/ppermute | solution.py:1719
  351.3 0.8 slice_multiply_fusion
  352.2 2.4 add_convert_fusion
  354.5 0.5 multiply_subtract_fusion.2
  355.1 1.9 convert_element_type.82
  357.3 0.2 slice_dynamic-update-slice_fusion.2
  358.1 0.2 copy-done.8
  358.3 0.2 copy-done.9
  358.5 2.0 multiply_subtract_fusion
  360.4 1.3 multiply_subtract_fusion.1
  (110 shorter events, 3.1 us)
Async XLA Ops:
  2.9 15.8 %collective-permute-start.1 = (bf16[2,2048]{1,0:T(2,128)(2,1)S(1)}, bf16[2,2048]{1,0:T(2,128)(2,1)S(1)}, u32[]{:S(2)}, u32[]{:S(2)}) collective-permute-start(bf16[2,2048]{1,0:T(2,128)(2,1)S(1)} %pad_maximum_fusion.5), channel_id=1, source_target_pairs={{0,31},{1,0},{2,1},{3,2},{4,3},{5,4},{6,5},{7,6},{8,7},{9,8},{10,9... | collective-permute-start | bytes 24584 | tf_op jit(solution)/shard_map/ppermute | solution.py:1719
  9.4 9.4 %collective-permute-start = (bf16[2,2048]{1,0:T(2,128)(2,1)S(1)}, bf16[2,2048]{1,0:T(2,128)(2,1)S(1)}, u32[]{:S(2)}, u32[]{:S(2)}) collective-permute-start(bf16[2,2048]{1,0:T(2,128)(2,1)S(1)} %pad_maximum_fusion.4), channel_id=1, source_target_pairs={{0,1},{1,2},{2,3},{3,4},{4,5},{5,6},{6,7},{7,8},{8,9},{9,10},{10,1... | collective-permute-start | bytes 24584 | tf_op jit(solution)/shard_map/ppermute | solution.py:1718
  12.3 8.0 %copy-start.17 = (f32[25]{0:T(128)}, f32[25]{0:T(128)S(1)}, u32[]{:S(2)}) copy-start(f32[25]{0:T(128)S(1)} %fusion.17.c_ref) | copy-start | bytes 304
  12.4 7.9 %copy-start.15 = (s32[1024]{0:T(1024)}, s32[1024]{0:T(1024)S(1)}, u32[]{:S(2)}) copy-start(s32[1024]{0:T(1024)S(1)} %fusion.15) | copy-start | bytes 12292
  205.7 85.5 %copy-start.16 = (f32[8,768]{1,0:T(8,128)S(1)}, f32[8,768]{1,0:T(8,128)}, u32[]{:S(2)}) copy-start(f32[8,768]{1,0:T(8,128)} %get-tuple-element.65) | copy-start | bytes 73732
  205.7 87.1 %copy-start.7 = (f32[8,192,128]{2,1,0:T(8,128)S(1)}, f32[8,192,128]{2,1,0:T(8,128)}, u32[]{:S(2)}) copy-start(f32[8,192,128]{2,1,0:T(8,128)} %get-tuple-element.67) | copy-start | bytes 2359300
  343.9 1.1 copy-start.10
  344.1 1.1 copy-start.4
  345.0 7.1 %copy-start.2 = (bf16[4,256,768]{2,1,0:T(8,128)(2,1)S(1)}, bf16[4,256,768]{2,1,0:T(8,128)(2,1)}, u32[]{:S(2)}) copy-start(bf16[4,256,768]{2,1,0:T(8,128)(2,1)} %get-tuple-element.62) | copy-start | bytes 4718596
  345.3 6.8 %copy-start = (f32[1024,768]{1,0:T(8,128)S(1)}, f32[1024,768]{1,0:T(8,128)}, u32[]{:S(2)}) copy-start(f32[1024,768]{1,0:T(8,128)} %get-tuple-element.44) | copy-start | bytes 9437188
  345.6 11.4 %collective-permute-start.2 = (f32[2,2048]{1,0:T(2,128)S(1)}, f32[2,2048]{1,0:T(2,128)S(1)}, u32[]{:S(2)}, u32[]{:S(2)}) collective-permute-start(f32[2,2048]{1,0:T(2,128)S(1)} %pad_maximum_fusion.1), channel_id=1, source_target_pairs={{0,1},{1,2},{2,3},{3,4},{4,5},{5,6},{6,7},{7,8},{8,9},{9,10},{10,1... | collective-permute-start | bytes 49160 | tf_op jit(solution)/shard_map/ppermute | solution.py:1718
  345.7 11.4 %collective-permute-start.3 = (f32[2,2048]{1,0:T(2,128)S(1)}, f32[2,2048]{1,0:T(2,128)S(1)}, u32[]{:S(2)}, u32[]{:S(2)}) collective-permute-start(f32[2,2048]{1,0:T(2,128)S(1)} %pad_maximum_fusion.2), channel_id=1, source_target_pairs={{0,31},{1,0},{2,1},{3,2},{4,3},{5,4},{6,5},{7,6},{8,7},{9,8},{10,9... | collective-permute-start | bytes 49160 | tf_op jit(solution)/shard_map/ppermute | solution.py:1719
  352.1 2.4 copy-start.18
  352.1 2.4 copy-start.19
  352.2 2.4 copy-start.20
  352.2 2.9 copy-start.3
  355.1 2.0 copy-start.14
  355.1 2.0 copy-start.5
  355.1 2.1 copy-start.11
  357.0 1.1 copy-start.1
  357.0 1.2 copy-start.8
  357.0 1.4 copy-start.9
  358.5 2.0 copy-start.6
  358.5 2.0 copy-start.12
  358.5 2.0 copy-start.13
